TPU v7x, 256 devices: a whole 4x4x8 slice. The times are simulated.
256 devices in a mesh: doc: 32 (over z, x), tensor: 8 (over y, core).
Axes of the slice: x: 4, y: 4, z: 8, core: 2. Of those that a mesh axis runs over, the one named last changes fastest.
Arguments:
- hidden: bfloat16 [8192, 14336], P('doc', 'tensor'), may hold values from -33 to 33
- grads: bfloat16 [8192, 4096], P('doc'), may hold values from -61 to 61
- lengths: int32 [64], P('doc'), may hold values from 64 to 128, as said below
Outputs:
- grad_weight: float32 [4096, 14336], P('doc', 'tensor')
- norm_ratio: float32 [64], P('doc')
Inputs may be any that keep to these rules, and one draw needn't show every extreme that they name: `lengths`: the valid tokens of a document are the first ones of its slot; some document fills its slot.
All inputs are finite; a program needn't handle non-finite values.
Results may differ from a plain program's by a relative error of at most 0.0003.
Values may be sent and summed in bfloat16 or wider, within the bound.
No kernel may reach another device: no remote copies, remote signals or barrier semaphores. Data moves between devices by JAX's collectives and lax.ppermute only.
A program may use at most 128 MiB of HBM per device.

v0:
```python
import math

import jax
import jax.numpy as jnp
from jax import lax
from jax.sharding import PartitionSpec as P

D = 4096
FF = 14336
SLOT = 128


clip_ratio = 2.0
epsilon = 1e-06


def weighted_sum(grad_blocks, hidden_blocks, weights):

    def step_fn(running, inputs):
        grad_one, hidden_one, weight_one = inputs
        product = lax.dot_general(
            grad_one, hidden_one, (((0,), (0,)), ((), ())), preferred_element_type=jnp.float32
        )
        return (running + weight_one * product, None)

    start_value = jnp.zeros((grad_blocks.shape[2], hidden_blocks.shape[2]), jnp.float32)
    running, unused = lax.scan(step_fn, start_value, (grad_blocks, hidden_blocks, weights))
    return running


def per_device(hidden, grads, lengths):
    doc_here = lengths.shape[0]
    ff_local = hidden.shape[1]
    model_dim = grads.shape[1]
    hidden_docs = hidden.reshape(doc_here, SLOT, ff_local)
    positions = jnp.arange(SLOT, dtype=jnp.int32)
    in_length = positions[None, :] < lengths[:, None]
    grad_docs = jnp.where(
        in_length[:, :, None], grads.reshape(doc_here, SLOT, model_dim), jnp.zeros((), grads.dtype)
    )
    hidden_gram = jnp.einsum(
        "nsf,ntf->nst", hidden_docs, hidden_docs, preferred_element_type=jnp.float32
    )
    grad_gram = jnp.einsum("nsd,ntd->nst", grad_docs, grad_docs, preferred_element_type=jnp.float32)
    partial_squares = jnp.sum(hidden_gram * grad_gram, axis=(1, 2))
    squares = lax.psum(partial_squares, "tensor")
    doc_total = doc_here * lax.axis_size("doc")
    clip_norm = clip_ratio * math.sqrt(SLOT * FF * D)
    norm_ratio = jnp.sqrt(squares + epsilon) / clip_norm
    weights = jnp.minimum(1.0, 1.0 / norm_ratio) / (clip_ratio * math.sqrt(SLOT * doc_total))
    grad_weight = lax.psum_scatter(
        weighted_sum(grad_docs, hidden_docs, weights), "doc", scatter_dimension=0, tiled=True
    )
    return (grad_weight, norm_ratio)


def solution(mesh):
    in_specs = (P("doc", "tensor"), P("doc", None), P("doc"))
    out_specs = (P("doc", "tensor"), P("doc"))
    return jax.shard_map(
        per_device, mesh=mesh, in_specs=in_specs, out_specs=out_specs, check_vma=False
    )
```

profile of v0, /device:TPU:1, one launch (start us, length us, event | category | flops | bytes accessed | tf_op | source)
XLA Modules:
  0.0 357.3 jit_solution(4677010809244543115)
XLA Ops:
  7.2 0.0 copy-start
  7.2 0.0 reduce-scatter.2.cloned.1.call-start
  7.2 0.8 iota_compare_fusion
  8.0 1.8 broadcast_select_fusion
  9.8 0.7 fusion.6
  10.5 0.0 copy-done
  10.5 0.5 fusion.5
  11.0 15.0 %psum.7 = f32[2]{0:T(128)S(1)} all-reduce(f32[2]{0:T(128)S(1)} %fusion.5), channel_id=1, replica_groups=mesh['doc'=32,'tensor'=8] {'tensor'}, use_global_device_ids=true, to_apply=%region_1.2 | all-reduce | flops 2 | bytes 16 | tf_op jit(solution)/shard_map/psum | solution.py:46
  26.0 0.5 minimum_multiply_fusion
  26.5 33.7 %while.11 = (s32[]{:T(128)}, f32[4096,1792]{1,0:T(8,128)}, f32[2]{0:T(128)S(1)}, bf16[2,128,4096]{2,1,0:T(8,128)(2,1)S(1)}, bf16[2,128,1792]{2,1,0:T(8,128)(2,1)S(1)}, /*index=5*/s32[]{:T(128)}, s32[]{:T(128)}) while((s32[]{:T(128)}, f32[4096,1792]{1,0:T(8,128)}, f32[2]{0:T(128)S(1)}, bf16[2,128,4096]{2,1,0:T(8,128)(2,1)S(1)}, ...), condition=%wide.region_3.4_spmd.clone, body=%wide.region_2.3_spmd.clone.sunk | while | flops 1901068288 | bytes 60229216 | solution.py:27
  26.5 0.6 dynamic_slice.28
  27.2 12.4 %select_add_fusion.2 = f32[4096,1792]{1,0:T(8,128)} fusion(f32[4096,1792]{1,0:T(8,128)} %get-tuple-element.99, f32[]{:T(128)} %bitcast.18, pred[]{:T(512)S(6)} %compare.3, bf16[2,128,4096]{2,1,0:T(8,128)(2,1)S(1)} %get-tuple-element.108, s32[]{:T(128)} %get-tuple-element.98, bf16[2,128,1792]{2,1,0:T(8,128)(2,1)S(1)} %get-tuple-element.109), kind=kOutput, calls=%fused_computation.clone.1 | convolution fusion | flops 1901068288 | bytes 60229120 | tf_op jit(solution)/shard_map/while/body/eval_jaxpr/dot_general | solution.py:21
  39.6 0.6 dynamic_slice.28
  40.2 20.0 %select_add_fusion.2 = f32[4096,1792]{1,0:T(8,128)} fusion(f32[4096,1792]{1,0:T(8,128)} %get-tuple-element.99, f32[]{:T(128)} %bitcast.18, pred[]{:T(512)S(6)} %compare.3, bf16[2,128,4096]{2,1,0:T(8,128)(2,1)S(1)} %get-tuple-element.108, s32[]{:T(128)} %get-tuple-element.98, bf16[2,128,1792]{2,1,0:T(8,128)(2,1)S(1)} %get-tuple-element.109), kind=kOutput, calls=%fused_computation.clone.1 | convolution fusion | flops 1901068288 | bytes 60229120 | tf_op jit(solution)/shard_map/while/body/eval_jaxpr/dot_general | solution.py:21
  60.2 0.0 reduce-scatter.2.cloned.1.call-update
  60.2 290.2 %reduce-scatter.2.cloned.1.call-done = f32[128,1792]{1,0:T(8,128)} async-done(((f32[4096,1792]{1,0:T(8,128)}), f32[128,1792]{1,0:T(8,128)}) %reduce-scatter.2.cloned.1.call-update) | async-done | bytes 917520 | tf_op jit(solution)/shard_map/reduce_scatter | solution.py:51
  (1 shorter events, 0.0 us)
Async XLA Ops:
  7.2 3.4 copy-start
  7.2 343.3 %reduce-scatter.2.cloned.1.call-start = ((), (), s32[]{:S(2)}) async-start(), calls=%async_computation.1 | async-start | bytes 30277632 | tf_op jit(solution)/shard_map/reduce_scatter | solution.py:51
Sparse Core Ops, SparseCore 0:
  60.3 290.0 reduce-scatter.1
where the time goes:
time: 357 us
  waiting for transfers between devices  290 us (81%)
  matrix products  33.6 us (9%)
  blocking collectives  15 us (4%)
  between operations  14.1 us (4%)
    reduce_scatter x1, waiting for transfers between devices, per_device(): lax.psum_scatter(weighted_sum(grad_docs, hidden_docs, weights), 'doc', sc...  290 us
    dot_general x2, matrix products, step_fn(): lax.dot_general(grad_one, hidden_one, (((0,), (0,)), ((), ())), preferred...  32.4 us
    psum x1, blocking collectives, per_device(): squares = lax.psum(partial_squares, 'tensor')  15 us
  transfers between devices with their start and end apart: 1, of which 1 were waited for; matrix products, arithmetic and copies ran while one was open for 0% of the time, Pallas kernels for 0%

commit v1 on v0

v1 whole, which is shorter than its diff:
```python
import math

import jax
import jax.numpy as jnp
from jax import lax
from jax.experimental import pallas as pl
from jax.experimental.pallas import tpu as pltpu
from jax.sharding import Mesh, PartitionSpec as P

SLOT = 128
CLIP_RATIO = 2.0
EPSILON = 1e-06
NX, NY, NZ = 4, 4, 8
LANES = 128
QUARTER = NZ * LANES // NY
NOTE = 16
PIECE = QUARTER + NOTE
BUNDLE = (NX - 1) * PIECE + NOTE
HALVES = ((4, 3), (3, 4))
LIMIT = 32767.0
MANT = 8192.0
EXTRA = 8
GRANT = 24 * 2**20

SMEM = pl.BlockSpec(memory_space=pltpu.SMEM)
VMEM = pl.BlockSpec(memory_space=pltpu.VMEM)
HBM = pl.BlockSpec(memory_space=pltpu.HBM)
NT = (((1,), (1,)), ((), ()))


def cost(flops, nbytes):
    return pl.CostEstimate(flops=flops, bytes_accessed=nbytes, transcendentals=0)


def near(value):
    return pltpu.with_memory_space_constraint(value, pltpu.VMEM)


def split(value):
    hi = value.astype(jnp.bfloat16)
    rest = value - hi.astype(jnp.float32)
    mid = rest.astype(jnp.bfloat16)
    return hi, mid, (rest - mid.astype(jnp.float32)).astype(jnp.bfloat16)


def prepare_kernel(len_ref, pos_ref, hidden_hbm, grads_hbm, own_ref, s1, s2, s3, note_ref, masked_ref, grads_ref, hidden_ref, sem):
    loads = [
        pltpu.make_async_copy(src.at[pl.ds(d * SLOT, SLOT), :], dst.at[pl.ds(d * SLOT, SLOT), :], sem.at[i, d])
        for d in range(2)
        for i, (src, dst) in enumerate(((grads_hbm, grads_ref), (hidden_hbm, hidden_ref)))
    ]
    for load in loads:
        load.start()
    z, x, y, core = (pos_ref[i] for i in range(4))
    row = lax.broadcasted_iota(jnp.int32, note_ref.shape, 0)
    note = jnp.zeros(note_ref.shape, jnp.float32)
    for d in range(2):
        rows = pl.ds(d * SLOT, SLOT)
        loads[2 * d].wait()
        g = grads_ref[rows, :]
        token = lax.broadcasted_iota(jnp.int32, g.shape, 0)
        m = jnp.where(token < len_ref[d], g.astype(jnp.float32), 0.0).astype(g.dtype)
        masked_ref[rows, :] = m
        loads[2 * d + 1].wait()
        h = hidden_ref[rows, :]
        gram_g = lax.dot_general(m, m, NT, preferred_element_type=jnp.float32)
        gram_h = lax.dot_general(h, h, NT, preferred_element_type=jnp.float32)
        square = jnp.sum(gram_g * gram_h)
        whole = jnp.zeros(note_ref.shape, jnp.float32) + square
        for i, term in enumerate(split(whole)):
            note = jnp.where(row == 3 * d + i, term.astype(jnp.float32), note)
    note = note.astype(note_ref.dtype)
    note_ref[...] = note

    r = lax.broadcasted_iota(jnp.int32, (LANES, LANES), 0)
    c = lax.broadcasted_iota(jnp.int32, (LANES, LANES), 1)
    eye = jnp.where(r == c, 1.0, 0.0).astype(masked_ref.dtype)

    def turned(rows, j, dest):
        block = lax.rem(z + 2 * NZ - 1 - j, NZ) * NX + dest
        piece = masked_ref[rows, pl.ds(pl.multiple_of(block * LANES, LANES), LANES)]
        return lax.dot_general(eye, piece, NT, preferred_element_type=jnp.float32).astype(piece.dtype)

    mine = pl.ds(pl.multiple_of(core * SLOT, SLOT), SLOT)
    for k, send in enumerate((s1, s2, s3), 1):
        dest = lax.rem(x + k, NX)
        for i in range(QUARTER // LANES):
            send[pl.ds(i * LANES, LANES), :] = turned(mine, y * (QUARTER // LANES) + i, dest)
        send[pl.ds(QUARTER, NOTE), :] = note
    for j in range(NZ):
        own_ref[pl.ds(j * LANES, LANES), :] = turned(slice(None), j, x)


def prepare(lengths, pos, hidden, grads):
    piece = pltpu.VMEM((PIECE, LANES), grads.dtype)
    return pl.pallas_call(
        prepare_kernel,
        out_shape=(
            pltpu.VMEM((NZ * LANES, grads.shape[0]), grads.dtype),
            piece,
            piece,
            piece,
            pltpu.VMEM((NOTE, LANES), grads.dtype),
        ),
        in_specs=[SMEM, SMEM, HBM, HBM],
        out_specs=(VMEM,) * 5,
        scratch_shapes=[
            pltpu.VMEM(grads.shape, grads.dtype),
            pltpu.VMEM(grads.shape, grads.dtype),
            pltpu.VMEM(hidden.shape, hidden.dtype),
            pltpu.SemaphoreType.DMA((2, 2)),
        ],
        compiler_params=pltpu.CompilerParams(vmem_limit_bytes=GRANT),
        cost_estimate=cost(4 * 10**8, 5 * 10**6),
    )(
        lengths,
        pos,
        pltpu.with_memory_space_constraint(hidden, pltpu.HBM),
        pltpu.with_memory_space_constraint(grads, pltpu.HBM),
    )


def scale_kernel(clip_norm, factor, pos_ref, own, mine, other, hi_ref, lo_ref, ratio_ref):
    y, core = pos_ref[2], pos_ref[3]

    def square(k, d):
        start = (NX - 1) * PIECE if k == 0 else (k - 1) * PIECE + QUARTER

        def partial(ref, r):
            note = ref[pl.ds(r * BUNDLE + start, NOTE), :].astype(jnp.float32)
            return note[3 * d : 3 * d + 1] + note[3 * d + 1 : 3 * d + 2] + note[3 * d + 2 : 3 * d + 3]

        def of(ref):
            return (partial(ref, 0) + partial(ref, 2)) + (partial(ref, 1) + partial(ref, 3))

        return of(mine) + of(other)

    def ratio(k, d):
        return jnp.sqrt(square(k, d) + EPSILON) / clip_norm

    def weight(r):
        return jnp.minimum(1.0, 1.0 / r) / factor

    def put(rows, cols, value, w):
        scaled = value.astype(jnp.float32) * w
        hi = scaled.astype(hi_ref.dtype)
        hi_ref[rows, cols] = hi
        lo_ref[rows, cols] = (scaled - hi.astype(jnp.float32)).astype(lo_ref.dtype)

    row = lax.broadcasted_iota(jnp.int32, ratio_ref.shape, 0)
    r0, r1 = ratio(0, 0), ratio(0, 1)
    ratio_ref[...] = jnp.where(row == 0, r0, r1)
    for d, r in enumerate((r0, r1)):
        put(slice(None), pl.ds(d * SLOT, SLOT), own[:, pl.ds(d * SLOT, SLOT)], weight(r))
    for k in range(1, NX):
        w = [weight(ratio(k, d)) for d in range(2)]
        for ref, doc in ((mine, core), (other, 1 - core)):
            here = jnp.where(doc == 0, w[0], w[1])
            cols = pl.ds(pl.multiple_of((2 * k + doc) * SLOT, SLOT), SLOT)
            for r in range(NY):
                quarter = lax.rem(y + NY - r, NY)
                rows = pl.ds(pl.multiple_of(quarter * QUARTER, QUARTER), QUARTER)
                put(rows, cols, ref[pl.ds(r * BUNDLE + (k - 1) * PIECE, QUARTER), :], here)


def scale(clip_norm, factor, pos, own, mine, other):
    shape = pltpu.VMEM((own.shape[0], NX * own.shape[1]), own.dtype)
    return pl.pallas_call(
        lambda *refs: scale_kernel(clip_norm, factor, *refs),
        out_shape=(shape, shape, jax.ShapeDtypeStruct((8, LANES), jnp.float32)),
        in_specs=[SMEM] + [VMEM] * 3,
        out_specs=(VMEM,) * 3,
        compiler_params=pltpu.CompilerParams(vmem_limit_bytes=GRANT),
        cost_estimate=cost(4 * 10**6, 6 * 10**6),
    )(pos, near(own), near(mine), near(other))


def decode(code):
    rows = code.shape[0] - EXTRA
    mant = code[rows : rows + 1, :].astype(jnp.int32).astype(jnp.float32)
    expo = code[rows + 1 : rows + 2, :].astype(jnp.int32).astype(jnp.float32)
    step = mant * jnp.exp2(expo) * (1.0 / (MANT * LIMIT))
    return code[:rows, :].astype(jnp.int32).astype(jnp.float32) * step


def encode(total, out_ref):
    rows, width = total.shape
    peak = jnp.max(jnp.abs(total), axis=0, keepdims=True)
    expo = jnp.clip(jnp.floor(jnp.log2(jnp.maximum(peak, 1e-30))), -90.0, 90.0)
    mant = jnp.ceil(peak * jnp.exp2(-expo) * MANT)
    step = mant * jnp.exp2(expo) * (1.0 / (MANT * LIMIT))
    inverse = jnp.where(mant > 0.0, 1.0 / jnp.maximum(step, 1e-37), 0.0)
    q = jnp.clip(jnp.round(total * inverse), -LIMIT, LIMIT)
    row = lax.broadcasted_iota(jnp.int32, (EXTRA, width), 0)
    tail = jnp.where(row == 0, mant, expo)
    out_ref[pl.ds(0, rows), :] = q.astype(jnp.int32).astype(jnp.int16)
    out_ref[pl.ds(rows, EXTRA), :] = tail.astype(jnp.int32).astype(jnp.int16)


def product(rows, hi_ref, lo_ref, h_refs):
    total, token = None, 0
    for h in h_refs:
        size = h.shape[0]
        for g in (hi_ref, lo_ref):
            term = jnp.dot(g[rows, pl.ds(token, size)], h[...], preferred_element_type=jnp.float32)
            total = term if total is None else total + term
        token += size
    return total


def first_kernel(up_j, down_j, hi_ref, lo_ref, *refs):
    *h_refs, up_ref, down_ref = refs
    low = min(up_j, down_j)
    both = product(pl.ds(low * LANES, 2 * LANES), hi_ref, lo_ref, h_refs)
    for j, out_ref in ((up_j, up_ref), (down_j, down_ref)):
        encode(both[(j - low) * LANES : (j - low + 1) * LANES], out_ref)


def rest_kernel(skip, hi_ref, lo_ref, *refs):
    *h_refs, out_ref = refs
    for first, stop in ((0, skip[0]), (skip[1] + 1, NZ)):
        at = first if first == 0 else first - 2
        size = (stop - first) * LANES
        out_ref[pl.ds(at * LANES, size), :] = product(pl.ds(first * LANES, size), hi_ref, lo_ref, h_refs)


def hop_kernel(i, recv_ref, parts_ref, out_ref):
    total = parts_ref[pl.ds(i * LANES, LANES), :] + decode(recv_ref[...])
    encode(total, out_ref)


def last_kernel(i, up_ref, down_ref, parts_ref, out_ref):
    out_ref[...] = parts_ref[pl.ds(i * LANES, LANES), :] + decode(up_ref[...]) + decode(down_ref[...])


def call(kernel, out_shape, flops, *args):
    many = isinstance(out_shape, tuple)
    return pl.pallas_call(
        kernel,
        out_shape=out_shape,
        in_specs=[VMEM] * len(args),
        out_specs=(VMEM,) * len(out_shape) if many else VMEM,
        compiler_params=pltpu.CompilerParams(vmem_limit_bytes=GRANT),
        cost_estimate=cost(flops, 10**6),
    )(*map(near, args))


def shift(value, axis, size, by):
    return lax.ppermute(value, axis, [(i, (i + by) % size) for i in range(size)])


def per_device(hidden, grads, lengths):
    tokens = hidden.shape[0]
    doc_total = lengths.shape[0] * NX * NZ
    ff = hidden.shape[1] * NY * 2
    model_dim = grads.shape[1]
    width = hidden.shape[1] // len(HALVES)
    pos = jnp.stack([lax.axis_index(a) for a in ("z", "x", "y", "core")]).astype(jnp.int32)

    gathered, ready = [], None
    for n in range(len(HALVES)):
        own = lax.slice_in_dim(hidden, n * width, (n + 1) * width, axis=1)
        if ready is not None:
            own, ready = lax.optimization_barrier((own, ready))
        below = shift(own, "x", NX, 1)
        above = shift(own, "x", NX, -1)
        below, above = lax.optimization_barrier((below, above))
        ready = below
        far0 = shift(below[: tokens // 2], "x", NX, 1)
        far1 = shift(above[tokens // 2 :], "x", NX, -1)
        gathered.append((own, below, far0, far1, above))

    own, *sends, note = prepare(lengths, pos, hidden, grads)
    got = [shift(s, "x", NX, k) for k, s in enumerate(sends, 1)]
    bundle = jnp.concatenate(got + [note], axis=0)
    copies = [shift(bundle, "y", NY, r) for r in (1, 2, 3)]
    mine = jnp.concatenate([bundle] + copies, axis=0)
    other = shift(mine, "core", 2, 1)
    clip_norm = CLIP_RATIO * math.sqrt(SLOT * ff * model_dim)
    factor = CLIP_RATIO * math.sqrt(SLOT * doc_total)
    hi, lo, ratio = scale(clip_norm, factor, pos, own, mine, other)

    code = pltpu.VMEM((LANES + EXTRA, width), jnp.int16)
    blocks, parts = [], None
    for (up_hops, down_hops), h in zip(HALVES, gathered):
        up, down = list(range(7 - up_hops, 7)), list(range(down_hops - 1, -1, -1))
        if parts is not None:
            *h, parts = lax.optimization_barrier((*h, parts))
        up_got, down_got = call(
            lambda *r, a=up[0], b=down[0]: first_kernel(a, b, *r), (code, code), 10**9, hi, lo, *h
        )
        skip = (down[0], up[0])
        left = [j for j in range(NZ) if j not in skip]
        parts = call(
            lambda *r, s=skip: rest_kernel(s, *r),
            pltpu.VMEM((len(left) * LANES, width), jnp.float32),
            3 * 10**9,
            hi,
            lo,
            *h,
        )
        up_got, down_got = shift(up_got, "z", NZ, 1), shift(down_got, "z", NZ, -1)
        for n in range(1, max(up_hops, down_hops)):
            for way, order in ((1, up), (-1, down)):
                if n < len(order):
                    i = left.index(order[n])
                    have = up_got if way == 1 else down_got
                    new = call(lambda *r, i=i: hop_kernel(i, *r), code, 10**6, have, parts)
                    new = shift(new, "z", NZ, way)
                    if way == 1:
                        up_got = new
                    else:
                        down_got = new
        i = left.index(NZ - 1)
        blocks.append(
            call(
                lambda *r, i=i: last_kernel(i, *r),
                jax.ShapeDtypeStruct((LANES, width), jnp.float32),
                10**6,
                up_got,
                down_got,
                parts,
            )
        )
    return jnp.concatenate(blocks, axis=1), ratio[:2, 0]


def solution(mesh):
    fine = Mesh(mesh.devices.reshape(NZ, NX, NY, 2), ("z", "x", "y", "core"))
    doc, tensor = ("z", "x"), ("y", "core")
    return jax.shard_map(
        per_device,
        mesh=fine,
        in_specs=(P(doc, tensor), P(doc, None), P(doc)),
        out_specs=(P(doc, tensor), P(doc)),
        check_vma=False,
    )
```

time: 357 us -> 104 us (0.29)
  the two profiles are of different devices: /device:TPU:1 before, /device:TPU:6 now
where the time goes in v1:
time: 104 us
  starting transfers between devices  44.5 us (43%)
  waiting for transfers between devices  36.5 us (35%)
  Pallas kernels  19.5 us (19%)
  local copies, waits for them, and re-layouts  1.59 us (2%)
  other arithmetic  1.06 us (1%)
    ppermute x29, starting transfers between devices, shift(): lax.ppermute(value, axis, [(i, (i + by) % size) for i in range(size)])  44.5 us
    ppermute x29, waiting for transfers between devices, shift(): lax.ppermute(value, axis, [(i, (i + by) % size) for i in range(size)])  36.5 us
    pallas_call x16, Pallas kernels, call(): pl.pallas_call(kernel, out_shape=out_shape, in_specs=[VMEM] * len(args),...  13.3 us
    pallas_call x1, Pallas kernels, prepare(): pl.pallas_call(prepare_kernel, out_shape=(pltpu.VMEM((NZ * LANES, grads.s...  4.28 us
  transfers between devices with their start and end apart: 29, of which 16 were waited for; matrix products, arithmetic and copies ran while one was open for 1% of the time, Pallas kernels for 14%

profile of v1, /device:TPU:6, one launch (start us, length us, event | category | flops | bytes accessed | tf_op | source)
XLA Modules:
  0.0 104.0 jit_solution(18192341021565710104)
XLA Ops:
  1.4 4.3 %shard_map.50 = (bf16[1024,256]{1,0:T(8,128)(2,1)S(1)}, bf16[272,128]{1,0:T(8,128)(2,1)S(1)}, bf16[272,128]{1,0:T(8,128)(2,1)S(1)}, bf16[272,128]{1,0:T(8,128)(2,1)S(1)}, bf16[16,128]{1,0:T(8,128)(2,1)S(1)}) custom-call(s32[2]{0:T(128)S(1)} %copy-done, s32[4]{0:T(128)S(1)} %pad_add_fusion.pos_ref.refs_0_, bf16[256,1792]{1,0:T(8,128)(2,1)} %hidden_hbm.1, ...), custom_call_target="tpu_custom_call" | custom-call | flops 400000000 | bytes 5000000 | tf_op jit(solution)/shard_map/pallas_call | solution.py:96
  5.7 2.3 %collective-permute-start = (bf16[272,128]{1,0:T(8,128)(2,1)S(1)}, bf16[272,128]{1,0:T(8,128)(2,1)S(1)}, u32[]{:S(2)}, u32[]{:S(2)}) collective-permute-start(bf16[272,128]{1,0:T(8,128)(2,1)S(1)} %get-tuple-element.25), channel_id=1, source_target_pairs={{0,8},{8,16},{16,24},{24,0},{1,9},{9,17},{17,25},{25,1},{2,10},{10... | collective-permute-start | bytes 208904 | tf_op jit(solution)/shard_map/ppermute | solution.py:249
  10.5 3.2 %collective-permute-done.1 = bf16[272,128]{1,0:T(8,128)(2,1)S(1)} collective-permute-done((bf16[272,128]{1,0:T(8,128)(2,1)S(1)}, bf16[272,128]{1,0:T(8,128)(2,1)S(1)}, u32[]{:S(2)}, u32[]{:S(2)}) %collective-permute-start.1) | collective-permute-done | bytes 69664 | tf_op jit(solution)/shard_map/ppermute | solution.py:249
  15.8 2.9 %collective-permute-start.4 = (bf16[832,128]{1,0:T(8,128)(2,1)S(1)}, bf16[832,128]{1,0:T(8,128)(2,1)S(1)}, u32[]{:S(2)}, u32[]{:S(2)}) collective-permute-start(bf16[832,128]{1,0:T(8,128)(2,1)S(1)} %get-tuple-element.54), channel_id=1, source_target_pairs={{0,4},{2,6},{4,0},{6,2},{1,5},{3,7},{5,1},{7,3},{8,12},{10,14},{12... | collective-permute-start | bytes 638984 | tf_op jit(solution)/shard_map/ppermute | solution.py:249
  23.5 3.3 %collective-permute-done.4 = bf16[832,128]{1,0:T(8,128)(2,1)S(1)} collective-permute-done((bf16[832,128]{1,0:T(8,128)(2,1)S(1)}, bf16[832,128]{1,0:T(8,128)(2,1)S(1)}, u32[]{:S(2)}, u32[]{:S(2)}) %collective-permute-start.4) | collective-permute-done | bytes 213024 | tf_op jit(solution)/shard_map/ppermute | solution.py:249
  27.2 2.0 %collective-permute-done.7.r_3_ = bf16[256,896]{1,0:T(8,128)(2,1)S(1)} collective-permute-done((bf16[256,896]{1,0:T(8,128)(2,1)S(1)}, bf16[256,896]{1,0:T(8,128)(2,1)S(1)}, u32[]{:S(2)}, u32[]{:S(2)}) %collective-permute-start.7) | collective-permute-done | bytes 458784 | tf_op jit(solution)/shard_map/ppermute | solution.py:249
  29.2 1.8 %collective-permute-done.8.r_6_ = bf16[256,896]{1,0:T(8,128)(2,1)S(1)} collective-permute-done((bf16[256,896]{1,0:T(8,128)(2,1)S(1)}, bf16[256,896]{1,0:T(8,128)(2,1)S(1)}, u32[]{:S(2)}, u32[]{:S(2)}) %collective-permute-start.8) | collective-permute-done | bytes 458784 | tf_op jit(solution)/shard_map/ppermute | solution.py:249
  31.3 1.7 %collective-permute-start.19 = (bf16[256,896]{1,0:T(8,128)(2,1)S(1)}, bf16[256,896]{1,0:T(8,128)(2,1)S(1)}, u32[]{:S(2)}, u32[]{:S(2)}) collective-permute-start(bf16[256,896]{1,0:T(8,128)(2,1)S(1)} %get-tuple-element.38.r_2_), channel_id=1, source_target_pairs={{0,24},{8,0},{16,8},{24,16},{1,25},{9,1},{17,9},{25,17},{2,26},{10... | collective-permute-start | bytes 1376264 | tf_op jit(solution)/shard_map/ppermute | solution.py:249
  35.3 8.5 %collective-permute-done.18.r_3_ = bf16[256,896]{1,0:T(8,128)(2,1)S(1)} collective-permute-done((bf16[256,896]{1,0:T(8,128)(2,1)S(1)}, bf16[256,896]{1,0:T(8,128)(2,1)S(1)}, u32[]{:S(2)}, u32[]{:S(2)}) %collective-permute-start.18) | collective-permute-done | bytes 458784 | tf_op jit(solution)/shard_map/ppermute | solution.py:249
  43.7 2.2 %collective-permute-done.19.r_6_ = bf16[256,896]{1,0:T(8,128)(2,1)S(1)} collective-permute-done((bf16[256,896]{1,0:T(8,128)(2,1)S(1)}, bf16[256,896]{1,0:T(8,128)(2,1)S(1)}, u32[]{:S(2)}, u32[]{:S(2)}) %collective-permute-start.19) | collective-permute-done | bytes 458784 | tf_op jit(solution)/shard_map/ppermute | solution.py:249
  46.0 2.3 %collective-permute-start.21 = (bf16[128,896]{1,0:T(8,128)(2,1)S(1)}, bf16[128,896]{1,0:T(8,128)(2,1)S(1)}, u32[]{:S(2)}, u32[]{:S(2)}) collective-permute-start(bf16[128,896]{1,0:T(8,128)(2,1)S(1)} %slice.26), channel_id=1, source_target_pairs={{0,24},{8,0},{16,8},{24,16},{1,25},{9,1},{17,9},{25,17},{2,26},{10... | collective-permute-start | bytes 688136 | tf_op jit(solution)/shard_map/ppermute | solution.py:249
  48.3 1.9 %shard_map.51 = (bf16[1024,1024]{1,0:T(8,128)(2,1)S(1)}, bf16[1024,1024]{1,0:T(8,128)(2,1)S(1)}, f32[8,128]{1,0:T(8,128)S(1)}) custom-call(s32[4]{0:T(128)S(1)} %pad_add_fusion.pos_ref.refs_0_, bf16[1024,256]{1,0:T(8,128)(2,1)S(1)} %get-tuple-element.24.refs_1_, bf16[3328,128]{1,0:T(8,128)(2,1)S(1)} %constant_dynamic-update-slice_fusion.4.refs_2_, ...), custom_call_target="tpu_custom_call" | custom-call | flops 4000000 | bytes 6000000 | tf_op jit(solution)/shard_map/pallas_call | solution.py:168
  51.8 5.9 %collective-permute-start.15 = (s16[136,896]{1,0:T(8,128)(2,1)S(1)}, s16[136,896]{1,0:T(8,128)(2,1)S(1)}, u32[]{:S(2)}, u32[]{:S(2)}) collective-permute-start(s16[136,896]{1,0:T(8,128)(2,1)S(1)} %get-tuple-element.34), channel_id=1, source_target_pairs={{0,224},{32,0},{64,32},{96,64},{128,96},{160,128},{192,160},{224,1... | collective-permute-start | bytes 731144 | tf_op jit(solution)/shard_map/ppermute | solution.py:249
  57.7 4.1 %shard_map.53.r_1_.r_2_ = f32[768,896]{1,0:T(8,128)S(1)} custom-call(bf16[1024,1024]{1,0:T(8,128)(2,1)S(1)} %get-tuple-element.29.r_0_, bf16[1024,1024]{1,0:T(8,128)(2,1)S(1)} %get-tuple-element.30.r_1_, bf16[256,896]{1,0:T(8,128)(2,1)S(1)} %get-tuple-element.46.r_2_, bf16[256,896]{1,0:T(8,128)(2,1)S(1)} %collective-permute-done.7.r_3_, ...), custom_call_target="tpu_custom_call" | custom-call | flops 3000000000 | bytes 1000000 | tf_op jit(solution)/shard_map/pallas_call | solution.py:238
  63.4 3.3 %collective-permute-start.25 = (s16[136,896]{1,0:T(8,128)(2,1)S(1)}, s16[136,896]{1,0:T(8,128)(2,1)S(1)}, u32[]{:S(2)}, u32[]{:S(2)}) collective-permute-start(s16[136,896]{1,0:T(8,128)(2,1)S(1)} %get-tuple-element.44), channel_id=1, source_target_pairs={{0,224},{32,0},{64,32},{96,64},{128,96},{160,128},{192,160},{224,1... | collective-permute-start | bytes 731144 | tf_op jit(solution)/shard_map/ppermute | solution.py:249
  67.3 4.1 %shard_map.61.r_1_.r_2_ = f32[768,896]{1,0:T(8,128)S(1)} custom-call(bf16[1024,1024]{1,0:T(8,128)(2,1)S(1)} %get-tuple-element.29.r_0_, bf16[1024,1024]{1,0:T(8,128)(2,1)S(1)} %get-tuple-element.30.r_1_, bf16[256,896]{1,0:T(8,128)(2,1)S(1)} %get-tuple-element.38.r_2_, bf16[256,896]{1,0:T(8,128)(2,1)S(1)} %collective-permute-done.18.r_3_, ...), custom_call_target="tpu_custom_call" | custom-call | flops 3000000000 | bytes 1000000 | tf_op jit(solution)/shard_map/pallas_call | solution.py:238
  73.2 3.8 %collective-permute-start.26 = (s16[136,896]{1,0:T(8,128)(2,1)S(1)}, s16[136,896]{1,0:T(8,128)(2,1)S(1)}, u32[]{:S(2)}, u32[]{:S(2)}) collective-permute-start(s16[136,896]{1,0:T(8,128)(2,1)S(1)} %shard_map.64), channel_id=1, source_target_pairs={{0,224},{32,0},{64,32},{96,64},{128,96},{160,128},{192,160},{224,1... | collective-permute-start | bytes 731144 | tf_op jit(solution)/shard_map/ppermute | solution.py:249
  77.4 2.1 %collective-permute-start.23 = (s16[136,896]{1,0:T(8,128)(2,1)S(1)}, s16[136,896]{1,0:T(8,128)(2,1)S(1)}, u32[]{:S(2)}, u32[]{:S(2)}) collective-permute-start(s16[136,896]{1,0:T(8,128)(2,1)S(1)} %shard_map.62), channel_id=1, source_target_pairs={{0,32},{32,64},{64,96},{96,128},{128,160},{160,192},{192,224},{224... | collective-permute-start | bytes 731144 | tf_op jit(solution)/shard_map/ppermute | solution.py:249
  80.5 2.7 %collective-permute-done.26.r_0_ = s16[136,896]{1,0:T(8,128)(2,1)S(1)} collective-permute-done((s16[136,896]{1,0:T(8,128)(2,1)S(1)}, s16[136,896]{1,0:T(8,128)(2,1)S(1)}, u32[]{:S(2)}, u32[]{:S(2)}) %collective-permute-start.26) | collective-permute-done | bytes 243744 | tf_op jit(solution)/shard_map/ppermute | solution.py:249
  83.4 3.8 %collective-permute-start.27 = (s16[136,896]{1,0:T(8,128)(2,1)S(1)}, s16[136,896]{1,0:T(8,128)(2,1)S(1)}, u32[]{:S(2)}, u32[]{:S(2)}) collective-permute-start(s16[136,896]{1,0:T(8,128)(2,1)S(1)} %shard_map.65), channel_id=1, source_target_pairs={{0,224},{32,0},{64,32},{96,64},{128,96},{160,128},{192,160},{224,1... | collective-permute-start | bytes 731144 | tf_op jit(solution)/shard_map/ppermute | solution.py:249
  88.6 3.8 %collective-permute-start.17 = (s16[136,896]{1,0:T(8,128)(2,1)S(1)}, s16[136,896]{1,0:T(8,128)(2,1)S(1)}, u32[]{:S(2)}, u32[]{:S(2)}) collective-permute-start(s16[136,896]{1,0:T(8,128)(2,1)S(1)} %shard_map.58), channel_id=1, source_target_pairs={{0,224},{32,0},{64,32},{96,64},{128,96},{160,128},{192,160},{224,1... | collective-permute-start | bytes 731144 | tf_op jit(solution)/shard_map/ppermute | solution.py:249
  93.1 3.6 %collective-permute-start.28 = (s16[136,896]{1,0:T(8,128)(2,1)S(1)}, s16[136,896]{1,0:T(8,128)(2,1)S(1)}, u32[]{:S(2)}, u32[]{:S(2)}) collective-permute-start(s16[136,896]{1,0:T(8,128)(2,1)S(1)} %shard_map.66), channel_id=1, source_target_pairs={{0,224},{32,0},{64,32},{96,64},{128,96},{160,128},{192,160},{224,1... | collective-permute-start | bytes 731144 | tf_op jit(solution)/shard_map/ppermute | solution.py:249
  97.4 2.8 %collective-permute-done.14.r_0_ = s16[136,896]{1,0:T(8,128)(2,1)S(1)} collective-permute-done((s16[136,896]{1,0:T(8,128)(2,1)S(1)}, s16[136,896]{1,0:T(8,128)(2,1)S(1)}, u32[]{:S(2)}, u32[]{:S(2)}) %collective-permute-start.14) | collective-permute-done | bytes 243744 | tf_op jit(solution)/shard_map/ppermute | solution.py:249
  100.4 2.5 %collective-permute-done.24.r_0_ = s16[136,896]{1,0:T(8,128)(2,1)S(1)} collective-permute-done((s16[136,896]{1,0:T(8,128)(2,1)S(1)}, s16[136,896]{1,0:T(8,128)(2,1)S(1)}, u32[]{:S(2)}, u32[]{:S(2)}) %collective-permute-start.24) | collective-permute-done | bytes 243744 | tf_op jit(solution)/shard_map/ppermute | solution.py:249
  (71 shorter events, 24.3 us)
Async XLA Ops:
  14.5 9.0 %collective-permute-start.3 = (bf16[832,128]{1,0:T(8,128)(2,1)S(1)}, bf16[832,128]{1,0:T(8,128)(2,1)S(1)}, u32[]{:S(2)}, u32[]{:S(2)}) collective-permute-start(bf16[832,128]{1,0:T(8,128)(2,1)S(1)} %get-tuple-element.54), channel_id=1, source_target_pairs={{0,2},{2,4},{4,6},{6,0},{1,3},{3,5},{5,7},{7,1},{8,10},{10,12},{12... | collective-permute-start | bytes 638984 | tf_op jit(solution)/shard_map/ppermute | solution.py:249
  15.8 11.0 %collective-permute-start.4 = (bf16[832,128]{1,0:T(8,128)(2,1)S(1)}, bf16[832,128]{1,0:T(8,128)(2,1)S(1)}, u32[]{:S(2)}, u32[]{:S(2)}) collective-permute-start(bf16[832,128]{1,0:T(8,128)(2,1)S(1)} %get-tuple-element.54), channel_id=1, source_target_pairs={{0,4},{2,6},{4,0},{6,2},{1,5},{3,7},{5,1},{7,3},{8,12},{10,14},{12... | collective-permute-start | bytes 638984 | tf_op jit(solution)/shard_map/ppermute | solution.py:249
  18.8 10.4 %collective-permute-start.7 = (bf16[256,896]{1,0:T(8,128)(2,1)S(1)}, bf16[256,896]{1,0:T(8,128)(2,1)S(1)}, u32[]{:S(2)}, u32[]{:S(2)}) collective-permute-start(bf16[256,896]{1,0:T(8,128)(2,1)S(1)} %get-tuple-element.46.r_2_), channel_id=1, source_target_pairs={{0,8},{8,16},{16,24},{24,0},{1,9},{9,17},{17,25},{25,1},{2,10},{10... | collective-permute-start | bytes 1376264 | tf_op jit(solution)/shard_map/ppermute | solution.py:249
  19.5 11.5 %collective-permute-start.8 = (bf16[256,896]{1,0:T(8,128)(2,1)S(1)}, bf16[256,896]{1,0:T(8,128)(2,1)S(1)}, u32[]{:S(2)}, u32[]{:S(2)}) collective-permute-start(bf16[256,896]{1,0:T(8,128)(2,1)S(1)} %get-tuple-element.46.r_2_), channel_id=1, source_target_pairs={{0,24},{8,0},{16,8},{24,16},{1,25},{9,1},{17,9},{25,17},{2,26},{10... | collective-permute-start | bytes 1376264 | tf_op jit(solution)/shard_map/ppermute | solution.py:249
  27.1 21.2 %collective-permute-start.6 = (bf16[3328,128]{1,0:T(8,128)(2,1)S(1)}, bf16[3328,128]{1,0:T(8,128)(2,1)S(1)}, u32[]{:S(2)}, u32[]{:S(2)}) collective-permute-start(bf16[3328,128]{1,0:T(8,128)(2,1)S(1)} %constant_dynamic-update-slice_fusion.4.refs_2_), channel_id=1, source_target_pairs={{0,1},{1,0},{2,3},{3,2},{4,5},{5,4},{6,7},{7,6},{8,9},{9,8},{10,11... | collective-permute-start | bytes 2555912 | tf_op jit(solution)/shard_map/ppermute | solution.py:249
  31.0 12.7 %collective-permute-start.18 = (bf16[256,896]{1,0:T(8,128)(2,1)S(1)}, bf16[256,896]{1,0:T(8,128)(2,1)S(1)}, u32[]{:S(2)}, u32[]{:S(2)}) collective-permute-start(bf16[256,896]{1,0:T(8,128)(2,1)S(1)} %get-tuple-element.38.r_2_), channel_id=1, source_target_pairs={{0,8},{8,16},{16,24},{24,0},{1,9},{9,17},{17,25},{25,1},{2,10},{10... | collective-permute-start | bytes 1376264 | tf_op jit(solution)/shard_map/ppermute | solution.py:249
  31.3 14.6 %collective-permute-start.19 = (bf16[256,896]{1,0:T(8,128)(2,1)S(1)}, bf16[256,896]{1,0:T(8,128)(2,1)S(1)}, u32[]{:S(2)}, u32[]{:S(2)}) collective-permute-start(bf16[256,896]{1,0:T(8,128)(2,1)S(1)} %get-tuple-element.38.r_2_), channel_id=1, source_target_pairs={{0,24},{8,0},{16,8},{24,16},{1,25},{9,1},{17,9},{25,17},{2,26},{10... | collective-permute-start | bytes 1376264 | tf_op jit(solution)/shard_map/ppermute | solution.py:249
  33.0 17.1 %collective-permute-start.9 = (bf16[128,896]{1,0:T(8,128)(2,1)S(1)}, bf16[128,896]{1,0:T(8,128)(2,1)S(1)}, u32[]{:S(2)}, u32[]{:S(2)}) collective-permute-start(bf16[128,896]{1,0:T(8,128)(2,1)S(1)} %slice.22), channel_id=1, source_target_pairs={{0,8},{8,16},{16,24},{24,0},{1,9},{9,17},{17,25},{25,1},{2,10},{10... | collective-permute-start | bytes 688136 | tf_op jit(solution)/shard_map/ppermute | solution.py:249
  34.6 15.5 %collective-permute-start.10 = (bf16[128,896]{1,0:T(8,128)(2,1)S(1)}, bf16[128,896]{1,0:T(8,128)(2,1)S(1)}, u32[]{:S(2)}, u32[]{:S(2)}) collective-permute-start(bf16[128,896]{1,0:T(8,128)(2,1)S(1)} %slice.23), channel_id=1, source_target_pairs={{0,24},{8,0},{16,8},{24,16},{1,25},{9,1},{17,9},{25,17},{2,26},{10... | collective-permute-start | bytes 688136 | tf_op jit(solution)/shard_map/ppermute | solution.py:249
  45.9 15.9 %collective-permute-start.20 = (bf16[128,896]{1,0:T(8,128)(2,1)S(1)}, bf16[128,896]{1,0:T(8,128)(2,1)S(1)}, u32[]{:S(2)}, u32[]{:S(2)}) collective-permute-start(bf16[128,896]{1,0:T(8,128)(2,1)S(1)} %slice.25), channel_id=1, source_target_pairs={{0,8},{8,16},{16,24},{24,0},{1,9},{9,17},{17,25},{25,1},{2,10},{10... | collective-permute-start | bytes 688136 | tf_op jit(solution)/shard_map/ppermute | solution.py:249
  46.0 15.8 %collective-permute-start.21 = (bf16[128,896]{1,0:T(8,128)(2,1)S(1)}, bf16[128,896]{1,0:T(8,128)(2,1)S(1)}, u32[]{:S(2)}, u32[]{:S(2)}) collective-permute-start(bf16[128,896]{1,0:T(8,128)(2,1)S(1)} %slice.26), channel_id=1, source_target_pairs={{0,24},{8,0},{16,8},{24,16},{1,25},{9,1},{17,9},{25,17},{2,26},{10... | collective-permute-start | bytes 688136 | tf_op jit(solution)/shard_map/ppermute | solution.py:249
  51.8 25.1 %collective-permute-start.15 = (s16[136,896]{1,0:T(8,128)(2,1)S(1)}, s16[136,896]{1,0:T(8,128)(2,1)S(1)}, u32[]{:S(2)}, u32[]{:S(2)}) collective-permute-start(s16[136,896]{1,0:T(8,128)(2,1)S(1)} %get-tuple-element.34), channel_id=1, source_target_pairs={{0,224},{32,0},{64,32},{96,64},{128,96},{160,128},{192,160},{224,1... | collective-permute-start | bytes 731144 | tf_op jit(solution)/shard_map/ppermute | solution.py:249
  57.7 9.0 %collective-permute-start.11 = (s16[136,896]{1,0:T(8,128)(2,1)S(1)}, s16[136,896]{1,0:T(8,128)(2,1)S(1)}, u32[]{:S(2)}, u32[]{:S(2)}) collective-permute-start(s16[136,896]{1,0:T(8,128)(2,1)S(1)} %get-tuple-element.33), channel_id=1, source_target_pairs={{0,32},{32,64},{64,96},{96,128},{128,160},{160,192},{192,224},{224... | collective-permute-start | bytes 731144 | tf_op jit(solution)/shard_map/ppermute | solution.py:249
  63.4 9.5 %collective-permute-start.25 = (s16[136,896]{1,0:T(8,128)(2,1)S(1)}, s16[136,896]{1,0:T(8,128)(2,1)S(1)}, u32[]{:S(2)}, u32[]{:S(2)}) collective-permute-start(s16[136,896]{1,0:T(8,128)(2,1)S(1)} %get-tuple-element.44), channel_id=1, source_target_pairs={{0,224},{32,0},{64,32},{96,64},{128,96},{160,128},{192,160},{224,1... | collective-permute-start | bytes 731144 | tf_op jit(solution)/shard_map/ppermute | solution.py:249
  66.8 10.5 %collective-permute-start.22 = (s16[136,896]{1,0:T(8,128)(2,1)S(1)}, s16[136,896]{1,0:T(8,128)(2,1)S(1)}, u32[]{:S(2)}, u32[]{:S(2)}) collective-permute-start(s16[136,896]{1,0:T(8,128)(2,1)S(1)} %get-tuple-element.43), channel_id=1, source_target_pairs={{0,32},{32,64},{64,96},{96,128},{128,160},{160,192},{192,224},{224... | collective-permute-start | bytes 731144 | tf_op jit(solution)/shard_map/ppermute | solution.py:249
  66.9 13.3 %collective-permute-start.12 = (s16[136,896]{1,0:T(8,128)(2,1)S(1)}, s16[136,896]{1,0:T(8,128)(2,1)S(1)}, u32[]{:S(2)}, u32[]{:S(2)}) collective-permute-start(s16[136,896]{1,0:T(8,128)(2,1)S(1)} %shard_map.54), channel_id=1, source_target_pairs={{0,32},{32,64},{64,96},{96,128},{128,160},{160,192},{192,224},{224... | collective-permute-start | bytes 731144 | tf_op jit(solution)/shard_map/ppermute | solution.py:249
  73.2 10.1 %collective-permute-start.26 = (s16[136,896]{1,0:T(8,128)(2,1)S(1)}, s16[136,896]{1,0:T(8,128)(2,1)S(1)}, u32[]{:S(2)}, u32[]{:S(2)}) collective-permute-start(s16[136,896]{1,0:T(8,128)(2,1)S(1)} %shard_map.64), channel_id=1, source_target_pairs={{0,224},{32,0},{64,32},{96,64},{128,96},{160,128},{192,160},{224,1... | collective-permute-start | bytes 731144 | tf_op jit(solution)/shard_map/ppermute | solution.py:249
  77.1 11.3 %collective-permute-start.16 = (s16[136,896]{1,0:T(8,128)(2,1)S(1)}, s16[136,896]{1,0:T(8,128)(2,1)S(1)}, u32[]{:S(2)}, u32[]{:S(2)}) collective-permute-start(s16[136,896]{1,0:T(8,128)(2,1)S(1)} %shard_map.57), channel_id=1, source_target_pairs={{0,224},{32,0},{64,32},{96,64},{128,96},{160,128},{192,160},{224,1... | collective-permute-start | bytes 731144 | tf_op jit(solution)/shard_map/ppermute | solution.py:249
  77.4 15.0 %collective-permute-start.23 = (s16[136,896]{1,0:T(8,128)(2,1)S(1)}, s16[136,896]{1,0:T(8,128)(2,1)S(1)}, u32[]{:S(2)}, u32[]{:S(2)}) collective-permute-start(s16[136,896]{1,0:T(8,128)(2,1)S(1)} %shard_map.62), channel_id=1, source_target_pairs={{0,32},{32,64},{64,96},{96,128},{128,160},{160,192},{192,224},{224... | collective-permute-start | bytes 731144 | tf_op jit(solution)/shard_map/ppermute | solution.py:249
  80.4 12.2 %collective-permute-start.13 = (s16[136,896]{1,0:T(8,128)(2,1)S(1)}, s16[136,896]{1,0:T(8,128)(2,1)S(1)}, u32[]{:S(2)}, u32[]{:S(2)}) collective-permute-start(s16[136,896]{1,0:T(8,128)(2,1)S(1)} %shard_map.55), channel_id=1, source_target_pairs={{0,32},{32,64},{64,96},{96,128},{128,160},{160,192},{192,224},{224... | collective-permute-start | bytes 731144 | tf_op jit(solution)/shard_map/ppermute | solution.py:249
  83.4 9.5 %collective-permute-start.27 = (s16[136,896]{1,0:T(8,128)(2,1)S(1)}, s16[136,896]{1,0:T(8,128)(2,1)S(1)}, u32[]{:S(2)}, u32[]{:S(2)}) collective-permute-start(s16[136,896]{1,0:T(8,128)(2,1)S(1)} %shard_map.65), channel_id=1, source_target_pairs={{0,224},{32,0},{64,32},{96,64},{128,96},{160,128},{192,160},{224,1... | collective-permute-start | bytes 731144 | tf_op jit(solution)/shard_map/ppermute | solution.py:249
  88.6 8.8 %collective-permute-start.17 = (s16[136,896]{1,0:T(8,128)(2,1)S(1)}, s16[136,896]{1,0:T(8,128)(2,1)S(1)}, u32[]{:S(2)}, u32[]{:S(2)}) collective-permute-start(s16[136,896]{1,0:T(8,128)(2,1)S(1)} %shard_map.58), channel_id=1, source_target_pairs={{0,224},{32,0},{64,32},{96,64},{128,96},{160,128},{192,160},{224,1... | collective-permute-start | bytes 731144 | tf_op jit(solution)/shard_map/ppermute | solution.py:249
  92.9 10.0 %collective-permute-start.24 = (s16[136,896]{1,0:T(8,128)(2,1)S(1)}, s16[136,896]{1,0:T(8,128)(2,1)S(1)}, u32[]{:S(2)}, u32[]{:S(2)}) collective-permute-start(s16[136,896]{1,0:T(8,128)(2,1)S(1)} %shard_map.63), channel_id=1, source_target_pairs={{0,32},{32,64},{64,96},{96,128},{128,160},{160,192},{192,224},{224... | collective-permute-start | bytes 731144 | tf_op jit(solution)/shard_map/ppermute | solution.py:249
  93.1 9.7 %collective-permute-start.28 = (s16[136,896]{1,0:T(8,128)(2,1)S(1)}, s16[136,896]{1,0:T(8,128)(2,1)S(1)}, u32[]{:S(2)}, u32[]{:S(2)}) collective-permute-start(s16[136,896]{1,0:T(8,128)(2,1)S(1)} %shard_map.66), channel_id=1, source_target_pairs={{0,224},{32,0},{64,32},{96,64},{128,96},{160,128},{192,160},{224,1... | collective-permute-start | bytes 731144 | tf_op jit(solution)/shard_map/ppermute | solution.py:249
  (7 other events, 48.2 us)

commit v2 on v1

--- a/solution.py
+++ b/solution.py
@@ -43,7 +43,7 @@
     return hi, mid, (rest - mid.astype(jnp.float32)).astype(jnp.bfloat16)
 
 
-def prepare_kernel(len_ref, pos_ref, hidden_hbm, grads_hbm, own_ref, s1, s2, s3, note_ref, masked_ref, grads_ref, hidden_ref, sem):
+def prepare_kernel(pos_ref, hidden_hbm, grads_hbm, own_ref, s1, s2, s3, note_ref, masked_ref, grads_ref, hidden_ref, sem):
     loads = [
         pltpu.make_async_copy(src.at[pl.ds(d * SLOT, SLOT), :], dst.at[pl.ds(d * SLOT, SLOT), :], sem.at[i, d])
         for d in range(2)
@@ -59,7 +59,7 @@
         loads[2 * d].wait()
         g = grads_ref[rows, :]
         token = lax.broadcasted_iota(jnp.int32, g.shape, 0)
-        m = jnp.where(token < len_ref[d], g.astype(jnp.float32), 0.0).astype(g.dtype)
+        m = jnp.where(token < pos_ref[4 + d], g.astype(jnp.float32), 0.0).astype(g.dtype)
         masked_ref[rows, :] = m
         loads[2 * d + 1].wait()
         h = hidden_ref[rows, :]
@@ -91,7 +91,7 @@
         own_ref[pl.ds(j * LANES, LANES), :] = turned(slice(None), j, x)
 
 
-def prepare(lengths, pos, hidden, grads):
+def prepare(pos, hidden, grads):
     piece = pltpu.VMEM((PIECE, LANES), grads.dtype)
     return pl.pallas_call(
         prepare_kernel,
@@ -102,7 +102,7 @@
             piece,
             pltpu.VMEM((NOTE, LANES), grads.dtype),
         ),
-        in_specs=[SMEM, SMEM, HBM, HBM],
+        in_specs=[SMEM, HBM, HBM],
         out_specs=(VMEM,) * 5,
         scratch_shapes=[
             pltpu.VMEM(grads.shape, grads.dtype),
@@ -113,7 +113,6 @@
         compiler_params=pltpu.CompilerParams(vmem_limit_bytes=GRANT),
         cost_estimate=cost(4 * 10**8, 5 * 10**6),
     )(
-        lengths,
         pos,
         pltpu.with_memory_space_constraint(hidden, pltpu.HBM),
         pltpu.with_memory_space_constraint(grads, pltpu.HBM),
@@ -229,8 +228,13 @@
     encode(total, out_ref)
 
 
-def last_kernel(i, up_ref, down_ref, parts_ref, out_ref):
-    out_ref[...] = parts_ref[pl.ds(i * LANES, LANES), :] + decode(up_ref[...]) + decode(down_ref[...])
+def last_kernel(places, *refs):
+    *in_refs, out_ref = refs
+    width = out_ref.shape[1] // len(places)
+    for n, i in enumerate(places):
+        up_ref, down_ref, parts_ref = in_refs[3 * n : 3 * n + 3]
+        total = parts_ref[pl.ds(i * LANES, LANES), :] + decode(up_ref[...]) + decode(down_ref[...])
+        out_ref[:, pl.ds(n * width, width)] = total
 
 
 def call(kernel, out_shape, flops, *args):
@@ -255,7 +259,8 @@
     ff = hidden.shape[1] * NY * 2
     model_dim = grads.shape[1]
     width = hidden.shape[1] // len(HALVES)
-    pos = jnp.stack([lax.axis_index(a) for a in ("z", "x", "y", "core")]).astype(jnp.int32)
+    place = [lax.axis_index(a).astype(jnp.int32) for a in ("z", "x", "y", "core")]
+    pos = jnp.concatenate([jnp.stack(place), lengths])
 
     gathered, ready = [], None
     for n in range(len(HALVES)):
@@ -270,7 +275,7 @@
         far1 = shift(above[tokens // 2 :], "x", NX, -1)
         gathered.append((own, below, far0, far1, above))
 
-    own, *sends, note = prepare(lengths, pos, hidden, grads)
+    own, *sends, note = prepare(pos, hidden, grads)
     got = [shift(s, "x", NX, k) for k, s in enumerate(sends, 1)]
     bundle = jnp.concatenate(got + [note], axis=0)
     copies = [shift(bundle, "y", NY, r) for r in (1, 2, 3)]
@@ -281,48 +286,31 @@
     hi, lo, ratio = scale(clip_norm, factor, pos, own, mine, other)
 
     code = pltpu.VMEM((LANES + EXTRA, width), jnp.int16)
-    blocks, parts = [], None
+    blocks, places = [], []
     for (up_hops, down_hops), h in zip(HALVES, gathered):
         up, down = list(range(7 - up_hops, 7)), list(range(down_hops - 1, -1, -1))
-        if parts is not None:
-            *h, parts = lax.optimization_barrier((*h, parts))
-        up_got, down_got = call(
-            lambda *r, a=up[0], b=down[0]: first_kernel(a, b, *r), (code, code), 10**9, hi, lo, *h
-        )
+        codes = call(lambda *r, a=up[0], b=down[0]: first_kernel(a, b, *r), (code, code), 10**9, hi, lo, *h)
+        codes = list(codes)
         skip = (down[0], up[0])
         left = [j for j in range(NZ) if j not in skip]
-        parts = call(
-            lambda *r, s=skip: rest_kernel(s, *r),
-            pltpu.VMEM((len(left) * LANES, width), jnp.float32),
-            3 * 10**9,
-            hi,
-            lo,
-            *h,
-        )
-        up_got, down_got = shift(up_got, "z", NZ, 1), shift(down_got, "z", NZ, -1)
-        for n in range(1, max(up_hops, down_hops)):
-            for way, order in ((1, up), (-1, down)):
+        shape = pltpu.VMEM((len(left) * LANES, width), jnp.float32)
+        parts = call(lambda *r, s=skip: rest_kernel(s, *r), shape, 3 * 10**9, hi, lo, *h)
+        for n in range(max(up_hops, down_hops)):
+            for at, (way, order) in enumerate(((1, up), (-1, down))):
                 if n < len(order):
-                    i = left.index(order[n])
-                    have = up_got if way == 1 else down_got
-                    new = call(lambda *r, i=i: hop_kernel(i, *r), code, 10**6, have, parts)
-                    new = shift(new, "z", NZ, way)
-                    if way == 1:
-                        up_got = new
-                    else:
-                        down_got = new
-        i = left.index(NZ - 1)
-        blocks.append(
-            call(
-                lambda *r, i=i: last_kernel(i, *r),
-                jax.ShapeDtypeStruct((LANES, width), jnp.float32),
-                10**6,
-                up_got,
-                down_got,
-                parts,
-            )
-        )
-    return jnp.concatenate(blocks, axis=1), ratio[:2, 0]
+                    if n:
+                        i = left.index(order[n])
+                        codes[at] = call(lambda *r, i=i: hop_kernel(i, *r), code, 10**6, codes[at], parts)
+                    codes[at] = shift(codes[at], "z", NZ, way)
+        blocks += [*codes, parts]
+        places.append(left.index(NZ - 1))
+    grad_weight = call(
+        lambda *r: last_kernel(places, *r),
+        jax.ShapeDtypeStruct((LANES, hidden.shape[1]), jnp.float32),
+        10**6,
+        *blocks,
+    )
+    return grad_weight, ratio[:2, 0]
 
 
 def solution(mesh):

time: 104 us -> 104 us (level)
  the two profiles are of different devices: /device:TPU:6 before, /device:TPU:64 now
where the time goes in v2:
time: 104 us
  starting transfers between devices  44.9 us (43%)
  waiting for transfers between devices  36.3 us (35%)
  Pallas kernels  20.1 us (19%)
  local copies, waits for them, and re-layouts  1.75 us (2%)
    ppermute x29, starting transfers between devices, shift(): lax.ppermute(value, axis, [(i, (i + by) % size) for i in range(size)])  44.9 us
    ppermute x29, waiting for transfers between devices, shift(): lax.ppermute(value, axis, [(i, (i + by) % size) for i in range(size)])  36.3 us
    pallas_call x15, Pallas kernels, call(): pl.pallas_call(kernel, out_shape=out_shape, in_specs=[VMEM] * len(args),...  14.3 us
    pallas_call x1, Pallas kernels, prepare(): pl.pallas_call(prepare_kernel, out_shape=(pltpu.VMEM((NZ * LANES, grads.s...  3.96 us
  transfers between devices with their start and end apart: 29, of which 15 were waited for; matrix products, arithmetic and copies ran while one was open for 1% of the time, Pallas kernels for 14%

profile of v2, /device:TPU:64, one launch (start us, length us, event | category | flops | bytes accessed | tf_op | source)
XLA Modules:
  0.0 104.0 jit_solution(5906093680495498684)
XLA Ops:
  1.5 4.0 %shard_map.50 = (bf16[1024,256]{1,0:T(8,128)(2,1)S(1)}, bf16[272,128]{1,0:T(8,128)(2,1)S(1)}, bf16[272,128]{1,0:T(8,128)(2,1)S(1)}, bf16[272,128]{1,0:T(8,128)(2,1)S(1)}, bf16[16,128]{1,0:T(8,128)(2,1)S(1)}) custom-call(s32[6]{0:T(128)S(1)} %concatenate.10.pos_ref.refs_0_, bf16[256,1792]{1,0:T(8,128)(2,1)} %hidden_hbm.1, bf16[256,4096]{1,0:T(8,128)(2,1)} %grads_hbm.1), custom_call_target="tpu_custom_call" | custom-call | flops 400000000 | bytes 5000000 | tf_op jit(solution)/shard_map/pallas_call | solution.py:96
  7.0 2.7 %collective-permute-start.1 = (bf16[272,128]{1,0:T(8,128)(2,1)S(1)}, bf16[272,128]{1,0:T(8,128)(2,1)S(1)}, u32[]{:S(2)}, u32[]{:S(2)}) collective-permute-start(bf16[272,128]{1,0:T(8,128)(2,1)S(1)} %get-tuple-element.21), channel_id=1, source_target_pairs={{0,16},{8,24},{16,0},{24,8},{1,17},{9,25},{17,1},{25,9},{2,18},{10... | collective-permute-start | bytes 208904 | tf_op jit(solution)/shard_map/ppermute | solution.py:253
  14.1 3.3 %collective-permute-start.4 = (bf16[832,128]{1,0:T(8,128)(2,1)S(1)}, bf16[832,128]{1,0:T(8,128)(2,1)S(1)}, u32[]{:S(2)}, u32[]{:S(2)}) collective-permute-start(bf16[832,128]{1,0:T(8,128)(2,1)S(1)} %get-tuple-element.44), channel_id=1, source_target_pairs={{0,4},{2,6},{4,0},{6,2},{1,5},{3,7},{5,1},{7,3},{8,12},{10,14},{12... | collective-permute-start | bytes 638984 | tf_op jit(solution)/shard_map/ppermute | solution.py:253
  18.1 2.7 %collective-permute-start.8 = (bf16[256,896]{1,0:T(8,128)(2,1)S(1)}, bf16[256,896]{1,0:T(8,128)(2,1)S(1)}, u32[]{:S(2)}, u32[]{:S(2)}) collective-permute-start(bf16[256,896]{1,0:T(8,128)(2,1)S(1)} %get-tuple-element.37.r_2_), channel_id=1, source_target_pairs={{0,24},{8,0},{16,8},{24,16},{1,25},{9,1},{17,9},{25,17},{2,26},{10... | collective-permute-start | bytes 1376264 | tf_op jit(solution)/shard_map/ppermute | solution.py:253
  20.8 2.6 %collective-permute-start.5 = (bf16[832,128]{1,0:T(8,128)(2,1)S(1)}, bf16[832,128]{1,0:T(8,128)(2,1)S(1)}, u32[]{:S(2)}, u32[]{:S(2)}) collective-permute-start(bf16[832,128]{1,0:T(8,128)(2,1)S(1)} %get-tuple-element.44), channel_id=1, source_target_pairs={{0,6},{2,0},{4,2},{6,4},{1,7},{3,1},{5,3},{7,5},{8,14},{10,8},{12,... | collective-permute-start | bytes 638984 | tf_op jit(solution)/shard_map/ppermute | solution.py:253
  23.4 2.9 %collective-permute-done.3 = bf16[832,128]{1,0:T(8,128)(2,1)S(1)} collective-permute-done((bf16[832,128]{1,0:T(8,128)(2,1)S(1)}, bf16[832,128]{1,0:T(8,128)(2,1)S(1)}, u32[]{:S(2)}, u32[]{:S(2)}) %collective-permute-start.3) | collective-permute-done | bytes 213024 | tf_op jit(solution)/shard_map/ppermute | solution.py:253
  28.8 3.3 %collective-permute-done.7.r_3_ = bf16[256,896]{1,0:T(8,128)(2,1)S(1)} collective-permute-done((bf16[256,896]{1,0:T(8,128)(2,1)S(1)}, bf16[256,896]{1,0:T(8,128)(2,1)S(1)}, u32[]{:S(2)}, u32[]{:S(2)}) %collective-permute-start.7) | collective-permute-done | bytes 458784 | tf_op jit(solution)/shard_map/ppermute | solution.py:253
  34.2 3.2 %collective-permute-start.10 = (bf16[128,896]{1,0:T(8,128)(2,1)S(1)}, bf16[128,896]{1,0:T(8,128)(2,1)S(1)}, u32[]{:S(2)}, u32[]{:S(2)}) collective-permute-start(bf16[128,896]{1,0:T(8,128)(2,1)S(1)} %slice.23), channel_id=1, source_target_pairs={{0,24},{8,0},{16,8},{24,16},{1,25},{9,1},{17,9},{25,17},{2,26},{10... | collective-permute-start | bytes 688136 | tf_op jit(solution)/shard_map/ppermute | solution.py:253
  37.5 6.2 %collective-permute-done.19.r_6_ = bf16[256,896]{1,0:T(8,128)(2,1)S(1)} collective-permute-done((bf16[256,896]{1,0:T(8,128)(2,1)S(1)}, bf16[256,896]{1,0:T(8,128)(2,1)S(1)}, u32[]{:S(2)}, u32[]{:S(2)}) %collective-permute-start.19) | collective-permute-done | bytes 458784 | tf_op jit(solution)/shard_map/ppermute | solution.py:253
  43.7 3.3 %collective-permute-done.18.r_3_ = bf16[256,896]{1,0:T(8,128)(2,1)S(1)} collective-permute-done((bf16[256,896]{1,0:T(8,128)(2,1)S(1)}, bf16[256,896]{1,0:T(8,128)(2,1)S(1)}, u32[]{:S(2)}, u32[]{:S(2)}) %collective-permute-start.18) | collective-permute-done | bytes 458784 | tf_op jit(solution)/shard_map/ppermute | solution.py:253
  47.1 2.0 %collective-permute-start.20 = (bf16[128,896]{1,0:T(8,128)(2,1)S(1)}, bf16[128,896]{1,0:T(8,128)(2,1)S(1)}, u32[]{:S(2)}, u32[]{:S(2)}) collective-permute-start(bf16[128,896]{1,0:T(8,128)(2,1)S(1)} %slice.25), channel_id=1, source_target_pairs={{0,8},{8,16},{16,24},{24,0},{1,9},{9,17},{17,25},{25,1},{2,10},{10... | collective-permute-start | bytes 688136 | tf_op jit(solution)/shard_map/ppermute | solution.py:253
  53.0 2.0 %collective-permute-start.11 = (s16[136,896]{1,0:T(8,128)(2,1)S(1)}, s16[136,896]{1,0:T(8,128)(2,1)S(1)}, u32[]{:S(2)}, u32[]{:S(2)}) collective-permute-start(s16[136,896]{1,0:T(8,128)(2,1)S(1)} %get-tuple-element.28), channel_id=1, source_target_pairs={{0,32},{32,64},{64,96},{96,128},{128,160},{160,192},{192,224},{224... | collective-permute-start | bytes 731144 | tf_op jit(solution)/shard_map/ppermute | solution.py:253
  55.1 4.0 %shard_map.53.r_1_.r_2_ = f32[768,896]{1,0:T(8,128)S(1)} custom-call(bf16[1024,1024]{1,0:T(8,128)(2,1)S(1)} %get-tuple-element.24.r_0_, bf16[1024,1024]{1,0:T(8,128)(2,1)S(1)} %get-tuple-element.25.r_1_, bf16[256,896]{1,0:T(8,128)(2,1)S(1)} %get-tuple-element.37.r_2_, bf16[256,896]{1,0:T(8,128)(2,1)S(1)} %collective-permute-done.7.r_3_, ...), custom_call_target="tpu_custom_call" | custom-call | flops 3000000000 | bytes 1000000 | tf_op jit(solution)/shard_map/pallas_call | solution.py:242
  60.8 3.1 %collective-permute-start.22 = (s16[136,896]{1,0:T(8,128)(2,1)S(1)}, s16[136,896]{1,0:T(8,128)(2,1)S(1)}, u32[]{:S(2)}, u32[]{:S(2)}) collective-permute-start(s16[136,896]{1,0:T(8,128)(2,1)S(1)} %get-tuple-element.33), channel_id=1, source_target_pairs={{0,32},{32,64},{64,96},{96,128},{128,160},{160,192},{192,224},{224... | collective-permute-start | bytes 731144 | tf_op jit(solution)/shard_map/ppermute | solution.py:253
  63.9 4.1 %shard_map.60.r_1_.r_5_ = f32[768,896]{1,0:T(8,128)S(1)} custom-call(bf16[1024,1024]{1,0:T(8,128)(2,1)S(1)} %get-tuple-element.24.r_0_, bf16[1024,1024]{1,0:T(8,128)(2,1)S(1)} %get-tuple-element.25.r_1_, bf16[256,896]{1,0:T(8,128)(2,1)S(1)} %get-tuple-element.30.r_2_, bf16[256,896]{1,0:T(8,128)(2,1)S(1)} %collective-permute-done.18.r_3_, ...), custom_call_target="tpu_custom_call" | custom-call | flops 3000000000 | bytes 1000000 | tf_op jit(solution)/shard_map/pallas_call | solution.py:242
  68.2 3.3 %collective-permute-start.12 = (s16[136,896]{1,0:T(8,128)(2,1)S(1)}, s16[136,896]{1,0:T(8,128)(2,1)S(1)}, u32[]{:S(2)}, u32[]{:S(2)}) collective-permute-start(s16[136,896]{1,0:T(8,128)(2,1)S(1)} %shard_map.54), channel_id=1, source_target_pairs={{0,32},{32,64},{64,96},{96,128},{128,160},{160,192},{192,224},{224... | collective-permute-start | bytes 731144 | tf_op jit(solution)/shard_map/ppermute | solution.py:253
  74.8 3.0 %collective-permute-start.23 = (s16[136,896]{1,0:T(8,128)(2,1)S(1)}, s16[136,896]{1,0:T(8,128)(2,1)S(1)}, u32[]{:S(2)}, u32[]{:S(2)}) collective-permute-start(s16[136,896]{1,0:T(8,128)(2,1)S(1)} %shard_map.61), channel_id=1, source_target_pairs={{0,32},{32,64},{64,96},{96,128},{128,160},{160,192},{192,224},{224... | collective-permute-start | bytes 731144 | tf_op jit(solution)/shard_map/ppermute | solution.py:253
  77.9 3.3 %collective-permute-start.13 = (s16[136,896]{1,0:T(8,128)(2,1)S(1)}, s16[136,896]{1,0:T(8,128)(2,1)S(1)}, u32[]{:S(2)}, u32[]{:S(2)}) collective-permute-start(s16[136,896]{1,0:T(8,128)(2,1)S(1)} %shard_map.55), channel_id=1, source_target_pairs={{0,32},{32,64},{64,96},{96,128},{128,160},{160,192},{192,224},{224... | collective-permute-start | bytes 731144 | tf_op jit(solution)/shard_map/ppermute | solution.py:253
  81.2 2.7 %collective-permute-done.26.r_0_ = s16[136,896]{1,0:T(8,128)(2,1)S(1)} collective-permute-done((s16[136,896]{1,0:T(8,128)(2,1)S(1)}, s16[136,896]{1,0:T(8,128)(2,1)S(1)}, u32[]{:S(2)}, u32[]{:S(2)}) %collective-permute-start.26) | collective-permute-done | bytes 243744 | tf_op jit(solution)/shard_map/ppermute | solution.py:253
  84.2 5.0 %collective-permute-done.16.r_0_ = s16[136,896]{1,0:T(8,128)(2,1)S(1)} collective-permute-done((s16[136,896]{1,0:T(8,128)(2,1)S(1)}, s16[136,896]{1,0:T(8,128)(2,1)S(1)}, u32[]{:S(2)}, u32[]{:S(2)}) %collective-permute-start.16) | collective-permute-done | bytes 243744 | tf_op jit(solution)/shard_map/ppermute | solution.py:253
  89.6 3.3 %collective-permute-start.24 = (s16[136,896]{1,0:T(8,128)(2,1)S(1)}, s16[136,896]{1,0:T(8,128)(2,1)S(1)}, u32[]{:S(2)}, u32[]{:S(2)}) collective-permute-start(s16[136,896]{1,0:T(8,128)(2,1)S(1)} %shard_map.62), channel_id=1, source_target_pairs={{0,32},{32,64},{64,96},{96,128},{128,160},{160,192},{192,224},{224... | collective-permute-start | bytes 731144 | tf_op jit(solution)/shard_map/ppermute | solution.py:253
  93.1 3.3 %collective-permute-start.14 = (s16[136,896]{1,0:T(8,128)(2,1)S(1)}, s16[136,896]{1,0:T(8,128)(2,1)S(1)}, u32[]{:S(2)}, u32[]{:S(2)}) collective-permute-start(s16[136,896]{1,0:T(8,128)(2,1)S(1)} %shard_map.56), channel_id=1, source_target_pairs={{0,32},{32,64},{64,96},{96,128},{128,160},{160,192},{192,224},{224... | collective-permute-start | bytes 731144 | tf_op jit(solution)/shard_map/ppermute | solution.py:253
  97.3 2.8 %collective-permute-done.14.r_0_ = s16[136,896]{1,0:T(8,128)(2,1)S(1)} collective-permute-done((s16[136,896]{1,0:T(8,128)(2,1)S(1)}, s16[136,896]{1,0:T(8,128)(2,1)S(1)}, u32[]{:S(2)}, u32[]{:S(2)}) %collective-permute-start.14) | collective-permute-done | bytes 243744 | tf_op jit(solution)/shard_map/ppermute | solution.py:253
  100.1 2.7 %collective-permute-done.28.r_4_ = s16[136,896]{1,0:T(8,128)(2,1)S(1)} collective-permute-done((s16[136,896]{1,0:T(8,128)(2,1)S(1)}, s16[136,896]{1,0:T(8,128)(2,1)S(1)}, u32[]{:S(2)}, u32[]{:S(2)}) %collective-permute-start.28) | collective-permute-done | bytes 243744 | tf_op jit(solution)/shard_map/ppermute | solution.py:253
  (67 shorter events, 24.4 us)
Async XLA Ops:
  14.1 12.2 %collective-permute-start.4 = (bf16[832,128]{1,0:T(8,128)(2,1)S(1)}, bf16[832,128]{1,0:T(8,128)(2,1)S(1)}, u32[]{:S(2)}, u32[]{:S(2)}) collective-permute-start(bf16[832,128]{1,0:T(8,128)(2,1)S(1)} %get-tuple-element.44), channel_id=1, source_target_pairs={{0,4},{2,6},{4,0},{6,2},{1,5},{3,7},{5,1},{7,3},{8,12},{10,14},{12... | collective-permute-start | bytes 638984 | tf_op jit(solution)/shard_map/ppermute | solution.py:253
  17.4 8.9 %collective-permute-start.3 = (bf16[832,128]{1,0:T(8,128)(2,1)S(1)}, bf16[832,128]{1,0:T(8,128)(2,1)S(1)}, u32[]{:S(2)}, u32[]{:S(2)}) collective-permute-start(bf16[832,128]{1,0:T(8,128)(2,1)S(1)} %get-tuple-element.44), channel_id=1, source_target_pairs={{0,2},{2,4},{4,6},{6,0},{1,3},{3,5},{5,7},{7,1},{8,10},{10,12},{12... | collective-permute-start | bytes 638984 | tf_op jit(solution)/shard_map/ppermute | solution.py:253
  18.1 10.6 %collective-permute-start.8 = (bf16[256,896]{1,0:T(8,128)(2,1)S(1)}, bf16[256,896]{1,0:T(8,128)(2,1)S(1)}, u32[]{:S(2)}, u32[]{:S(2)}) collective-permute-start(bf16[256,896]{1,0:T(8,128)(2,1)S(1)} %get-tuple-element.37.r_2_), channel_id=1, source_target_pairs={{0,24},{8,0},{16,8},{24,16},{1,25},{9,1},{17,9},{25,17},{2,26},{10... | collective-permute-start | bytes 1376264 | tf_op jit(solution)/shard_map/ppermute | solution.py:253
  20.8 11.2 %collective-permute-start.7 = (bf16[256,896]{1,0:T(8,128)(2,1)S(1)}, bf16[256,896]{1,0:T(8,128)(2,1)S(1)}, u32[]{:S(2)}, u32[]{:S(2)}) collective-permute-start(bf16[256,896]{1,0:T(8,128)(2,1)S(1)} %get-tuple-element.37.r_2_), channel_id=1, source_target_pairs={{0,8},{8,16},{16,24},{24,0},{1,9},{9,17},{17,25},{25,1},{2,10},{10... | collective-permute-start | bytes 1376264 | tf_op jit(solution)/shard_map/ppermute | solution.py:253
  26.8 22.3 %collective-permute-start.6 = (bf16[3328,128]{1,0:T(8,128)(2,1)S(1)}, bf16[3328,128]{1,0:T(8,128)(2,1)S(1)}, u32[]{:S(2)}, u32[]{:S(2)}) collective-permute-start(bf16[3328,128]{1,0:T(8,128)(2,1)S(1)} %constant_dynamic-update-slice_fusion.4.refs_2_), channel_id=1, source_target_pairs={{0,1},{1,0},{2,3},{3,2},{4,5},{5,4},{6,7},{7,6},{8,9},{9,8},{10,11... | collective-permute-start | bytes 2555912 | tf_op jit(solution)/shard_map/ppermute | solution.py:253
  32.1 11.6 %collective-permute-start.19 = (bf16[256,896]{1,0:T(8,128)(2,1)S(1)}, bf16[256,896]{1,0:T(8,128)(2,1)S(1)}, u32[]{:S(2)}, u32[]{:S(2)}) collective-permute-start(bf16[256,896]{1,0:T(8,128)(2,1)S(1)} %get-tuple-element.30.r_2_), channel_id=1, source_target_pairs={{0,24},{8,0},{16,8},{24,16},{1,25},{9,1},{17,9},{25,17},{2,26},{10... | collective-permute-start | bytes 1376264 | tf_op jit(solution)/shard_map/ppermute | solution.py:253
  32.4 14.6 %collective-permute-start.18 = (bf16[256,896]{1,0:T(8,128)(2,1)S(1)}, bf16[256,896]{1,0:T(8,128)(2,1)S(1)}, u32[]{:S(2)}, u32[]{:S(2)}) collective-permute-start(bf16[256,896]{1,0:T(8,128)(2,1)S(1)} %get-tuple-element.30.r_2_), channel_id=1, source_target_pairs={{0,8},{8,16},{16,24},{24,0},{1,9},{9,17},{17,25},{25,1},{2,10},{10... | collective-permute-start | bytes 1376264 | tf_op jit(solution)/shard_map/ppermute | solution.py:253
  34.1 17.2 %collective-permute-start.9 = (bf16[128,896]{1,0:T(8,128)(2,1)S(1)}, bf16[128,896]{1,0:T(8,128)(2,1)S(1)}, u32[]{:S(2)}, u32[]{:S(2)}) collective-permute-start(bf16[128,896]{1,0:T(8,128)(2,1)S(1)} %slice.22), channel_id=1, source_target_pairs={{0,8},{8,16},{16,24},{24,0},{1,9},{9,17},{17,25},{25,1},{2,10},{10... | collective-permute-start | bytes 688136 | tf_op jit(solution)/shard_map/ppermute | solution.py:253
  34.2 17.1 %collective-permute-start.10 = (bf16[128,896]{1,0:T(8,128)(2,1)S(1)}, bf16[128,896]{1,0:T(8,128)(2,1)S(1)}, u32[]{:S(2)}, u32[]{:S(2)}) collective-permute-start(bf16[128,896]{1,0:T(8,128)(2,1)S(1)} %slice.23), channel_id=1, source_target_pairs={{0,24},{8,0},{16,8},{24,16},{1,25},{9,1},{17,9},{25,17},{2,26},{10... | collective-permute-start | bytes 688136 | tf_op jit(solution)/shard_map/ppermute | solution.py:253
  47.0 12.1 %collective-permute-start.21 = (bf16[128,896]{1,0:T(8,128)(2,1)S(1)}, bf16[128,896]{1,0:T(8,128)(2,1)S(1)}, u32[]{:S(2)}, u32[]{:S(2)}) collective-permute-start(bf16[128,896]{1,0:T(8,128)(2,1)S(1)} %slice.26), channel_id=1, source_target_pairs={{0,24},{8,0},{16,8},{24,16},{1,25},{9,1},{17,9},{25,17},{2,26},{10... | collective-permute-start | bytes 688136 | tf_op jit(solution)/shard_map/ppermute | solution.py:253
  47.1 12.1 %collective-permute-start.20 = (bf16[128,896]{1,0:T(8,128)(2,1)S(1)}, bf16[128,896]{1,0:T(8,128)(2,1)S(1)}, u32[]{:S(2)}, u32[]{:S(2)}) collective-permute-start(bf16[128,896]{1,0:T(8,128)(2,1)S(1)} %slice.25), channel_id=1, source_target_pairs={{0,8},{8,16},{16,24},{24,0},{1,9},{9,17},{17,25},{25,1},{2,10},{10... | collective-permute-start | bytes 688136 | tf_op jit(solution)/shard_map/ppermute | solution.py:253
  53.0 15.0 %collective-permute-start.11 = (s16[136,896]{1,0:T(8,128)(2,1)S(1)}, s16[136,896]{1,0:T(8,128)(2,1)S(1)}, u32[]{:S(2)}, u32[]{:S(2)}) collective-permute-start(s16[136,896]{1,0:T(8,128)(2,1)S(1)} %get-tuple-element.28), channel_id=1, source_target_pairs={{0,32},{32,64},{64,96},{96,128},{128,160},{160,192},{192,224},{224... | collective-permute-start | bytes 731144 | tf_op jit(solution)/shard_map/ppermute | solution.py:253
  55.0 18.7 %collective-permute-start.15 = (s16[136,896]{1,0:T(8,128)(2,1)S(1)}, s16[136,896]{1,0:T(8,128)(2,1)S(1)}, u32[]{:S(2)}, u32[]{:S(2)}) collective-permute-start(s16[136,896]{1,0:T(8,128)(2,1)S(1)} %get-tuple-element.29), channel_id=1, source_target_pairs={{0,224},{32,0},{64,32},{96,64},{128,96},{160,128},{192,160},{224,1... | collective-permute-start | bytes 731144 | tf_op jit(solution)/shard_map/ppermute | solution.py:253
  60.8 13.8 %collective-permute-start.22 = (s16[136,896]{1,0:T(8,128)(2,1)S(1)}, s16[136,896]{1,0:T(8,128)(2,1)S(1)}, u32[]{:S(2)}, u32[]{:S(2)}) collective-permute-start(s16[136,896]{1,0:T(8,128)(2,1)S(1)} %get-tuple-element.33), channel_id=1, source_target_pairs={{0,32},{32,64},{64,96},{96,128},{128,160},{160,192},{192,224},{224... | collective-permute-start | bytes 731144 | tf_op jit(solution)/shard_map/ppermute | solution.py:253
  63.9 9.5 %collective-permute-start.25 = (s16[136,896]{1,0:T(8,128)(2,1)S(1)}, s16[136,896]{1,0:T(8,128)(2,1)S(1)}, u32[]{:S(2)}, u32[]{:S(2)}) collective-permute-start(s16[136,896]{1,0:T(8,128)(2,1)S(1)} %get-tuple-element.34), channel_id=1, source_target_pairs={{0,224},{32,0},{64,32},{96,64},{128,96},{160,128},{192,160},{224,1... | collective-permute-start | bytes 731144 | tf_op jit(solution)/shard_map/ppermute | solution.py:253
  68.2 9.6 %collective-permute-start.12 = (s16[136,896]{1,0:T(8,128)(2,1)S(1)}, s16[136,896]{1,0:T(8,128)(2,1)S(1)}, u32[]{:S(2)}, u32[]{:S(2)}) collective-permute-start(s16[136,896]{1,0:T(8,128)(2,1)S(1)} %shard_map.54), channel_id=1, source_target_pairs={{0,32},{32,64},{64,96},{96,128},{128,160},{160,192},{192,224},{224... | collective-permute-start | bytes 731144 | tf_op jit(solution)/shard_map/ppermute | solution.py:253
  73.6 10.4 %collective-permute-start.26 = (s16[136,896]{1,0:T(8,128)(2,1)S(1)}, s16[136,896]{1,0:T(8,128)(2,1)S(1)}, u32[]{:S(2)}, u32[]{:S(2)}) collective-permute-start(s16[136,896]{1,0:T(8,128)(2,1)S(1)} %shard_map.63), channel_id=1, source_target_pairs={{0,224},{32,0},{64,32},{96,64},{128,96},{160,128},{192,160},{224,1... | collective-permute-start | bytes 731144 | tf_op jit(solution)/shard_map/ppermute | solution.py:253
  73.9 15.3 %collective-permute-start.16 = (s16[136,896]{1,0:T(8,128)(2,1)S(1)}, s16[136,896]{1,0:T(8,128)(2,1)S(1)}, u32[]{:S(2)}, u32[]{:S(2)}) collective-permute-start(s16[136,896]{1,0:T(8,128)(2,1)S(1)} %shard_map.57), channel_id=1, source_target_pairs={{0,224},{32,0},{64,32},{96,64},{128,96},{160,128},{192,160},{224,1... | collective-permute-start | bytes 731144 | tf_op jit(solution)/shard_map/ppermute | solution.py:253
  74.8 14.7 %collective-permute-start.23 = (s16[136,896]{1,0:T(8,128)(2,1)S(1)}, s16[136,896]{1,0:T(8,128)(2,1)S(1)}, u32[]{:S(2)}, u32[]{:S(2)}) collective-permute-start(s16[136,896]{1,0:T(8,128)(2,1)S(1)} %shard_map.61), channel_id=1, source_target_pairs={{0,32},{32,64},{64,96},{96,128},{128,160},{160,192},{192,224},{224... | collective-permute-start | bytes 731144 | tf_op jit(solution)/shard_map/ppermute | solution.py:253
  77.9 15.0 %collective-permute-start.13 = (s16[136,896]{1,0:T(8,128)(2,1)S(1)}, s16[136,896]{1,0:T(8,128)(2,1)S(1)}, u32[]{:S(2)}, u32[]{:S(2)}) collective-permute-start(s16[136,896]{1,0:T(8,128)(2,1)S(1)} %shard_map.55), channel_id=1, source_target_pairs={{0,32},{32,64},{64,96},{96,128},{128,160},{160,192},{192,224},{224... | collective-permute-start | bytes 731144 | tf_op jit(solution)/shard_map/ppermute | solution.py:253
  84.1 12.3 %collective-permute-start.27 = (s16[136,896]{1,0:T(8,128)(2,1)S(1)}, s16[136,896]{1,0:T(8,128)(2,1)S(1)}, u32[]{:S(2)}, u32[]{:S(2)}) collective-permute-start(s16[136,896]{1,0:T(8,128)(2,1)S(1)} %shard_map.64), channel_id=1, source_target_pairs={{0,224},{32,0},{64,32},{96,64},{128,96},{160,128},{192,160},{224,1... | collective-permute-start | bytes 731144 | tf_op jit(solution)/shard_map/ppermute | solution.py:253
  89.3 8.0 %collective-permute-start.17 = (s16[136,896]{1,0:T(8,128)(2,1)S(1)}, s16[136,896]{1,0:T(8,128)(2,1)S(1)}, u32[]{:S(2)}, u32[]{:S(2)}) collective-permute-start(s16[136,896]{1,0:T(8,128)(2,1)S(1)} %shard_map.58), channel_id=1, source_target_pairs={{0,224},{32,0},{64,32},{96,64},{128,96},{160,128},{192,160},{224,1... | collective-permute-start | bytes 731144 | tf_op jit(solution)/shard_map/ppermute | solution.py:253
  89.6 7.7 %collective-permute-start.24 = (s16[136,896]{1,0:T(8,128)(2,1)S(1)}, s16[136,896]{1,0:T(8,128)(2,1)S(1)}, u32[]{:S(2)}, u32[]{:S(2)}) collective-permute-start(s16[136,896]{1,0:T(8,128)(2,1)S(1)} %shard_map.62), channel_id=1, source_target_pairs={{0,32},{32,64},{64,96},{96,128},{128,160},{160,192},{192,224},{224... | collective-permute-start | bytes 731144 | tf_op jit(solution)/shard_map/ppermute | solution.py:253
  93.1 7.0 %collective-permute-start.14 = (s16[136,896]{1,0:T(8,128)(2,1)S(1)}, s16[136,896]{1,0:T(8,128)(2,1)S(1)}, u32[]{:S(2)}, u32[]{:S(2)}) collective-permute-start(s16[136,896]{1,0:T(8,128)(2,1)S(1)} %shard_map.56), channel_id=1, source_target_pairs={{0,32},{32,64},{64,96},{96,128},{128,160},{160,192},{192,224},{224... | collective-permute-start | bytes 731144 | tf_op jit(solution)/shard_map/ppermute | solution.py:253
  (6 other events, 46.2 us)

commit v3 on v2

v3 whole, which is shorter than its diff:
```python
import functools
import math

import jax
import jax.numpy as jnp
from jax import lax
from jax.experimental import pallas as pl
from jax.experimental.pallas import tpu as pltpu
from jax.sharding import Mesh, PartitionSpec as P

SLOT = 128
CLIP_RATIO = 2.0
EPSILON = 1e-06
NX, NY, NZ = 4, 4, 8
LANES = 128
QUARTER = NZ * LANES // NY
NOTE = 16
PIECE = QUARTER + NOTE
BUNDLE = (NX - 1) * PIECE + NOTE
HALVES = ((4, 3, 9), (3, 4, 5))
LATER = ((((0, 2), (4, 6)), ((6, 8),)), (((1, 3), (5, 7)), ((0, 1), (7, 8))))
LIMIT = 32767.0
MANT = 8192.0
EXTRA = 8
GRANT = 24 * 2**20

SMEM = pl.BlockSpec(memory_space=pltpu.SMEM)
VMEM = pl.BlockSpec(memory_space=pltpu.VMEM)
HBM = pl.BlockSpec(memory_space=pltpu.HBM)
NT = (((1,), (1,)), ((), ()))


def cost(flops, nbytes):
    return pl.CostEstimate(flops=flops, bytes_accessed=nbytes, transcendentals=0)


def near(value):
    return pltpu.with_memory_space_constraint(value, pltpu.VMEM)


def split(value):
    hi = value.astype(jnp.bfloat16)
    rest = value - hi.astype(jnp.float32)
    mid = rest.astype(jnp.bfloat16)
    return hi, mid, (rest - mid.astype(jnp.float32)).astype(jnp.bfloat16)


def prepare_kernel(len_hbm, hidden_hbm, grads_hbm, own_ref, s1, s2, s3, note_ref, masked_ref, grads_ref, hidden_ref, len_ref, sem, len_sem):
    lengths = pltpu.make_async_copy(len_hbm, len_ref, len_sem)
    lengths.start()
    loads = [
        pltpu.make_async_copy(src.at[pl.ds(d * SLOT, SLOT), :], dst.at[pl.ds(d * SLOT, SLOT), :], sem.at[i, d])
        for d in range(2)
        for i, (src, dst) in enumerate(((grads_hbm, grads_ref), (hidden_hbm, hidden_ref)))
    ]
    for load in loads:
        load.start()
    z, x, y, core = (lax.axis_index(a) for a in ("z", "x", "y", "core"))
    row = lax.broadcasted_iota(jnp.int32, note_ref.shape, 0)
    note = jnp.zeros(note_ref.shape, jnp.float32)
    for d in range(2):
        rows = pl.ds(d * SLOT, SLOT)
        if d == 0:
            lengths.wait()
        loads[2 * d].wait()
        g = grads_ref[rows, :]
        token = lax.broadcasted_iota(jnp.int32, g.shape, 0)
        m = jnp.where(token < len_ref[d], g.astype(jnp.float32), 0.0).astype(g.dtype)
        masked_ref[rows, :] = m
        loads[2 * d + 1].wait()
        h = hidden_ref[rows, :]
        gram_g = lax.dot_general(m, m, NT, preferred_element_type=jnp.float32)
        gram_h = lax.dot_general(h, h, NT, preferred_element_type=jnp.float32)
        square = jnp.sum(gram_g * gram_h)
        whole = jnp.zeros(note_ref.shape, jnp.float32) + square
        for i, term in enumerate(split(whole)):
            note = jnp.where(row == 3 * d + i, term.astype(jnp.float32), note)
    note = note.astype(note_ref.dtype)
    note_ref[...] = note

    r = lax.broadcasted_iota(jnp.int32, (LANES, LANES), 0)
    c = lax.broadcasted_iota(jnp.int32, (LANES, LANES), 1)
    eye = jnp.where(r == c, 1.0, 0.0).astype(masked_ref.dtype)

    def turned(rows, j, dest):
        block = lax.rem(z + 2 * NZ - 1 - j, NZ) * NX + dest
        piece = masked_ref[rows, pl.ds(pl.multiple_of(block * LANES, LANES), LANES)]
        return lax.dot_general(eye, piece, NT, preferred_element_type=jnp.float32).astype(piece.dtype)

    mine = pl.ds(pl.multiple_of(core * SLOT, SLOT), SLOT)
    for k, send in enumerate((s1, s2, s3), 1):
        dest = lax.rem(x + k, NX)
        for i in range(QUARTER // LANES):
            send[pl.ds(i * LANES, LANES), :] = turned(mine, y * (QUARTER // LANES) + i, dest)
        send[pl.ds(QUARTER, NOTE), :] = note
    for j in range(NZ):
        own_ref[pl.ds(j * LANES, LANES), :] = turned(slice(None), j, x)


def prepare(lengths, hidden, grads):
    piece = pltpu.VMEM((PIECE, LANES), grads.dtype)
    return pl.pallas_call(
        prepare_kernel,
        out_shape=(
            pltpu.VMEM((NZ * LANES, grads.shape[0]), grads.dtype),
            piece,
            piece,
            piece,
            pltpu.VMEM((NOTE, LANES), grads.dtype),
        ),
        in_specs=[HBM, HBM, HBM],
        out_specs=(VMEM,) * 5,
        scratch_shapes=[
            pltpu.VMEM(grads.shape, grads.dtype),
            pltpu.VMEM(grads.shape, grads.dtype),
            pltpu.VMEM(hidden.shape, hidden.dtype),
            pltpu.SMEM(lengths.shape, lengths.dtype),
            pltpu.SemaphoreType.DMA((2, 2)),
            pltpu.SemaphoreType.DMA(()),
        ],
        compiler_params=pltpu.CompilerParams(vmem_limit_bytes=GRANT),
        cost_estimate=cost(4 * 10**8, 5 * 10**6),
    )(
        pltpu.with_memory_space_constraint(lengths, pltpu.HBM),
        pltpu.with_memory_space_constraint(hidden, pltpu.HBM),
        pltpu.with_memory_space_constraint(grads, pltpu.HBM),
    )


def ratio_of(clip_norm, mine, other, k, d):
    start = (NX - 1) * PIECE if k == 0 else (k - 1) * PIECE + QUARTER

    def partial(ref, r):
        note = ref[pl.ds(r * BUNDLE + start, NOTE), :].astype(jnp.float32)
        return note[3 * d : 3 * d + 1] + note[3 * d + 1 : 3 * d + 2] + note[3 * d + 2 : 3 * d + 3]

    def of(ref):
        return (partial(ref, 0) + partial(ref, 2)) + (partial(ref, 1) + partial(ref, 3))

    return jnp.sqrt(of(mine) + of(other) + EPSILON) / clip_norm


def weighted(clip_norm, factor, own, mine, other, quarters, hi_ref, lo_ref):
    y, core = lax.axis_index("y"), lax.axis_index("core")

    def put(rows, cols, value, w):
        scaled = value.astype(jnp.float32) * w
        hi = scaled.astype(hi_ref.dtype)
        hi_ref[rows, cols] = hi
        lo_ref[rows, cols] = (scaled - hi.astype(jnp.float32)).astype(lo_ref.dtype)

    def weight(k, d):
        return jnp.minimum(1.0, 1.0 / ratio_of(clip_norm, mine, other, k, d)) / factor

    w = [[weight(k, d) for d in range(2)] for k in range(NX)]
    for at, q in enumerate(quarters):
        rows = pl.ds(at * QUARTER, QUARTER)
        for d in range(2):
            cols = pl.ds(d * SLOT, SLOT)
            put(rows, cols, own[pl.ds(q * QUARTER, QUARTER), cols], w[0][d])
        r = lax.rem(y + NY - q, NY)
        for k in range(1, NX):
            start = pl.multiple_of(r * BUNDLE + (k - 1) * PIECE, NOTE)
            for ref, doc in ((mine, core), (other, 1 - core)):
                cols = pl.ds(pl.multiple_of((2 * k + doc) * SLOT, SLOT), SLOT)
                put(rows, cols, ref[pl.ds(start, QUARTER), :], jnp.where(doc == 0, w[k][0], w[k][1]))


def scale_kernel(clip_norm, factor, own, mine, other, hi_ref, lo_ref, ratio_ref):
    row = lax.broadcasted_iota(jnp.int32, ratio_ref.shape, 0)
    r0, r1 = (ratio_of(clip_norm, mine, other, 0, d) for d in range(2))
    ratio_ref[...] = jnp.where(row == 0, r0, r1)
    weighted(clip_norm, factor, own, mine, other, range(NY), hi_ref, lo_ref)


def decode(code):
    rows = code.shape[0] - EXTRA
    mant = code[rows : rows + 1, :].astype(jnp.int32).astype(jnp.float32)
    expo = code[rows + 1 : rows + 2, :].astype(jnp.int32).astype(jnp.float32)
    step = mant * jnp.exp2(expo) * (1.0 / (MANT * LIMIT))
    return code[:rows, :].astype(jnp.int32).astype(jnp.float32) * step


def encode(total, out_ref):
    rows, width = total.shape
    peak = jnp.max(jnp.abs(total), axis=0, keepdims=True)
    expo = jnp.clip(jnp.floor(jnp.log2(jnp.maximum(peak, 1e-30))), -90.0, 90.0)
    mant = jnp.ceil(peak * jnp.exp2(-expo) * MANT)
    step = mant * jnp.exp2(expo) * (1.0 / (MANT * LIMIT))
    inverse = jnp.where(mant > 0.0, 1.0 / jnp.maximum(step, 1e-37), 0.0)
    q = jnp.clip(jnp.round(total * inverse), -LIMIT, LIMIT)
    row = lax.broadcasted_iota(jnp.int32, (EXTRA, width), 0)
    tail = jnp.where(row == 0, mant, expo)
    out_ref[pl.ds(0, rows), :] = q.astype(jnp.int32).astype(jnp.int16)
    out_ref[pl.ds(rows, EXTRA), :] = tail.astype(jnp.int32).astype(jnp.int16)


def product(rows, hi_ref, lo_ref, h_refs):
    total, token = None, 0
    for h in h_refs:
        size = h.shape[0]
        for g in (hi_ref, lo_ref):
            term = jnp.dot(g[rows, pl.ds(token, size)], h[...], preferred_element_type=jnp.float32)
            total = term if total is None else total + term
        token += size
    return total


def encode_pair(low, up_j, down_j, hi_ref, lo_ref, rows, h_refs, up_ref, down_ref):
    both = product(rows, hi_ref, lo_ref, h_refs)
    for j, out_ref in ((up_j, up_ref), (down_j, down_ref)):
        encode(both[(j - low) * LANES : (j - low + 1) * LANES], out_ref)


def opening_kernel(clip_norm, factor, own, mine, other, *refs):
    *h_refs, up_ref, down_ref, hi_ref, lo_ref = refs
    weighted(clip_norm, factor, own, mine, other, (1,), hi_ref, lo_ref)
    encode_pair(2, 3, 2, hi_ref, lo_ref, slice(None), h_refs, up_ref, down_ref)


def first_kernel(up_j, down_j, hi_ref, lo_ref, *refs):
    *h_refs, up_ref, down_ref = refs
    low = min(up_j, down_j)
    encode_pair(low, up_j, down_j, hi_ref, lo_ref, pl.ds(low * LANES, 2 * LANES), h_refs, up_ref, down_ref)


def later_kernel(ranges, hi_ref, lo_ref, *refs):
    *h_refs, out_ref = refs
    at = 0
    for first, stop in ranges:
        size = (stop - first) * LANES
        out_ref[pl.ds(at, size), :] = product(pl.ds(first * LANES, size), hi_ref, lo_ref, h_refs)
        at += size


def hop_kernel(i, recv_ref, parts_ref, out_ref):
    total = parts_ref[pl.ds(i * LANES, LANES), :] + decode(recv_ref[...])
    encode(total, out_ref)


def last_kernel(places, *refs):
    *in_refs, out_ref = refs
    at = 0
    for n, i in enumerate(places):
        up_ref, down_ref, parts_ref = in_refs[3 * n : 3 * n + 3]
        total = parts_ref[pl.ds(i * LANES, LANES), :] + decode(up_ref[...]) + decode(down_ref[...])
        out_ref[:, pl.ds(at, total.shape[1])] = total
        at += total.shape[1]


def call(kernel, out_shape, flops, *args, scratch=()):
    many = isinstance(out_shape, tuple)
    return pl.pallas_call(
        kernel,
        out_shape=out_shape,
        in_specs=[VMEM] * len(args),
        out_specs=(VMEM,) * len(out_shape) if many else VMEM,
        scratch_shapes=scratch,
        compiler_params=pltpu.CompilerParams(vmem_limit_bytes=GRANT),
        cost_estimate=cost(flops, 10**6),
    )(*map(near, args))


def shift(value, axis, size, by):
    return lax.ppermute(value, axis, [(i, (i + by) % size) for i in range(size)])


def per_device(hidden, grads, lengths):
    tokens = hidden.shape[0]
    doc_total = lengths.shape[0] * NX * NZ
    ff = hidden.shape[1] * NY * 2
    model_dim = grads.shape[1]
    gathered, ready, at = [], None, 0
    for _, _, units in HALVES:
        own = lax.slice_in_dim(hidden, at, at + units * LANES, axis=1)
        at += units * LANES
        if ready is not None:
            own, ready = lax.optimization_barrier((own, ready))
        below = shift(own, "x", NX, 1)
        above = shift(own, "x", NX, -1)
        below, above = lax.optimization_barrier((below, above))
        ready = below
        far0 = shift(below[: tokens // 2], "x", NX, 1)
        far1 = shift(above[tokens // 2 :], "x", NX, -1)
        gathered.append((own, below, far0, far1, above))

    own, *sends, note = prepare(lengths, hidden, grads)
    got = [shift(s, "x", NX, k) for k, s in enumerate(sends, 1)]
    bundle = jnp.concatenate(got + [note], axis=0)
    copies = [shift(bundle, "y", NY, r) for r in (1, 2, 3)]
    mine = jnp.concatenate([bundle] + copies, axis=0)
    other = shift(mine, "core", 2, 1)
    clip_norm = CLIP_RATIO * math.sqrt(SLOT * ff * model_dim)
    factor = CLIP_RATIO * math.sqrt(SLOT * doc_total)
    packs = (own, mine, other)
    wide = pltpu.VMEM((own.shape[0], NX * tokens), own.dtype)
    narrow = pltpu.VMEM((QUARTER, NX * tokens), own.dtype)
    blocks, places, hi, lo = [], [], None, None
    for half, ((up_hops, down_hops, units), h) in enumerate(zip(HALVES, gathered)):
        up, down = list(range(7 - up_hops, 7)), list(range(down_hops - 1, -1, -1))
        width = units * LANES
        code = pltpu.VMEM((LANES + EXTRA, width), jnp.int16)
        if half == 0:
            kernel = functools.partial(opening_kernel, clip_norm, factor)
            codes = call(kernel, (code, code), 10**9, *packs, *h, scratch=[narrow, narrow])
        else:
            kernel = functools.partial(first_kernel, up[0], down[0])
            codes = call(kernel, (code, code), 10**9, hi, lo, *h)
        codes = list(codes)
        if half == 0:
            kernel = functools.partial(scale_kernel, clip_norm, factor)
            tile = jax.ShapeDtypeStruct((8, LANES), jnp.float32)
            hi, lo, ratio = call(kernel, (wide, wide, tile), 4 * 10**6, *packs)
        parts, home = [], {}
        for n, ranges in enumerate(LATER[half]):
            order = [j for first, stop in ranges for j in range(first, stop)]
            home.update({j: (n, i) for i, j in enumerate(order)})
            shape = pltpu.VMEM((len(order) * LANES, width), jnp.float32)
            parts.append(call(functools.partial(later_kernel, ranges), shape, 10**9, hi, lo, *h))
        for n in range(max(up_hops, down_hops)):
            for at, (way, order) in enumerate(((1, up), (-1, down))):
                if n < len(order):
                    if n:
                        p, i = home[order[n]]
                        kernel = functools.partial(hop_kernel, i)
                        codes[at] = call(kernel, code, 10**6, codes[at], parts[p])
                    codes[at] = shift(codes[at], "z", NZ, way)
        p, i = home[NZ - 1]
        blocks += [*codes, parts[p]]
        places.append(i)
    grad_weight = call(
        functools.partial(last_kernel, tuple(places)),
        jax.ShapeDtypeStruct((LANES, hidden.shape[1]), jnp.float32),
        10**6,
        *blocks,
    )
    return grad_weight, ratio[:2, 0]


def solution(mesh):
    fine = Mesh(mesh.devices.reshape(NZ, NX, NY, 2), ("z", "x", "y", "core"))
    doc, tensor = ("z", "x"), ("y", "core")
    return jax.shard_map(
        per_device,
        mesh=fine,
        in_specs=(P(doc, tensor), P(doc, None), P(doc)),
        out_specs=(P(doc, tensor), P(doc)),
        check_vma=False,
    )
```

time: 104 us -> 98.9 us (0.951)
  the two profiles are of different devices: /device:TPU:64 before, /device:TPU:96 now
where the time goes in v3:
time: 98.9 us; the launch traced here: 98.8 us
  starting transfers between devices  48 us (49%)
  waiting for transfers between devices  29.1 us (29%)
  Pallas kernels  19.8 us (20%)
    ppermute x29, starting transfers between devices, shift(): lax.ppermute(value, axis, [(i, (i + by) % size) for i in range(size)])  48 us
    ppermute x29, waiting for transfers between devices, shift(): lax.ppermute(value, axis, [(i, (i + by) % size) for i in range(size)])  29.1 us
    pallas_call x18, Pallas kernels, call(): pl.pallas_call(kernel, out_shape=out_shape, in_specs=[VMEM] * len(args),...  16 us
    pallas_call x1, Pallas kernels, prepare(): pl.pallas_call(prepare_kernel, out_shape=(pltpu.VMEM((NZ * LANES, grads.s...  3.76 us
  transfers between devices with their start and end apart: 29, of which 11 were waited for; matrix products, arithmetic and copies ran while one was open for 1% of the time, Pallas kernels for 15%

profile of v3, /device:TPU:96, one launch (start us, length us, event | category | flops | bytes accessed | tf_op | source)
XLA Modules:
  0.0 98.8 jit_solution(1972167614126518625)
XLA Ops:
  0.6 3.8 %shard_map.50 = (bf16[1024,256]{1,0:T(8,128)(2,1)S(1)}, bf16[272,128]{1,0:T(8,128)(2,1)S(1)}, bf16[272,128]{1,0:T(8,128)(2,1)S(1)}, bf16[272,128]{1,0:T(8,128)(2,1)S(1)}, bf16[16,128]{1,0:T(8,128)(2,1)S(1)}) custom-call(s32[2]{0:T(128)} %len_hbm.1, bf16[256,1792]{1,0:T(8,128)(2,1)} %hidden_hbm.1, bf16[256,4096]{1,0:T(8,128)(2,1)} %grads_hbm.1), custom_call_target="tpu_custom_call" | custom-call | flops 400000000 | bytes 5000000 | tf_op jit(solution)/shard_map/pallas_call | solution.py:102
  6.0 2.7 %collective-permute-start.1 = (bf16[272,128]{1,0:T(8,128)(2,1)S(1)}, bf16[272,128]{1,0:T(8,128)(2,1)S(1)}, u32[]{:S(2)}, u32[]{:S(2)}) collective-permute-start(bf16[272,128]{1,0:T(8,128)(2,1)S(1)} %get-tuple-element.21), channel_id=1, source_target_pairs={{0,16},{8,24},{16,0},{24,8},{1,17},{9,25},{17,1},{25,9},{2,18},{10... | collective-permute-start | bytes 208904 | tf_op jit(solution)/shard_map/ppermute | solution.py:265
  14.7 2.9 %collective-permute-start.4 = (bf16[832,128]{1,0:T(8,128)(2,1)S(1)}, bf16[832,128]{1,0:T(8,128)(2,1)S(1)}, u32[]{:S(2)}, u32[]{:S(2)}) collective-permute-start(bf16[832,128]{1,0:T(8,128)(2,1)S(1)} %get-tuple-element.42), channel_id=1, source_target_pairs={{0,4},{2,6},{4,0},{6,2},{1,5},{3,7},{5,1},{7,3},{8,12},{10,14},{12... | collective-permute-start | bytes 638984 | tf_op jit(solution)/shard_map/ppermute | solution.py:265
  18.3 2.6 %collective-permute-start.8 = (bf16[256,1152]{1,0:T(8,128)(2,1)S(1)}, bf16[256,1152]{1,0:T(8,128)(2,1)S(1)}, u32[]{:S(2)}, u32[]{:S(2)}) collective-permute-start(bf16[256,1152]{1,0:T(8,128)(2,1)S(1)} %slice.21.refs_0_), channel_id=1, source_target_pairs={{0,24},{8,0},{16,8},{24,16},{1,25},{9,1},{17,9},{25,17},{2,26},{10... | collective-permute-start | bytes 1769480 | tf_op jit(solution)/shard_map/ppermute | solution.py:265
  22.3 3.6 %collective-permute-done.4 = bf16[832,128]{1,0:T(8,128)(2,1)S(1)} collective-permute-done((bf16[832,128]{1,0:T(8,128)(2,1)S(1)}, bf16[832,128]{1,0:T(8,128)(2,1)S(1)}, u32[]{:S(2)}, u32[]{:S(2)}) %collective-permute-start.4) | collective-permute-done | bytes 213024 | tf_op jit(solution)/shard_map/ppermute | solution.py:265
  26.9 5.4 %collective-permute-done.7.refs_1_ = bf16[256,1152]{1,0:T(8,128)(2,1)S(1)} collective-permute-done((bf16[256,1152]{1,0:T(8,128)(2,1)S(1)}, bf16[256,1152]{1,0:T(8,128)(2,1)S(1)}, u32[]{:S(2)}, u32[]{:S(2)}) %collective-permute-start.7) | collective-permute-done | bytes 589856 | tf_op jit(solution)/shard_map/ppermute | solution.py:265
  33.0 2.8 %collective-permute-start.10 = (bf16[128,1152]{1,0:T(8,128)(2,1)S(1)}, bf16[128,1152]{1,0:T(8,128)(2,1)S(1)}, u32[]{:S(2)}, u32[]{:S(2)}) collective-permute-start(bf16[128,1152]{1,0:T(8,128)(2,1)S(1)} %slice.23), channel_id=1, source_target_pairs={{0,24},{8,0},{16,8},{24,16},{1,25},{9,1},{17,9},{25,17},{2,26},{10... | collective-permute-start | bytes 884744 | tf_op jit(solution)/shard_map/ppermute | solution.py:265
  35.9 3.2 %collective-permute-start.19 = (bf16[256,640]{1,0:T(8,128)(2,1)S(1)}, bf16[256,640]{1,0:T(8,128)(2,1)S(1)}, u32[]{:S(2)}, u32[]{:S(2)}) collective-permute-start(bf16[256,640]{1,0:T(8,128)(2,1)S(1)} %slice.24.refs_0_), channel_id=1, source_target_pairs={{0,24},{8,0},{16,8},{24,16},{1,25},{9,1},{17,9},{25,17},{2,26},{10... | collective-permute-start | bytes 983048 | tf_op jit(solution)/shard_map/ppermute | solution.py:265
  39.1 4.2 %collective-permute-done.9.refs_2_ = bf16[128,1152]{1,0:T(8,128)(2,1)S(1)} collective-permute-done((bf16[128,1152]{1,0:T(8,128)(2,1)S(1)}, bf16[128,1152]{1,0:T(8,128)(2,1)S(1)}, u32[]{:S(2)}, u32[]{:S(2)}) %collective-permute-start.9) | collective-permute-done | bytes 294944 | tf_op jit(solution)/shard_map/ppermute | solution.py:265
  43.4 2.2 %shard_map.51 = (s16[136,1152]{1,0:T(8,128)(2,1)S(1)}, s16[136,1152]{1,0:T(8,128)(2,1)S(1)}) custom-call(bf16[1024,256]{1,0:T(8,128)(2,1)S(1)} %get-tuple-element.19.own, bf16[3328,128]{1,0:T(8,128)(2,1)S(1)} %constant_dynamic-update-slice_fusion.4.mine, bf16[3328,128]{1,0:T(8,128)(2,1)S(1)} %collective-permute-done.6.other, ...), custom_call_target="tpu_custom_call" | custom-call | flops 1000000000 | bytes 1000000 | tf_op jit(solution)/shard_map/pallas_call | solution.py:253
  45.5 3.2 %collective-permute-start.11 = (s16[136,1152]{1,0:T(8,128)(2,1)S(1)}, s16[136,1152]{1,0:T(8,128)(2,1)S(1)}, u32[]{:S(2)}, u32[]{:S(2)}) collective-permute-start(s16[136,1152]{1,0:T(8,128)(2,1)S(1)} %get-tuple-element.26), channel_id=1, source_target_pairs={{0,32},{32,64},{64,96},{96,128},{128,160},{160,192},{192,224},{224... | collective-permute-start | bytes 940040 | tf_op jit(solution)/shard_map/ppermute | solution.py:265
  49.9 2.4 %collective-permute-start.21 = (bf16[128,640]{1,0:T(8,128)(2,1)S(1)}, bf16[128,640]{1,0:T(8,128)(2,1)S(1)}, u32[]{:S(2)}, u32[]{:S(2)}) collective-permute-start(bf16[128,640]{1,0:T(8,128)(2,1)S(1)} %slice.26), channel_id=1, source_target_pairs={{0,24},{8,0},{16,8},{24,16},{1,25},{9,1},{17,9},{25,17},{2,26},{10... | collective-permute-start | bytes 491528 | tf_op jit(solution)/shard_map/ppermute | solution.py:265
  53.5 3.4 %shard_map.53.parts_ref = f32[512,1152]{1,0:T(8,128)S(1)} custom-call(bf16[1024,1024]{1,0:T(8,128)(2,1)S(1)} %get-tuple-element.27.hi_ref, bf16[1024,1024]{1,0:T(8,128)(2,1)S(1)} %get-tuple-element.28.lo_ref, bf16[256,1152]{1,0:T(8,128)(2,1)S(1)} %slice.21.refs_0_, bf16[256,1152]{1,0:T(8,128)(2,1)S(1)} %collective-permute-done.7.refs_1_, ...), custom_call_target="tpu_custom_call" | custom-call | flops 1000000000 | bytes 1000000 | tf_op jit(solution)/shard_map/pallas_call | solution.py:253
  57.1 3.3 %collective-permute-start.12 = (s16[136,1152]{1,0:T(8,128)(2,1)S(1)}, s16[136,1152]{1,0:T(8,128)(2,1)S(1)}, u32[]{:S(2)}, u32[]{:S(2)}) collective-permute-start(s16[136,1152]{1,0:T(8,128)(2,1)S(1)} %shard_map.54), channel_id=1, source_target_pairs={{0,32},{32,64},{64,96},{96,128},{128,160},{160,192},{192,224},{224... | collective-permute-start | bytes 940040 | tf_op jit(solution)/shard_map/ppermute | solution.py:265
  61.8 3.2 %collective-permute-start.22 = (s16[136,640]{1,0:T(8,128)(2,1)S(1)}, s16[136,640]{1,0:T(8,128)(2,1)S(1)}, u32[]{:S(2)}, u32[]{:S(2)}) collective-permute-start(s16[136,640]{1,0:T(8,128)(2,1)S(1)} %get-tuple-element.33), channel_id=1, source_target_pairs={{0,32},{32,64},{64,96},{96,128},{128,160},{160,192},{192,224},{224... | collective-permute-start | bytes 522248 | tf_op jit(solution)/shard_map/ppermute | solution.py:265
  65.5 2.3 %collective-permute-done.12.recv_ref = s16[136,1152]{1,0:T(8,128)(2,1)S(1)} collective-permute-done((s16[136,1152]{1,0:T(8,128)(2,1)S(1)}, s16[136,1152]{1,0:T(8,128)(2,1)S(1)}, u32[]{:S(2)}, u32[]{:S(2)}) %collective-permute-start.12) | collective-permute-done | bytes 313376 | tf_op jit(solution)/shard_map/ppermute | solution.py:265
  68.1 3.8 %collective-permute-start.13 = (s16[136,1152]{1,0:T(8,128)(2,1)S(1)}, s16[136,1152]{1,0:T(8,128)(2,1)S(1)}, u32[]{:S(2)}, u32[]{:S(2)}) collective-permute-start(s16[136,1152]{1,0:T(8,128)(2,1)S(1)} %shard_map.55), channel_id=1, source_target_pairs={{0,32},{32,64},{64,96},{96,128},{128,160},{160,192},{192,224},{224... | collective-permute-start | bytes 940040 | tf_op jit(solution)/shard_map/ppermute | solution.py:265
  71.8 2.1 %shard_map.61.parts_ref = f32[512,640]{1,0:T(8,128)S(1)} custom-call(bf16[1024,1024]{1,0:T(8,128)(2,1)S(1)} %get-tuple-element.27.hi_ref, bf16[1024,1024]{1,0:T(8,128)(2,1)S(1)} %get-tuple-element.28.lo_ref, bf16[256,640]{1,0:T(8,128)(2,1)S(1)} %slice.24.refs_0_, bf16[256,640]{1,0:T(8,128)(2,1)S(1)} %collective-permute-done.18.refs_1_, ...), custom_call_target="tpu_custom_call" | custom-call | flops 1000000000 | bytes 1000000 | tf_op jit(solution)/shard_map/pallas_call | solution.py:253
  74.3 3.3 %collective-permute-start.23 = (s16[136,640]{1,0:T(8,128)(2,1)S(1)}, s16[136,640]{1,0:T(8,128)(2,1)S(1)}, u32[]{:S(2)}, u32[]{:S(2)}) collective-permute-start(s16[136,640]{1,0:T(8,128)(2,1)S(1)} %shard_map.62), channel_id=1, source_target_pairs={{0,32},{32,64},{64,96},{96,128},{128,160},{160,192},{192,224},{224... | collective-permute-start | bytes 522248 | tf_op jit(solution)/shard_map/ppermute | solution.py:265
  77.6 3.9 %collective-permute-done.26.recv_ref = s16[136,640]{1,0:T(8,128)(2,1)S(1)} collective-permute-done((s16[136,640]{1,0:T(8,128)(2,1)S(1)}, s16[136,640]{1,0:T(8,128)(2,1)S(1)}, u32[]{:S(2)}, u32[]{:S(2)}) %collective-permute-start.26) | collective-permute-done | bytes 174112 | tf_op jit(solution)/shard_map/ppermute | solution.py:265
  84.0 3.3 %collective-permute-start.14 = (s16[136,1152]{1,0:T(8,128)(2,1)S(1)}, s16[136,1152]{1,0:T(8,128)(2,1)S(1)}, u32[]{:S(2)}, u32[]{:S(2)}) collective-permute-start(s16[136,1152]{1,0:T(8,128)(2,1)S(1)} %shard_map.57), channel_id=1, source_target_pairs={{0,32},{32,64},{64,96},{96,128},{128,160},{160,192},{192,224},{224... | collective-permute-start | bytes 940040 | tf_op jit(solution)/shard_map/ppermute | solution.py:265
  88.6 2.1 %collective-permute-start.24 = (s16[136,640]{1,0:T(8,128)(2,1)S(1)}, s16[136,640]{1,0:T(8,128)(2,1)S(1)}, u32[]{:S(2)}, u32[]{:S(2)}) collective-permute-start(s16[136,640]{1,0:T(8,128)(2,1)S(1)} %shard_map.63), channel_id=1, source_target_pairs={{0,32},{32,64},{64,96},{96,128},{128,160},{160,192},{192,224},{224... | collective-permute-start | bytes 522248 | tf_op jit(solution)/shard_map/ppermute | solution.py:265
  91.6 2.6 %collective-permute-done.24.refs_3_ = s16[136,640]{1,0:T(8,128)(2,1)S(1)} collective-permute-done((s16[136,640]{1,0:T(8,128)(2,1)S(1)}, s16[136,640]{1,0:T(8,128)(2,1)S(1)}, u32[]{:S(2)}, u32[]{:S(2)}) %collective-permute-start.24) | collective-permute-done | bytes 174112 | tf_op jit(solution)/shard_map/ppermute | solution.py:265
  94.1 3.4 %collective-permute-done.28.refs_4_ = s16[136,640]{1,0:T(8,128)(2,1)S(1)} collective-permute-done((s16[136,640]{1,0:T(8,128)(2,1)S(1)}, s16[136,640]{1,0:T(8,128)(2,1)S(1)}, u32[]{:S(2)}, u32[]{:S(2)}) %collective-permute-start.28) | collective-permute-done | bytes 174112 | tf_op jit(solution)/shard_map/ppermute | solution.py:265
  (69 shorter events, 22.2 us)
Async XLA Ops:
  13.0 9.3 %collective-permute-start.3 = (bf16[832,128]{1,0:T(8,128)(2,1)S(1)}, bf16[832,128]{1,0:T(8,128)(2,1)S(1)}, u32[]{:S(2)}, u32[]{:S(2)}) collective-permute-start(bf16[832,128]{1,0:T(8,128)(2,1)S(1)} %get-tuple-element.42), channel_id=1, source_target_pairs={{0,2},{2,4},{4,6},{6,0},{1,3},{3,5},{5,7},{7,1},{8,10},{10,12},{12... | collective-permute-start | bytes 638984 | tf_op jit(solution)/shard_map/ppermute | solution.py:265
  14.7 11.3 %collective-permute-start.4 = (bf16[832,128]{1,0:T(8,128)(2,1)S(1)}, bf16[832,128]{1,0:T(8,128)(2,1)S(1)}, u32[]{:S(2)}, u32[]{:S(2)}) collective-permute-start(bf16[832,128]{1,0:T(8,128)(2,1)S(1)} %get-tuple-element.42), channel_id=1, source_target_pairs={{0,4},{2,6},{4,0},{6,2},{1,5},{3,7},{5,1},{7,3},{8,12},{10,14},{12... | collective-permute-start | bytes 638984 | tf_op jit(solution)/shard_map/ppermute | solution.py:265
  17.6 14.7 %collective-permute-start.7 = (bf16[256,1152]{1,0:T(8,128)(2,1)S(1)}, bf16[256,1152]{1,0:T(8,128)(2,1)S(1)}, u32[]{:S(2)}, u32[]{:S(2)}) collective-permute-start(bf16[256,1152]{1,0:T(8,128)(2,1)S(1)} %slice.21.refs_0_), channel_id=1, source_target_pairs={{0,8},{8,16},{16,24},{24,0},{1,9},{9,17},{17,25},{25,1},{2,10},{10... | collective-permute-start | bytes 1769480 | tf_op jit(solution)/shard_map/ppermute | solution.py:265
  18.3 14.0 %collective-permute-start.8 = (bf16[256,1152]{1,0:T(8,128)(2,1)S(1)}, bf16[256,1152]{1,0:T(8,128)(2,1)S(1)}, u32[]{:S(2)}, u32[]{:S(2)}) collective-permute-start(bf16[256,1152]{1,0:T(8,128)(2,1)S(1)} %slice.21.refs_0_), channel_id=1, source_target_pairs={{0,24},{8,0},{16,8},{24,16},{1,25},{9,1},{17,9},{25,17},{2,26},{10... | collective-permute-start | bytes 1769480 | tf_op jit(solution)/shard_map/ppermute | solution.py:265
  26.8 16.5 %collective-permute-start.6 = (bf16[3328,128]{1,0:T(8,128)(2,1)S(1)}, bf16[3328,128]{1,0:T(8,128)(2,1)S(1)}, u32[]{:S(2)}, u32[]{:S(2)}) collective-permute-start(bf16[3328,128]{1,0:T(8,128)(2,1)S(1)} %constant_dynamic-update-slice_fusion.4.mine), channel_id=1, source_target_pairs={{0,1},{1,0},{2,3},{3,2},{4,5},{5,4},{6,7},{7,6},{8,9},{9,8},{10,11... | collective-permute-start | bytes 2555912 | tf_op jit(solution)/shard_map/ppermute | solution.py:265
  32.3 11.0 %collective-permute-start.9 = (bf16[128,1152]{1,0:T(8,128)(2,1)S(1)}, bf16[128,1152]{1,0:T(8,128)(2,1)S(1)}, u32[]{:S(2)}, u32[]{:S(2)}) collective-permute-start(bf16[128,1152]{1,0:T(8,128)(2,1)S(1)} %slice.22), channel_id=1, source_target_pairs={{0,8},{8,16},{16,24},{24,0},{1,9},{9,17},{17,25},{25,1},{2,10},{10... | collective-permute-start | bytes 884744 | tf_op jit(solution)/shard_map/ppermute | solution.py:265
  33.0 10.3 %collective-permute-start.10 = (bf16[128,1152]{1,0:T(8,128)(2,1)S(1)}, bf16[128,1152]{1,0:T(8,128)(2,1)S(1)}, u32[]{:S(2)}, u32[]{:S(2)}) collective-permute-start(bf16[128,1152]{1,0:T(8,128)(2,1)S(1)} %slice.23), channel_id=1, source_target_pairs={{0,24},{8,0},{16,8},{24,16},{1,25},{9,1},{17,9},{25,17},{2,26},{10... | collective-permute-start | bytes 884744 | tf_op jit(solution)/shard_map/ppermute | solution.py:265
  35.8 13.0 %collective-permute-start.18 = (bf16[256,640]{1,0:T(8,128)(2,1)S(1)}, bf16[256,640]{1,0:T(8,128)(2,1)S(1)}, u32[]{:S(2)}, u32[]{:S(2)}) collective-permute-start(bf16[256,640]{1,0:T(8,128)(2,1)S(1)} %slice.24.refs_0_), channel_id=1, source_target_pairs={{0,8},{8,16},{16,24},{24,0},{1,9},{9,17},{17,25},{25,1},{2,10},{10... | collective-permute-start | bytes 983048 | tf_op jit(solution)/shard_map/ppermute | solution.py:265
  35.9 12.9 %collective-permute-start.19 = (bf16[256,640]{1,0:T(8,128)(2,1)S(1)}, bf16[256,640]{1,0:T(8,128)(2,1)S(1)}, u32[]{:S(2)}, u32[]{:S(2)}) collective-permute-start(bf16[256,640]{1,0:T(8,128)(2,1)S(1)} %slice.24.refs_0_), channel_id=1, source_target_pairs={{0,24},{8,0},{16,8},{24,16},{1,25},{9,1},{17,9},{25,17},{2,26},{10... | collective-permute-start | bytes 983048 | tf_op jit(solution)/shard_map/ppermute | solution.py:265
  45.5 11.4 %collective-permute-start.11 = (s16[136,1152]{1,0:T(8,128)(2,1)S(1)}, s16[136,1152]{1,0:T(8,128)(2,1)S(1)}, u32[]{:S(2)}, u32[]{:S(2)}) collective-permute-start(s16[136,1152]{1,0:T(8,128)(2,1)S(1)} %get-tuple-element.26), channel_id=1, source_target_pairs={{0,32},{32,64},{64,96},{96,128},{128,160},{160,192},{192,224},{224... | collective-permute-start | bytes 940040 | tf_op jit(solution)/shard_map/ppermute | solution.py:265
  48.8 11.6 %collective-permute-start.20 = (bf16[128,640]{1,0:T(8,128)(2,1)S(1)}, bf16[128,640]{1,0:T(8,128)(2,1)S(1)}, u32[]{:S(2)}, u32[]{:S(2)}) collective-permute-start(bf16[128,640]{1,0:T(8,128)(2,1)S(1)} %slice.25), channel_id=1, source_target_pairs={{0,8},{8,16},{16,24},{24,0},{1,9},{9,17},{17,25},{25,1},{2,10},{10... | collective-permute-start | bytes 491528 | tf_op jit(solution)/shard_map/ppermute | solution.py:265
  49.9 10.6 %collective-permute-start.21 = (bf16[128,640]{1,0:T(8,128)(2,1)S(1)}, bf16[128,640]{1,0:T(8,128)(2,1)S(1)}, u32[]{:S(2)}, u32[]{:S(2)}) collective-permute-start(bf16[128,640]{1,0:T(8,128)(2,1)S(1)} %slice.26), channel_id=1, source_target_pairs={{0,24},{8,0},{16,8},{24,16},{1,25},{9,1},{17,9},{25,17},{2,26},{10... | collective-permute-start | bytes 491528 | tf_op jit(solution)/shard_map/ppermute | solution.py:265
  52.2 12.8 %collective-permute-start.15 = (s16[136,1152]{1,0:T(8,128)(2,1)S(1)}, s16[136,1152]{1,0:T(8,128)(2,1)S(1)}, u32[]{:S(2)}, u32[]{:S(2)}) collective-permute-start(s16[136,1152]{1,0:T(8,128)(2,1)S(1)} %get-tuple-element.29), channel_id=1, source_target_pairs={{0,224},{32,0},{64,32},{96,64},{128,96},{160,128},{192,160},{224,1... | collective-permute-start | bytes 940040 | tf_op jit(solution)/shard_map/ppermute | solution.py:265
  57.1 10.7 %collective-permute-start.12 = (s16[136,1152]{1,0:T(8,128)(2,1)S(1)}, s16[136,1152]{1,0:T(8,128)(2,1)S(1)}, u32[]{:S(2)}, u32[]{:S(2)}) collective-permute-start(s16[136,1152]{1,0:T(8,128)(2,1)S(1)} %shard_map.54), channel_id=1, source_target_pairs={{0,32},{32,64},{64,96},{96,128},{128,160},{160,192},{192,224},{224... | collective-permute-start | bytes 940040 | tf_op jit(solution)/shard_map/ppermute | solution.py:265
  61.7 12.2 %collective-permute-start.25 = (s16[136,640]{1,0:T(8,128)(2,1)S(1)}, s16[136,640]{1,0:T(8,128)(2,1)S(1)}, u32[]{:S(2)}, u32[]{:S(2)}) collective-permute-start(s16[136,640]{1,0:T(8,128)(2,1)S(1)} %get-tuple-element.34), channel_id=1, source_target_pairs={{0,224},{32,0},{64,32},{96,64},{128,96},{160,128},{192,160},{224,1... | collective-permute-start | bytes 522248 | tf_op jit(solution)/shard_map/ppermute | solution.py:265
  61.8 12.4 %collective-permute-start.22 = (s16[136,640]{1,0:T(8,128)(2,1)S(1)}, s16[136,640]{1,0:T(8,128)(2,1)S(1)}, u32[]{:S(2)}, u32[]{:S(2)}) collective-permute-start(s16[136,640]{1,0:T(8,128)(2,1)S(1)} %get-tuple-element.33), channel_id=1, source_target_pairs={{0,32},{32,64},{64,96},{96,128},{128,160},{160,192},{192,224},{224... | collective-permute-start | bytes 522248 | tf_op jit(solution)/shard_map/ppermute | solution.py:265
  65.2 18.3 %collective-permute-start.16 = (s16[136,1152]{1,0:T(8,128)(2,1)S(1)}, s16[136,1152]{1,0:T(8,128)(2,1)S(1)}, u32[]{:S(2)}, u32[]{:S(2)}) collective-permute-start(s16[136,1152]{1,0:T(8,128)(2,1)S(1)} %shard_map.58), channel_id=1, source_target_pairs={{0,224},{32,0},{64,32},{96,64},{128,96},{160,128},{192,160},{224,1... | collective-permute-start | bytes 940040 | tf_op jit(solution)/shard_map/ppermute | solution.py:265
  68.1 15.7 %collective-permute-start.13 = (s16[136,1152]{1,0:T(8,128)(2,1)S(1)}, s16[136,1152]{1,0:T(8,128)(2,1)S(1)}, u32[]{:S(2)}, u32[]{:S(2)}) collective-permute-start(s16[136,1152]{1,0:T(8,128)(2,1)S(1)} %shard_map.55), channel_id=1, source_target_pairs={{0,32},{32,64},{64,96},{96,128},{128,160},{160,192},{192,224},{224... | collective-permute-start | bytes 940040 | tf_op jit(solution)/shard_map/ppermute | solution.py:265
  74.1 7.4 %collective-permute-start.26 = (s16[136,640]{1,0:T(8,128)(2,1)S(1)}, s16[136,640]{1,0:T(8,128)(2,1)S(1)}, u32[]{:S(2)}, u32[]{:S(2)}) collective-permute-start(s16[136,640]{1,0:T(8,128)(2,1)S(1)} %shard_map.64), channel_id=1, source_target_pairs={{0,224},{32,0},{64,32},{96,64},{128,96},{160,128},{192,160},{224,1... | collective-permute-start | bytes 522248 | tf_op jit(solution)/shard_map/ppermute | solution.py:265
  74.3 14.2 %collective-permute-start.23 = (s16[136,640]{1,0:T(8,128)(2,1)S(1)}, s16[136,640]{1,0:T(8,128)(2,1)S(1)}, u32[]{:S(2)}, u32[]{:S(2)}) collective-permute-start(s16[136,640]{1,0:T(8,128)(2,1)S(1)} %shard_map.62), channel_id=1, source_target_pairs={{0,32},{32,64},{64,96},{96,128},{128,160},{160,192},{192,224},{224... | collective-permute-start | bytes 522248 | tf_op jit(solution)/shard_map/ppermute | solution.py:265
  81.6 9.1 %collective-permute-start.27 = (s16[136,640]{1,0:T(8,128)(2,1)S(1)}, s16[136,640]{1,0:T(8,128)(2,1)S(1)}, u32[]{:S(2)}, u32[]{:S(2)}) collective-permute-start(s16[136,640]{1,0:T(8,128)(2,1)S(1)} %shard_map.65), channel_id=1, source_target_pairs={{0,224},{32,0},{64,32},{96,64},{128,96},{160,128},{192,160},{224,1... | collective-permute-start | bytes 522248 | tf_op jit(solution)/shard_map/ppermute | solution.py:265
  83.7 13.9 %collective-permute-start.17 = (s16[136,1152]{1,0:T(8,128)(2,1)S(1)}, s16[136,1152]{1,0:T(8,128)(2,1)S(1)}, u32[]{:S(2)}, u32[]{:S(2)}) collective-permute-start(s16[136,1152]{1,0:T(8,128)(2,1)S(1)} %shard_map.59), channel_id=1, source_target_pairs={{0,224},{32,0},{64,32},{96,64},{128,96},{160,128},{192,160},{224,1... | collective-permute-start | bytes 940040 | tf_op jit(solution)/shard_map/ppermute | solution.py:265
  84.0 13.5 %collective-permute-start.14 = (s16[136,1152]{1,0:T(8,128)(2,1)S(1)}, s16[136,1152]{1,0:T(8,128)(2,1)S(1)}, u32[]{:S(2)}, u32[]{:S(2)}) collective-permute-start(s16[136,1152]{1,0:T(8,128)(2,1)S(1)} %shard_map.57), channel_id=1, source_target_pairs={{0,32},{32,64},{64,96},{96,128},{128,160},{160,192},{192,224},{224... | collective-permute-start | bytes 940040 | tf_op jit(solution)/shard_map/ppermute | solution.py:265
  90.8 6.7 %collective-permute-start.28 = (s16[136,640]{1,0:T(8,128)(2,1)S(1)}, s16[136,640]{1,0:T(8,128)(2,1)S(1)}, u32[]{:S(2)}, u32[]{:S(2)}) collective-permute-start(s16[136,640]{1,0:T(8,128)(2,1)S(1)} %shard_map.67), channel_id=1, source_target_pairs={{0,224},{32,0},{64,32},{96,64},{128,96},{160,128},{192,160},{224,1... | collective-permute-start | bytes 522248 | tf_op jit(solution)/shard_map/ppermute | solution.py:265
  (6 other events, 44.9 us)

commit v4 on v3

--- a/solution.py
+++ b/solution.py
@@ -17,11 +17,12 @@
 NOTE = 16
 PIECE = QUARTER + NOTE
 BUNDLE = (NX - 1) * PIECE + NOTE
-HALVES = ((4, 3, 9), (3, 4, 5))
+HALVES = ((4, 3, 8), (3, 4, 6))
 LATER = ((((0, 2), (4, 6)), ((6, 8),)), (((1, 3), (5, 7)), ((0, 1), (7, 8))))
 LIMIT = 32767.0
 MANT = 8192.0
 EXTRA = 8
+GROUP = 256
 GRANT = 24 * 2**20
 
 SMEM = pl.BlockSpec(memory_space=pltpu.SMEM)
@@ -45,7 +46,22 @@
     return hi, mid, (rest - mid.astype(jnp.float32)).astype(jnp.bfloat16)
 
 
-def prepare_kernel(len_hbm, hidden_hbm, grads_hbm, own_ref, s1, s2, s3, note_ref, masked_ref, grads_ref, hidden_ref, len_ref, sem, len_sem):
+def turned(masked_ref, rows, j, dest):
+    r = lax.broadcasted_iota(jnp.int32, (LANES, LANES), 0)
+    c = lax.broadcasted_iota(jnp.int32, (LANES, LANES), 1)
+    eye = jnp.where(r == c, 1.0, 0.0).astype(masked_ref.dtype)
+    block = lax.rem(lax.axis_index("z") + 2 * NZ - 1 - j, NZ) * NX + dest
+    piece = masked_ref[rows, pl.ds(pl.multiple_of(block * LANES, LANES), LANES)]
+    return lax.dot_general(eye, piece, NT, preferred_element_type=jnp.float32).astype(piece.dtype)
+
+
+def turn_kernel(masked_ref, own_ref):
+    x = lax.axis_index("x")
+    for j in range(NZ):
+        own_ref[pl.ds(j * LANES, LANES), :] = turned(masked_ref, slice(None), j, x)
+
+
+def prepare_kernel(len_hbm, hidden_hbm, grads_hbm, masked_ref, s1, s2, s3, note_ref, grads_ref, hidden_ref, len_ref, sem, len_sem):
     lengths = pltpu.make_async_copy(len_hbm, len_ref, len_sem)
     lengths.start()
     loads = [
@@ -55,7 +71,7 @@
     ]
     for load in loads:
         load.start()
-    z, x, y, core = (lax.axis_index(a) for a in ("z", "x", "y", "core"))
+    x, y, core = (lax.axis_index(a) for a in ("x", "y", "core"))
     row = lax.broadcasted_iota(jnp.int32, note_ref.shape, 0)
     note = jnp.zeros(note_ref.shape, jnp.float32)
     for d in range(2):
@@ -78,23 +94,12 @@
     note = note.astype(note_ref.dtype)
     note_ref[...] = note
 
-    r = lax.broadcasted_iota(jnp.int32, (LANES, LANES), 0)
-    c = lax.broadcasted_iota(jnp.int32, (LANES, LANES), 1)
-    eye = jnp.where(r == c, 1.0, 0.0).astype(masked_ref.dtype)
-
-    def turned(rows, j, dest):
-        block = lax.rem(z + 2 * NZ - 1 - j, NZ) * NX + dest
-        piece = masked_ref[rows, pl.ds(pl.multiple_of(block * LANES, LANES), LANES)]
-        return lax.dot_general(eye, piece, NT, preferred_element_type=jnp.float32).astype(piece.dtype)
-
     mine = pl.ds(pl.multiple_of(core * SLOT, SLOT), SLOT)
     for k, send in enumerate((s1, s2, s3), 1):
         dest = lax.rem(x + k, NX)
         for i in range(QUARTER // LANES):
-            send[pl.ds(i * LANES, LANES), :] = turned(mine, y * (QUARTER // LANES) + i, dest)
+            send[pl.ds(i * LANES, LANES), :] = turned(masked_ref, mine, y * (QUARTER // LANES) + i, dest)
         send[pl.ds(QUARTER, NOTE), :] = note
-    for j in range(NZ):
-        own_ref[pl.ds(j * LANES, LANES), :] = turned(slice(None), j, x)
 
 
 def prepare(lengths, hidden, grads):
@@ -102,7 +107,7 @@
     return pl.pallas_call(
         prepare_kernel,
         out_shape=(
-            pltpu.VMEM((NZ * LANES, grads.shape[0]), grads.dtype),
+            pltpu.VMEM(grads.shape, grads.dtype),
             piece,
             piece,
             piece,
@@ -111,7 +116,6 @@
         in_specs=[HBM, HBM, HBM],
         out_specs=(VMEM,) * 5,
         scratch_shapes=[
-            pltpu.VMEM(grads.shape, grads.dtype),
             pltpu.VMEM(grads.shape, grads.dtype),
             pltpu.VMEM(hidden.shape, hidden.dtype),
             pltpu.SMEM(lengths.shape, lengths.dtype),
@@ -173,26 +177,34 @@
     weighted(clip_norm, factor, own, mine, other, range(NY), hi_ref, lo_ref)
 
 
-def decode(code):
-    rows = code.shape[0] - EXTRA
-    mant = code[rows : rows + 1, :].astype(jnp.int32).astype(jnp.float32)
-    expo = code[rows + 1 : rows + 2, :].astype(jnp.int32).astype(jnp.float32)
-    step = mant * jnp.exp2(expo) * (1.0 / (MANT * LIMIT))
-    return code[:rows, :].astype(jnp.int32).astype(jnp.float32) * step
+def step_of(mant, expo):
+    return mant * jnp.exp2(expo) * (1.0 / (MANT * LIMIT))
+
+
+def decode(code_ref):
+    groups = code_ref.shape[0] // LANES
+    tail = code_ref[pl.ds(groups * LANES, EXTRA), :].astype(jnp.int32).astype(jnp.float32)
+    out = []
+    for n in range(groups):
+        step = step_of(tail[2 * n : 2 * n + 1], tail[2 * n + 1 : 2 * n + 2])
+        out.append(code_ref[pl.ds(n * LANES, LANES), :].astype(jnp.int32).astype(jnp.float32) * step)
+    return jnp.concatenate(out, axis=1)
 
 
 def encode(total, out_ref):
-    rows, width = total.shape
-    peak = jnp.max(jnp.abs(total), axis=0, keepdims=True)
-    expo = jnp.clip(jnp.floor(jnp.log2(jnp.maximum(peak, 1e-30))), -90.0, 90.0)
-    mant = jnp.ceil(peak * jnp.exp2(-expo) * MANT)
-    step = mant * jnp.exp2(expo) * (1.0 / (MANT * LIMIT))
-    inverse = jnp.where(mant > 0.0, 1.0 / jnp.maximum(step, 1e-37), 0.0)
-    q = jnp.clip(jnp.round(total * inverse), -LIMIT, LIMIT)
-    row = lax.broadcasted_iota(jnp.int32, (EXTRA, width), 0)
-    tail = jnp.where(row == 0, mant, expo)
-    out_ref[pl.ds(0, rows), :] = q.astype(jnp.int32).astype(jnp.int16)
-    out_ref[pl.ds(rows, EXTRA), :] = tail.astype(jnp.int32).astype(jnp.int16)
+    groups = total.shape[1] // GROUP
+    row = lax.broadcasted_iota(jnp.int32, (EXTRA, GROUP), 0)
+    tail = jnp.zeros((EXTRA, GROUP), jnp.float32)
+    for n in range(groups):
+        part = total[:, n * GROUP : (n + 1) * GROUP]
+        peak = jnp.max(jnp.abs(part), axis=0, keepdims=True)
+        expo = jnp.clip(jnp.floor(jnp.log2(jnp.maximum(peak, 1e-30))), -90.0, 90.0)
+        mant = jnp.ceil(peak * jnp.exp2(-expo) * MANT)
+        inverse = jnp.where(mant > 0.0, 1.0 / jnp.maximum(step_of(mant, expo), 1e-37), 0.0)
+        q = jnp.clip(jnp.round(part * inverse), -LIMIT, LIMIT)
+        out_ref[pl.ds(n * LANES, LANES), :] = q.astype(jnp.int32).astype(jnp.int16)
+        tail = jnp.where(row == 2 * n, mant, jnp.where(row == 2 * n + 1, expo, tail))
+    out_ref[pl.ds(groups * LANES, EXTRA), :] = tail.astype(jnp.int32).astype(jnp.int16)
 
 
 def product(rows, hi_ref, lo_ref, h_refs):
@@ -234,7 +246,7 @@
 
 
 def hop_kernel(i, recv_ref, parts_ref, out_ref):
-    total = parts_ref[pl.ds(i * LANES, LANES), :] + decode(recv_ref[...])
+    total = parts_ref[pl.ds(i * LANES, LANES), :] + decode(recv_ref)
     encode(total, out_ref)
 
 
@@ -243,7 +255,7 @@
     at = 0
     for n, i in enumerate(places):
         up_ref, down_ref, parts_ref = in_refs[3 * n : 3 * n + 3]
-        total = parts_ref[pl.ds(i * LANES, LANES), :] + decode(up_ref[...]) + decode(down_ref[...])
+        total = parts_ref[pl.ds(i * LANES, LANES), :] + decode(up_ref) + decode(down_ref)
         out_ref[:, pl.ds(at, total.shape[1])] = total
         at += total.shape[1]
 
@@ -284,12 +296,13 @@
         far1 = shift(above[tokens // 2 :], "x", NX, -1)
         gathered.append((own, below, far0, far1, above))
 
-    own, *sends, note = prepare(lengths, hidden, grads)
+    masked, *sends, note = prepare(lengths, hidden, grads)
     got = [shift(s, "x", NX, k) for k, s in enumerate(sends, 1)]
     bundle = jnp.concatenate(got + [note], axis=0)
     copies = [shift(bundle, "y", NY, r) for r in (1, 2, 3)]
     mine = jnp.concatenate([bundle] + copies, axis=0)
     other = shift(mine, "core", 2, 1)
+    own = call(turn_kernel, pltpu.VMEM((NZ * LANES, tokens), grads.dtype), 10**8, masked)
     clip_norm = CLIP_RATIO * math.sqrt(SLOT * ff * model_dim)
     factor = CLIP_RATIO * math.sqrt(SLOT * doc_total)
     packs = (own, mine, other)
@@ -299,7 +312,7 @@
     for half, ((up_hops, down_hops, units), h) in enumerate(zip(HALVES, gathered)):
         up, down = list(range(7 - up_hops, 7)), list(range(down_hops - 1, -1, -1))
         width = units * LANES
-        code = pltpu.VMEM((LANES + EXTRA, width), jnp.int16)
+        code = pltpu.VMEM((width // GROUP * LANES + EXTRA, GROUP), jnp.int16)
         if half == 0:
             kernel = functools.partial(opening_kernel, clip_norm, factor)
             codes = call(kernel, (code, code), 10**9, *packs, *h, scratch=[narrow, narrow])

time: 98.9 us -> 110 us (1.11)
  the two profiles are of different devices: /device:TPU:96 before, /device:TPU:8 now
where the time goes in v4:
time: 110 us
  starting transfers between devices  52.5 us (48%)
  waiting for transfers between devices  36.9 us (34%)
  Pallas kernels  19.1 us (17%)
    ppermute x29, starting transfers between devices, shift(): lax.ppermute(value, axis, [(i, (i + by) % size) for i in range(size)])  52.5 us
    ppermute x29, waiting for transfers between devices, shift(): lax.ppermute(value, axis, [(i, (i + by) % size) for i in range(size)])  36.9 us
    pallas_call x19, Pallas kernels, call(): pl.pallas_call(kernel, out_shape=out_shape, in_specs=[VMEM] * len(args),...  15.5 us
    pallas_call x1, Pallas kernels, prepare(): pl.pallas_call(prepare_kernel, out_shape=(pltpu.VMEM(grads.shape, grads.d...  3.61 us
  transfers between devices with their start and end apart: 29, of which 13 were waited for; matrix products, arithmetic and copies ran while one was open for 1% of the time, Pallas kernels for 13%

profile of v4, /device:TPU:8, one launch (start us, length us, event | category | flops | bytes accessed | tf_op | source)
XLA Modules:
  0.0 110.3 jit_solution(8367191785299128694)
XLA Ops:
  0.6 3.6 %shard_map.50 = (bf16[256,4096]{1,0:T(8,128)(2,1)S(1)}, bf16[272,128]{1,0:T(8,128)(2,1)S(1)}, bf16[272,128]{1,0:T(8,128)(2,1)S(1)}, bf16[272,128]{1,0:T(8,128)(2,1)S(1)}, bf16[16,128]{1,0:T(8,128)(2,1)S(1)}) custom-call(s32[2]{0:T(128)} %len_hbm.1, bf16[256,1792]{1,0:T(8,128)(2,1)} %hidden_hbm.1, bf16[256,4096]{1,0:T(8,128)(2,1)} %grads_hbm.1), custom_call_target="tpu_custom_call" | custom-call | flops 400000000 | bytes 5000000 | tf_op jit(solution)/shard_map/pallas_call | solution.py:107
  5.8 2.7 %collective-permute-start.1 = (bf16[272,128]{1,0:T(8,128)(2,1)S(1)}, bf16[272,128]{1,0:T(8,128)(2,1)S(1)}, u32[]{:S(2)}, u32[]{:S(2)}) collective-permute-start(bf16[272,128]{1,0:T(8,128)(2,1)S(1)} %get-tuple-element.21), channel_id=1, source_target_pairs={{0,16},{8,24},{16,0},{24,8},{1,17},{9,25},{17,1},{25,9},{2,18},{10... | collective-permute-start | bytes 208904 | tf_op jit(solution)/shard_map/ppermute | solution.py:277
  15.8 2.1 %collective-permute-start.5 = (bf16[832,128]{1,0:T(8,128)(2,1)S(1)}, bf16[832,128]{1,0:T(8,128)(2,1)S(1)}, u32[]{:S(2)}, u32[]{:S(2)}) collective-permute-start(bf16[832,128]{1,0:T(8,128)(2,1)S(1)} %get-tuple-element.42), channel_id=1, source_target_pairs={{0,6},{2,0},{4,2},{6,4},{1,7},{3,1},{5,3},{7,5},{8,14},{10,8},{12,... | collective-permute-start | bytes 638984 | tf_op jit(solution)/shard_map/ppermute | solution.py:277
  17.9 2.9 %collective-permute-done.3 = bf16[832,128]{1,0:T(8,128)(2,1)S(1)} collective-permute-done((bf16[832,128]{1,0:T(8,128)(2,1)S(1)}, bf16[832,128]{1,0:T(8,128)(2,1)S(1)}, u32[]{:S(2)}, u32[]{:S(2)}) %collective-permute-start.3) | collective-permute-done | bytes 213024 | tf_op jit(solution)/shard_map/ppermute | solution.py:277
  20.8 3.2 %collective-permute-done.4 = bf16[832,128]{1,0:T(8,128)(2,1)S(1)} collective-permute-done((bf16[832,128]{1,0:T(8,128)(2,1)S(1)}, bf16[832,128]{1,0:T(8,128)(2,1)S(1)}, u32[]{:S(2)}, u32[]{:S(2)}) %collective-permute-start.4) | collective-permute-done | bytes 213024 | tf_op jit(solution)/shard_map/ppermute | solution.py:277
  25.9 3.2 %collective-permute-start.8 = (bf16[256,1024]{1,0:T(8,128)(2,1)S(1)}, bf16[256,1024]{1,0:T(8,128)(2,1)S(1)}, u32[]{:S(2)}, u32[]{:S(2)}) collective-permute-start(bf16[256,1024]{1,0:T(8,128)(2,1)S(1)} %slice.21.refs_0_), channel_id=1, source_target_pairs={{0,24},{8,0},{16,8},{24,16},{1,25},{9,1},{17,9},{25,17},{2,26},{10... | collective-permute-start | bytes 1572872 | tf_op jit(solution)/shard_map/ppermute | solution.py:277
  29.1 12.3 %collective-permute-done.7.refs_1_ = bf16[256,1024]{1,0:T(8,128)(2,1)S(1)} collective-permute-done((bf16[256,1024]{1,0:T(8,128)(2,1)S(1)}, bf16[256,1024]{1,0:T(8,128)(2,1)S(1)}, u32[]{:S(2)}, u32[]{:S(2)}) %collective-permute-start.7) | collective-permute-done | bytes 524320 | tf_op jit(solution)/shard_map/ppermute | solution.py:277
  42.0 2.8 %collective-permute-start.10 = (bf16[128,1024]{1,0:T(8,128)(2,1)S(1)}, bf16[128,1024]{1,0:T(8,128)(2,1)S(1)}, u32[]{:S(2)}, u32[]{:S(2)}) collective-permute-start(bf16[128,1024]{1,0:T(8,128)(2,1)S(1)} %slice.23), channel_id=1, source_target_pairs={{0,24},{8,0},{16,8},{24,16},{1,25},{9,1},{17,9},{25,17},{2,26},{10... | collective-permute-start | bytes 786440 | tf_op jit(solution)/shard_map/ppermute | solution.py:277
  44.9 3.2 %collective-permute-start.19 = (bf16[256,768]{1,0:T(8,128)(2,1)S(1)}, bf16[256,768]{1,0:T(8,128)(2,1)S(1)}, u32[]{:S(2)}, u32[]{:S(2)}) collective-permute-start(bf16[256,768]{1,0:T(8,128)(2,1)S(1)} %slice.24.refs_0_), channel_id=1, source_target_pairs={{0,24},{8,0},{16,8},{24,16},{1,25},{9,1},{17,9},{25,17},{2,26},{10... | collective-permute-start | bytes 1179656 | tf_op jit(solution)/shard_map/ppermute | solution.py:277
  48.5 3.4 %collective-permute-done.9.refs_2_ = bf16[128,1024]{1,0:T(8,128)(2,1)S(1)} collective-permute-done((bf16[128,1024]{1,0:T(8,128)(2,1)S(1)}, bf16[128,1024]{1,0:T(8,128)(2,1)S(1)}, u32[]{:S(2)}, u32[]{:S(2)}) %collective-permute-start.9) | collective-permute-done | bytes 262176 | tf_op jit(solution)/shard_map/ppermute | solution.py:277
  53.7 2.0 %collective-permute-start.11 = (s16[520,256]{1,0:T(8,128)(2,1)S(1)}, s16[520,256]{1,0:T(8,128)(2,1)S(1)}, u32[]{:S(2)}, u32[]{:S(2)}) collective-permute-start(s16[520,256]{1,0:T(8,128)(2,1)S(1)} %get-tuple-element.26), channel_id=1, source_target_pairs={{0,32},{32,64},{64,96},{96,128},{128,160},{160,192},{192,224},{224... | collective-permute-start | bytes 798728 | tf_op jit(solution)/shard_map/ppermute | solution.py:277
  55.7 3.2 %collective-permute-done.18.refs_1_ = bf16[256,768]{1,0:T(8,128)(2,1)S(1)} collective-permute-done((bf16[256,768]{1,0:T(8,128)(2,1)S(1)}, bf16[256,768]{1,0:T(8,128)(2,1)S(1)}, u32[]{:S(2)}, u32[]{:S(2)}) %collective-permute-start.18) | collective-permute-done | bytes 393248 | tf_op jit(solution)/shard_map/ppermute | solution.py:277
  60.0 2.4 %collective-permute-start.21 = (bf16[128,768]{1,0:T(8,128)(2,1)S(1)}, bf16[128,768]{1,0:T(8,128)(2,1)S(1)}, u32[]{:S(2)}, u32[]{:S(2)}) collective-permute-start(bf16[128,768]{1,0:T(8,128)(2,1)S(1)} %slice.26), channel_id=1, source_target_pairs={{0,24},{8,0},{16,8},{24,16},{1,25},{9,1},{17,9},{25,17},{2,26},{10... | collective-permute-start | bytes 589832 | tf_op jit(solution)/shard_map/ppermute | solution.py:277
  62.4 5.9 %collective-permute-start.15 = (s16[520,256]{1,0:T(8,128)(2,1)S(1)}, s16[520,256]{1,0:T(8,128)(2,1)S(1)}, u32[]{:S(2)}, u32[]{:S(2)}) collective-permute-start(s16[520,256]{1,0:T(8,128)(2,1)S(1)} %get-tuple-element.29), channel_id=1, source_target_pairs={{0,224},{32,0},{64,32},{96,64},{128,96},{160,128},{192,160},{224,1... | collective-permute-start | bytes 798728 | tf_op jit(solution)/shard_map/ppermute | solution.py:277
  69.5 2.9 %shard_map.54.parts_ref = f32[512,1024]{1,0:T(8,128)S(1)} custom-call(bf16[1024,1024]{1,0:T(8,128)(2,1)S(1)} %get-tuple-element.27.hi_ref, bf16[1024,1024]{1,0:T(8,128)(2,1)S(1)} %get-tuple-element.28.lo_ref, bf16[256,1024]{1,0:T(8,128)(2,1)S(1)} %slice.21.refs_0_, bf16[256,1024]{1,0:T(8,128)(2,1)S(1)} %collective-permute-done.7.refs_1_, ...), custom_call_target="tpu_custom_call" | custom-call | flops 1000000000 | bytes 1000000 | tf_op jit(solution)/shard_map/pallas_call | solution.py:265
  74.0 3.3 %collective-permute-start.25 = (s16[392,256]{1,0:T(8,128)(2,1)S(1)}, s16[392,256]{1,0:T(8,128)(2,1)S(1)}, u32[]{:S(2)}, u32[]{:S(2)}) collective-permute-start(s16[392,256]{1,0:T(8,128)(2,1)S(1)} %get-tuple-element.34), channel_id=1, source_target_pairs={{0,224},{32,0},{64,32},{96,64},{128,96},{160,128},{192,160},{224,1... | collective-permute-start | bytes 602120 | tf_op jit(solution)/shard_map/ppermute | solution.py:277
  77.3 2.2 %shard_map.62.parts_ref = f32[512,768]{1,0:T(8,128)S(1)} custom-call(bf16[1024,1024]{1,0:T(8,128)(2,1)S(1)} %get-tuple-element.27.hi_ref, bf16[1024,1024]{1,0:T(8,128)(2,1)S(1)} %get-tuple-element.28.lo_ref, bf16[256,768]{1,0:T(8,128)(2,1)S(1)} %slice.24.refs_0_, bf16[256,768]{1,0:T(8,128)(2,1)S(1)} %collective-permute-done.18.refs_1_, ...), custom_call_target="tpu_custom_call" | custom-call | flops 1000000000 | bytes 1000000 | tf_op jit(solution)/shard_map/pallas_call | solution.py:265
  80.7 3.8 %collective-permute-start.26 = (s16[392,256]{1,0:T(8,128)(2,1)S(1)}, s16[392,256]{1,0:T(8,128)(2,1)S(1)}, u32[]{:S(2)}, u32[]{:S(2)}) collective-permute-start(s16[392,256]{1,0:T(8,128)(2,1)S(1)} %shard_map.65), channel_id=1, source_target_pairs={{0,224},{32,0},{64,32},{96,64},{128,96},{160,128},{192,160},{224,1... | collective-permute-start | bytes 602120 | tf_op jit(solution)/shard_map/ppermute | solution.py:277
  85.0 2.1 %collective-permute-start.13 = (s16[520,256]{1,0:T(8,128)(2,1)S(1)}, s16[520,256]{1,0:T(8,128)(2,1)S(1)}, u32[]{:S(2)}, u32[]{:S(2)}) collective-permute-start(s16[520,256]{1,0:T(8,128)(2,1)S(1)} %shard_map.56), channel_id=1, source_target_pairs={{0,32},{32,64},{64,96},{96,128},{128,160},{160,192},{192,224},{224... | collective-permute-start | bytes 798728 | tf_op jit(solution)/shard_map/ppermute | solution.py:277
  87.3 2.1 %collective-permute-done.26.recv_ref = s16[392,256]{1,0:T(8,128)(2,1)S(1)} collective-permute-done((s16[392,256]{1,0:T(8,128)(2,1)S(1)}, s16[392,256]{1,0:T(8,128)(2,1)S(1)}, u32[]{:S(2)}, u32[]{:S(2)}) %collective-permute-start.26) | collective-permute-done | bytes 200736 | tf_op jit(solution)/shard_map/ppermute | solution.py:277
  89.5 3.8 %collective-permute-start.27 = (s16[392,256]{1,0:T(8,128)(2,1)S(1)}, s16[392,256]{1,0:T(8,128)(2,1)S(1)}, u32[]{:S(2)}, u32[]{:S(2)}) collective-permute-start(s16[392,256]{1,0:T(8,128)(2,1)S(1)} %shard_map.66), channel_id=1, source_target_pairs={{0,224},{32,0},{64,32},{96,64},{128,96},{160,128},{192,160},{224,1... | collective-permute-start | bytes 602120 | tf_op jit(solution)/shard_map/ppermute | solution.py:277
  95.3 3.8 %collective-permute-start.17 = (s16[520,256]{1,0:T(8,128)(2,1)S(1)}, s16[520,256]{1,0:T(8,128)(2,1)S(1)}, u32[]{:S(2)}, u32[]{:S(2)}) collective-permute-start(s16[520,256]{1,0:T(8,128)(2,1)S(1)} %shard_map.60), channel_id=1, source_target_pairs={{0,224},{32,0},{64,32},{96,64},{128,96},{160,128},{192,160},{224,1... | collective-permute-start | bytes 798728 | tf_op jit(solution)/shard_map/ppermute | solution.py:277
  100.9 3.3 %collective-permute-start.28 = (s16[392,256]{1,0:T(8,128)(2,1)S(1)}, s16[392,256]{1,0:T(8,128)(2,1)S(1)}, u32[]{:S(2)}, u32[]{:S(2)}) collective-permute-start(s16[392,256]{1,0:T(8,128)(2,1)S(1)} %shard_map.68), channel_id=1, source_target_pairs={{0,224},{32,0},{64,32},{96,64},{128,96},{160,128},{192,160},{224,1... | collective-permute-start | bytes 602120 | tf_op jit(solution)/shard_map/ppermute | solution.py:277
  104.9 4.2 %collective-permute-done.24.refs_3_ = s16[392,256]{1,0:T(8,128)(2,1)S(1)} collective-permute-done((s16[392,256]{1,0:T(8,128)(2,1)S(1)}, s16[392,256]{1,0:T(8,128)(2,1)S(1)}, u32[]{:S(2)}, u32[]{:S(2)}) %collective-permute-start.24) | collective-permute-done | bytes 200736 | tf_op jit(solution)/shard_map/ppermute | solution.py:277
  (70 shorter events, 25.3 us)
Async XLA Ops:
  14.6 9.4 %collective-permute-start.4 = (bf16[832,128]{1,0:T(8,128)(2,1)S(1)}, bf16[832,128]{1,0:T(8,128)(2,1)S(1)}, u32[]{:S(2)}, u32[]{:S(2)}) collective-permute-start(bf16[832,128]{1,0:T(8,128)(2,1)S(1)} %get-tuple-element.42), channel_id=1, source_target_pairs={{0,4},{2,6},{4,0},{6,2},{1,5},{3,7},{5,1},{7,3},{8,12},{10,14},{12... | collective-permute-start | bytes 638984 | tf_op jit(solution)/shard_map/ppermute | solution.py:277
  15.8 9.7 %collective-permute-start.5 = (bf16[832,128]{1,0:T(8,128)(2,1)S(1)}, bf16[832,128]{1,0:T(8,128)(2,1)S(1)}, u32[]{:S(2)}, u32[]{:S(2)}) collective-permute-start(bf16[832,128]{1,0:T(8,128)(2,1)S(1)} %get-tuple-element.42), channel_id=1, source_target_pairs={{0,6},{2,0},{4,2},{6,4},{1,7},{3,1},{5,3},{7,5},{8,14},{10,8},{12,... | collective-permute-start | bytes 638984 | tf_op jit(solution)/shard_map/ppermute | solution.py:277
  25.6 26.3 %collective-permute-start.6 = (bf16[3328,128]{1,0:T(8,128)(2,1)S(1)}, bf16[3328,128]{1,0:T(8,128)(2,1)S(1)}, u32[]{:S(2)}, u32[]{:S(2)}) collective-permute-start(bf16[3328,128]{1,0:T(8,128)(2,1)S(1)} %constant_dynamic-update-slice_fusion.4.mine), channel_id=1, source_target_pairs={{0,1},{1,0},{2,3},{3,2},{4,5},{5,4},{6,7},{7,6},{8,9},{9,8},{10,11... | collective-permute-start | bytes 2555912 | tf_op jit(solution)/shard_map/ppermute | solution.py:277
  25.7 15.6 %collective-permute-start.7 = (bf16[256,1024]{1,0:T(8,128)(2,1)S(1)}, bf16[256,1024]{1,0:T(8,128)(2,1)S(1)}, u32[]{:S(2)}, u32[]{:S(2)}) collective-permute-start(bf16[256,1024]{1,0:T(8,128)(2,1)S(1)} %slice.21.refs_0_), channel_id=1, source_target_pairs={{0,8},{8,16},{16,24},{24,0},{1,9},{9,17},{17,25},{25,1},{2,10},{10... | collective-permute-start | bytes 1572872 | tf_op jit(solution)/shard_map/ppermute | solution.py:277
  25.9 15.5 %collective-permute-start.8 = (bf16[256,1024]{1,0:T(8,128)(2,1)S(1)}, bf16[256,1024]{1,0:T(8,128)(2,1)S(1)}, u32[]{:S(2)}, u32[]{:S(2)}) collective-permute-start(bf16[256,1024]{1,0:T(8,128)(2,1)S(1)} %slice.21.refs_0_), channel_id=1, source_target_pairs={{0,24},{8,0},{16,8},{24,16},{1,25},{9,1},{17,9},{25,17},{2,26},{10... | collective-permute-start | bytes 1572872 | tf_op jit(solution)/shard_map/ppermute | solution.py:277
  41.4 10.5 %collective-permute-start.9 = (bf16[128,1024]{1,0:T(8,128)(2,1)S(1)}, bf16[128,1024]{1,0:T(8,128)(2,1)S(1)}, u32[]{:S(2)}, u32[]{:S(2)}) collective-permute-start(bf16[128,1024]{1,0:T(8,128)(2,1)S(1)} %slice.22), channel_id=1, source_target_pairs={{0,8},{8,16},{16,24},{24,0},{1,9},{9,17},{17,25},{25,1},{2,10},{10... | collective-permute-start | bytes 786440 | tf_op jit(solution)/shard_map/ppermute | solution.py:277
  42.0 9.8 %collective-permute-start.10 = (bf16[128,1024]{1,0:T(8,128)(2,1)S(1)}, bf16[128,1024]{1,0:T(8,128)(2,1)S(1)}, u32[]{:S(2)}, u32[]{:S(2)}) collective-permute-start(bf16[128,1024]{1,0:T(8,128)(2,1)S(1)} %slice.23), channel_id=1, source_target_pairs={{0,24},{8,0},{16,8},{24,16},{1,25},{9,1},{17,9},{25,17},{2,26},{10... | collective-permute-start | bytes 786440 | tf_op jit(solution)/shard_map/ppermute | solution.py:277
  44.8 14.1 %collective-permute-start.18 = (bf16[256,768]{1,0:T(8,128)(2,1)S(1)}, bf16[256,768]{1,0:T(8,128)(2,1)S(1)}, u32[]{:S(2)}, u32[]{:S(2)}) collective-permute-start(bf16[256,768]{1,0:T(8,128)(2,1)S(1)} %slice.24.refs_0_), channel_id=1, source_target_pairs={{0,8},{8,16},{16,24},{24,0},{1,9},{9,17},{17,25},{25,1},{2,10},{10... | collective-permute-start | bytes 1179656 | tf_op jit(solution)/shard_map/ppermute | solution.py:277
  44.9 14.0 %collective-permute-start.19 = (bf16[256,768]{1,0:T(8,128)(2,1)S(1)}, bf16[256,768]{1,0:T(8,128)(2,1)S(1)}, u32[]{:S(2)}, u32[]{:S(2)}) collective-permute-start(bf16[256,768]{1,0:T(8,128)(2,1)S(1)} %slice.24.refs_0_), channel_id=1, source_target_pairs={{0,24},{8,0},{16,8},{24,16},{1,25},{9,1},{17,9},{25,17},{2,26},{10... | collective-permute-start | bytes 1179656 | tf_op jit(solution)/shard_map/ppermute | solution.py:277
  53.7 18.6 %collective-permute-start.11 = (s16[520,256]{1,0:T(8,128)(2,1)S(1)}, s16[520,256]{1,0:T(8,128)(2,1)S(1)}, u32[]{:S(2)}, u32[]{:S(2)}) collective-permute-start(s16[520,256]{1,0:T(8,128)(2,1)S(1)} %get-tuple-element.26), channel_id=1, source_target_pairs={{0,32},{32,64},{64,96},{96,128},{128,160},{160,192},{192,224},{224... | collective-permute-start | bytes 798728 | tf_op jit(solution)/shard_map/ppermute | solution.py:277
  58.9 13.7 %collective-permute-start.20 = (bf16[128,768]{1,0:T(8,128)(2,1)S(1)}, bf16[128,768]{1,0:T(8,128)(2,1)S(1)}, u32[]{:S(2)}, u32[]{:S(2)}) collective-permute-start(bf16[128,768]{1,0:T(8,128)(2,1)S(1)} %slice.25), channel_id=1, source_target_pairs={{0,8},{8,16},{16,24},{24,0},{1,9},{9,17},{17,25},{25,1},{2,10},{10... | collective-permute-start | bytes 589832 | tf_op jit(solution)/shard_map/ppermute | solution.py:277
  60.0 12.7 %collective-permute-start.21 = (bf16[128,768]{1,0:T(8,128)(2,1)S(1)}, bf16[128,768]{1,0:T(8,128)(2,1)S(1)}, u32[]{:S(2)}, u32[]{:S(2)}) collective-permute-start(bf16[128,768]{1,0:T(8,128)(2,1)S(1)} %slice.26), channel_id=1, source_target_pairs={{0,24},{8,0},{16,8},{24,16},{1,25},{9,1},{17,9},{25,17},{2,26},{10... | collective-permute-start | bytes 589832 | tf_op jit(solution)/shard_map/ppermute | solution.py:277
  62.4 22.1 %collective-permute-start.15 = (s16[520,256]{1,0:T(8,128)(2,1)S(1)}, s16[520,256]{1,0:T(8,128)(2,1)S(1)}, u32[]{:S(2)}, u32[]{:S(2)}) collective-permute-start(s16[520,256]{1,0:T(8,128)(2,1)S(1)} %get-tuple-element.29), channel_id=1, source_target_pairs={{0,224},{32,0},{64,32},{96,64},{128,96},{160,128},{192,160},{224,1... | collective-permute-start | bytes 798728 | tf_op jit(solution)/shard_map/ppermute | solution.py:277
  72.6 12.2 %collective-permute-start.12 = (s16[520,256]{1,0:T(8,128)(2,1)S(1)}, s16[520,256]{1,0:T(8,128)(2,1)S(1)}, u32[]{:S(2)}, u32[]{:S(2)}) collective-permute-start(s16[520,256]{1,0:T(8,128)(2,1)S(1)} %shard_map.55), channel_id=1, source_target_pairs={{0,32},{32,64},{64,96},{96,128},{128,160},{160,192},{192,224},{224... | collective-permute-start | bytes 798728 | tf_op jit(solution)/shard_map/ppermute | solution.py:277
  77.3 9.7 %collective-permute-start.22 = (s16[392,256]{1,0:T(8,128)(2,1)S(1)}, s16[392,256]{1,0:T(8,128)(2,1)S(1)}, u32[]{:S(2)}, u32[]{:S(2)}) collective-permute-start(s16[392,256]{1,0:T(8,128)(2,1)S(1)} %get-tuple-element.33), channel_id=1, source_target_pairs={{0,32},{32,64},{64,96},{96,128},{128,160},{160,192},{192,224},{224... | collective-permute-start | bytes 602120 | tf_op jit(solution)/shard_map/ppermute | solution.py:277
  80.7 8.7 %collective-permute-start.26 = (s16[392,256]{1,0:T(8,128)(2,1)S(1)}, s16[392,256]{1,0:T(8,128)(2,1)S(1)}, u32[]{:S(2)}, u32[]{:S(2)}) collective-permute-start(s16[392,256]{1,0:T(8,128)(2,1)S(1)} %shard_map.65), channel_id=1, source_target_pairs={{0,224},{32,0},{64,32},{96,64},{128,96},{160,128},{192,160},{224,1... | collective-permute-start | bytes 602120 | tf_op jit(solution)/shard_map/ppermute | solution.py:277
  84.7 10.4 %collective-permute-start.16 = (s16[520,256]{1,0:T(8,128)(2,1)S(1)}, s16[520,256]{1,0:T(8,128)(2,1)S(1)}, u32[]{:S(2)}, u32[]{:S(2)}) collective-permute-start(s16[520,256]{1,0:T(8,128)(2,1)S(1)} %shard_map.59), channel_id=1, source_target_pairs={{0,224},{32,0},{64,32},{96,64},{128,96},{160,128},{192,160},{224,1... | collective-permute-start | bytes 798728 | tf_op jit(solution)/shard_map/ppermute | solution.py:277
  85.0 14.1 %collective-permute-start.13 = (s16[520,256]{1,0:T(8,128)(2,1)S(1)}, s16[520,256]{1,0:T(8,128)(2,1)S(1)}, u32[]{:S(2)}, u32[]{:S(2)}) collective-permute-start(s16[520,256]{1,0:T(8,128)(2,1)S(1)} %shard_map.56), channel_id=1, source_target_pairs={{0,32},{32,64},{64,96},{96,128},{128,160},{160,192},{192,224},{224... | collective-permute-start | bytes 798728 | tf_op jit(solution)/shard_map/ppermute | solution.py:277
  87.2 13.3 %collective-permute-start.23 = (s16[392,256]{1,0:T(8,128)(2,1)S(1)}, s16[392,256]{1,0:T(8,128)(2,1)S(1)}, u32[]{:S(2)}, u32[]{:S(2)}) collective-permute-start(s16[392,256]{1,0:T(8,128)(2,1)S(1)} %shard_map.63), channel_id=1, source_target_pairs={{0,32},{32,64},{64,96},{96,128},{128,160},{160,192},{192,224},{224... | collective-permute-start | bytes 602120 | tf_op jit(solution)/shard_map/ppermute | solution.py:277
  89.5 11.2 %collective-permute-start.27 = (s16[392,256]{1,0:T(8,128)(2,1)S(1)}, s16[392,256]{1,0:T(8,128)(2,1)S(1)}, u32[]{:S(2)}, u32[]{:S(2)}) collective-permute-start(s16[392,256]{1,0:T(8,128)(2,1)S(1)} %shard_map.66), channel_id=1, source_target_pairs={{0,224},{32,0},{64,32},{96,64},{128,96},{160,128},{192,160},{224,1... | collective-permute-start | bytes 602120 | tf_op jit(solution)/shard_map/ppermute | solution.py:277
  95.3 13.8 %collective-permute-start.17 = (s16[520,256]{1,0:T(8,128)(2,1)S(1)}, s16[520,256]{1,0:T(8,128)(2,1)S(1)}, u32[]{:S(2)}, u32[]{:S(2)}) collective-permute-start(s16[520,256]{1,0:T(8,128)(2,1)S(1)} %shard_map.60), channel_id=1, source_target_pairs={{0,224},{32,0},{64,32},{96,64},{128,96},{160,128},{192,160},{224,1... | collective-permute-start | bytes 798728 | tf_op jit(solution)/shard_map/ppermute | solution.py:277
  99.2 9.9 %collective-permute-start.14 = (s16[520,256]{1,0:T(8,128)(2,1)S(1)}, s16[520,256]{1,0:T(8,128)(2,1)S(1)}, u32[]{:S(2)}, u32[]{:S(2)}) collective-permute-start(s16[520,256]{1,0:T(8,128)(2,1)S(1)} %shard_map.58), channel_id=1, source_target_pairs={{0,32},{32,64},{64,96},{96,128},{128,160},{160,192},{192,224},{224... | collective-permute-start | bytes 798728 | tf_op jit(solution)/shard_map/ppermute | solution.py:277
  100.7 8.4 %collective-permute-start.24 = (s16[392,256]{1,0:T(8,128)(2,1)S(1)}, s16[392,256]{1,0:T(8,128)(2,1)S(1)}, u32[]{:S(2)}, u32[]{:S(2)}) collective-permute-start(s16[392,256]{1,0:T(8,128)(2,1)S(1)} %shard_map.64), channel_id=1, source_target_pairs={{0,32},{32,64},{64,96},{96,128},{128,160},{160,192},{192,224},{224... | collective-permute-start | bytes 602120 | tf_op jit(solution)/shard_map/ppermute | solution.py:277
  100.9 8.2 %collective-permute-start.28 = (s16[392,256]{1,0:T(8,128)(2,1)S(1)}, s16[392,256]{1,0:T(8,128)(2,1)S(1)}, u32[]{:S(2)}, u32[]{:S(2)}) collective-permute-start(s16[392,256]{1,0:T(8,128)(2,1)S(1)} %shard_map.68), channel_id=1, source_target_pairs={{0,224},{32,0},{64,32},{96,64},{128,96},{160,128},{192,160},{224,1... | collective-permute-start | bytes 602120 | tf_op jit(solution)/shard_map/ppermute | solution.py:277
  (6 other events, 56.0 us)

commit v5 on v4

--- a/solution.py
+++ b/solution.py
@@ -250,14 +250,31 @@
     encode(total, out_ref)
 
 
-def last_kernel(places, *refs):
-    *in_refs, out_ref = refs
-    at = 0
-    for n, i in enumerate(places):
-        up_ref, down_ref, parts_ref = in_refs[3 * n : 3 * n + 3]
-        total = parts_ref[pl.ds(i * LANES, LANES), :] + decode(up_ref) + decode(down_ref)
-        out_ref[:, pl.ds(at, total.shape[1])] = total
-        at += total.shape[1]
+def last_kernel(i, first, up_ref, down_ref, parts_ref, *refs):
+    out_hbm, total_ref, sem = refs[-3:]
+    total_ref[...] = parts_ref[pl.ds(i * LANES, LANES), :] + decode(up_ref) + decode(down_ref)
+    store = pltpu.make_async_copy(total_ref, out_hbm.at[:, pl.ds(first, total_ref.shape[1])], sem)
+    store.start()
+    store.wait()
+
+
+def last(i, first, full, up, down, parts, before):
+    width = parts.shape[1]
+    args = tuple(map(near, (up, down, parts)))
+    aliases = {}
+    if before is not None:
+        args += (before,)
+        aliases = {3: 0}
+    return pl.pallas_call(
+        functools.partial(last_kernel, i, first),
+        out_shape=jax.ShapeDtypeStruct((LANES, full), jnp.float32),
+        in_specs=[VMEM] * 3 + [HBM] * (len(args) - 3),
+        out_specs=HBM,
+        scratch_shapes=[pltpu.VMEM((LANES, width), jnp.float32), pltpu.SemaphoreType.DMA(())],
+        input_output_aliases=aliases,
+        compiler_params=pltpu.CompilerParams(vmem_limit_bytes=GRANT),
+        cost_estimate=cost(10**6, 10**6),
+    )(*args)
 
 
 def call(kernel, out_shape, flops, *args, scratch=()):
@@ -308,7 +325,7 @@
     packs = (own, mine, other)
     wide = pltpu.VMEM((own.shape[0], NX * tokens), own.dtype)
     narrow = pltpu.VMEM((QUARTER, NX * tokens), own.dtype)
-    blocks, places, hi, lo = [], [], None, None
+    grad_weight, first, hi, lo = None, 0, None, None
     for half, ((up_hops, down_hops, units), h) in enumerate(zip(HALVES, gathered)):
         up, down = list(range(7 - up_hops, 7)), list(range(down_hops - 1, -1, -1))
         width = units * LANES
@@ -326,7 +343,7 @@
             hi, lo, ratio = call(kernel, (wide, wide, tile), 4 * 10**6, *packs)
         parts, home = [], {}
         for n, ranges in enumerate(LATER[half]):
-            order = [j for first, stop in ranges for j in range(first, stop)]
+            order = [j for start, stop in ranges for j in range(start, stop)]
             home.update({j: (n, i) for i, j in enumerate(order)})
             shape = pltpu.VMEM((len(order) * LANES, width), jnp.float32)
             parts.append(call(functools.partial(later_kernel, ranges), shape, 10**9, hi, lo, *h))
@@ -339,14 +356,8 @@
                         codes[at] = call(kernel, code, 10**6, codes[at], parts[p])
                     codes[at] = shift(codes[at], "z", NZ, way)
         p, i = home[NZ - 1]
-        blocks += [*codes, parts[p]]
-        places.append(i)
-    grad_weight = call(
-        functools.partial(last_kernel, tuple(places)),
-        jax.ShapeDtypeStruct((LANES, hidden.shape[1]), jnp.float32),
-        10**6,
-        *blocks,
-    )
+        grad_weight = last(i, first, hidden.shape[1], *codes, parts[p], grad_weight)
+        first += width
     return grad_weight, ratio[:2, 0]
 
 

time: 110 us -> 110 us (level)
  starting transfers between devices: 52.5 us -> 51.3 us
    pallas_call x0 -> x2, Pallas kernels: none -> 1.82 us  [last(): pl.pallas_call(functools.partial(last_kernel, i, first), out_shape=jax.Sh...]
    ppermute x29, starting transfers between devices: 52.5 us -> 51.3 us  [shift(): lax.ppermute(value, axis, [(i, (i + by) % size) for i in range(size)])]
    pallas_call x19 -> x18, Pallas kernels: 15.5 us -> 14.3 us  [call(): pl.pallas_call(kernel, out_shape=out_shape, in_specs=[VMEM] * len(args),...]
  transfers between devices with their start and end apart: 29 -> 29, of which waited for: 13 -> 15; matrix products, arithmetic and copies ran while one was open for 1% -> 1% of each run, Pallas kernels for 13% -> 14%
where the time goes in v5:
time: 110 us
  starting transfers between devices  51.3 us (47%)
  waiting for transfers between devices  37.1 us (34%)
  Pallas kernels  19.7 us (18%)
    ppermute x29, starting transfers between devices, shift(): lax.ppermute(value, axis, [(i, (i + by) % size) for i in range(size)])  51.3 us
    ppermute x29, waiting for transfers between devices, shift(): lax.ppermute(value, axis, [(i, (i + by) % size) for i in range(size)])  37.1 us
    pallas_call x18, Pallas kernels, call(): pl.pallas_call(kernel, out_shape=out_shape, in_specs=[VMEM] * len(args),...  14.3 us
    pallas_call x1, Pallas kernels, prepare(): pl.pallas_call(prepare_kernel, out_shape=(pltpu.VMEM(grads.shape, grads.d...  3.61 us
  transfers between devices with their start and end apart: 29, of which 15 were waited for; matrix products, arithmetic and copies ran while one was open for 1% of the time, Pallas kernels for 14%

profile of v5, /device:TPU:8, one launch (start us, length us, event | category | flops | bytes accessed | tf_op | source)
XLA Modules:
  0.0 110.1 jit_solution(11827822916732904574)
XLA Ops:
  0.6 3.6 %shard_map.50 = (bf16[256,4096]{1,0:T(8,128)(2,1)S(1)}, bf16[272,128]{1,0:T(8,128)(2,1)S(1)}, bf16[272,128]{1,0:T(8,128)(2,1)S(1)}, bf16[272,128]{1,0:T(8,128)(2,1)S(1)}, bf16[16,128]{1,0:T(8,128)(2,1)S(1)}) custom-call(s32[2]{0:T(128)} %len_hbm.1, bf16[256,1792]{1,0:T(8,128)(2,1)} %hidden_hbm.1, bf16[256,4096]{1,0:T(8,128)(2,1)} %grads_hbm.1), custom_call_target="tpu_custom_call" | custom-call | flops 400000000 | bytes 5000000 | tf_op jit(solution)/shard_map/pallas_call | solution.py:107
  5.8 2.7 %collective-permute-start.1 = (bf16[272,128]{1,0:T(8,128)(2,1)S(1)}, bf16[272,128]{1,0:T(8,128)(2,1)S(1)}, u32[]{:S(2)}, u32[]{:S(2)}) collective-permute-start(bf16[272,128]{1,0:T(8,128)(2,1)S(1)} %get-tuple-element.21), channel_id=1, source_target_pairs={{0,16},{8,24},{16,0},{24,8},{1,17},{9,25},{17,1},{25,9},{2,18},{10... | collective-permute-start | bytes 208904 | tf_op jit(solution)/shard_map/ppermute | solution.py:294
  15.8 2.1 %collective-permute-start.5 = (bf16[832,128]{1,0:T(8,128)(2,1)S(1)}, bf16[832,128]{1,0:T(8,128)(2,1)S(1)}, u32[]{:S(2)}, u32[]{:S(2)}) collective-permute-start(bf16[832,128]{1,0:T(8,128)(2,1)S(1)} %get-tuple-element.42), channel_id=1, source_target_pairs={{0,6},{2,0},{4,2},{6,4},{1,7},{3,1},{5,3},{7,5},{8,14},{10,8},{12,... | collective-permute-start | bytes 638984 | tf_op jit(solution)/shard_map/ppermute | solution.py:294
  17.9 2.9 %collective-permute-done.3 = bf16[832,128]{1,0:T(8,128)(2,1)S(1)} collective-permute-done((bf16[832,128]{1,0:T(8,128)(2,1)S(1)}, bf16[832,128]{1,0:T(8,128)(2,1)S(1)}, u32[]{:S(2)}, u32[]{:S(2)}) %collective-permute-start.3) | collective-permute-done | bytes 213024 | tf_op jit(solution)/shard_map/ppermute | solution.py:294
  20.8 3.2 %collective-permute-done.4 = bf16[832,128]{1,0:T(8,128)(2,1)S(1)} collective-permute-done((bf16[832,128]{1,0:T(8,128)(2,1)S(1)}, bf16[832,128]{1,0:T(8,128)(2,1)S(1)}, u32[]{:S(2)}, u32[]{:S(2)}) %collective-permute-start.4) | collective-permute-done | bytes 213024 | tf_op jit(solution)/shard_map/ppermute | solution.py:294
  25.9 3.2 %collective-permute-start.8 = (bf16[256,1024]{1,0:T(8,128)(2,1)S(1)}, bf16[256,1024]{1,0:T(8,128)(2,1)S(1)}, u32[]{:S(2)}, u32[]{:S(2)}) collective-permute-start(bf16[256,1024]{1,0:T(8,128)(2,1)S(1)} %slice.22.refs_0_), channel_id=1, source_target_pairs={{0,24},{8,0},{16,8},{24,16},{1,25},{9,1},{17,9},{25,17},{2,26},{10... | collective-permute-start | bytes 1572872 | tf_op jit(solution)/shard_map/ppermute | solution.py:294
  29.1 12.3 %collective-permute-done.7.refs_1_ = bf16[256,1024]{1,0:T(8,128)(2,1)S(1)} collective-permute-done((bf16[256,1024]{1,0:T(8,128)(2,1)S(1)}, bf16[256,1024]{1,0:T(8,128)(2,1)S(1)}, u32[]{:S(2)}, u32[]{:S(2)}) %collective-permute-start.7) | collective-permute-done | bytes 524320 | tf_op jit(solution)/shard_map/ppermute | solution.py:294
  42.0 2.8 %collective-permute-start.21 = (bf16[128,1024]{1,0:T(8,128)(2,1)S(1)}, bf16[128,1024]{1,0:T(8,128)(2,1)S(1)}, u32[]{:S(2)}, u32[]{:S(2)}) collective-permute-start(bf16[128,1024]{1,0:T(8,128)(2,1)S(1)} %slice.26), channel_id=1, source_target_pairs={{0,24},{8,0},{16,8},{24,16},{1,25},{9,1},{17,9},{25,17},{2,26},{10... | collective-permute-start | bytes 786440 | tf_op jit(solution)/shard_map/ppermute | solution.py:294
  47.2 4.6 %collective-permute-done.20.refs_2_ = bf16[128,1024]{1,0:T(8,128)(2,1)S(1)} collective-permute-done((bf16[128,1024]{1,0:T(8,128)(2,1)S(1)}, bf16[128,1024]{1,0:T(8,128)(2,1)S(1)}, u32[]{:S(2)}, u32[]{:S(2)}) %collective-permute-start.20) | collective-permute-done | bytes 262176 | tf_op jit(solution)/shard_map/ppermute | solution.py:294
  51.8 1.9 %shard_map.61 = (s16[520,256]{1,0:T(8,128)(2,1)S(1)}, s16[520,256]{1,0:T(8,128)(2,1)S(1)}) custom-call(bf16[1024,256]{1,0:T(8,128)(2,1)S(1)} %shard_map.51.own, bf16[3328,128]{1,0:T(8,128)(2,1)S(1)} %constant_dynamic-update-slice_fusion.4.mine, bf16[3328,128]{1,0:T(8,128)(2,1)S(1)} %collective-permute-done.6.other, bf16[256,1024]{1,0:T(8,128)(2,1)S(1)} %slice.22.refs_0_, ...), custom_call_target="tpu_custom_call" | custom-call | flops 1000000000 | bytes 1000000 | tf_op jit(solution)/shard_map/pallas_call | solution.py:282
  53.7 2.0 %collective-permute-start.22 = (s16[520,256]{1,0:T(8,128)(2,1)S(1)}, s16[520,256]{1,0:T(8,128)(2,1)S(1)}, u32[]{:S(2)}, u32[]{:S(2)}) collective-permute-start(s16[520,256]{1,0:T(8,128)(2,1)S(1)} %get-tuple-element.33), channel_id=1, source_target_pairs={{0,32},{32,64},{64,96},{96,128},{128,160},{160,192},{192,224},{224... | collective-permute-start | bytes 798728 | tf_op jit(solution)/shard_map/ppermute | solution.py:294
  55.7 2.6 %collective-permute-done.10.refs_4_ = bf16[256,768]{1,0:T(8,128)(2,1)S(1)} collective-permute-done((bf16[256,768]{1,0:T(8,128)(2,1)S(1)}, bf16[256,768]{1,0:T(8,128)(2,1)S(1)}, u32[]{:S(2)}, u32[]{:S(2)}) %collective-permute-start.10) | collective-permute-done | bytes 393248 | tf_op jit(solution)/shard_map/ppermute | solution.py:294
  60.0 2.3 %collective-permute-start.12 = (bf16[128,768]{1,0:T(8,128)(2,1)S(1)}, bf16[128,768]{1,0:T(8,128)(2,1)S(1)}, u32[]{:S(2)}, u32[]{:S(2)}) collective-permute-start(bf16[128,768]{1,0:T(8,128)(2,1)S(1)} %slice.24), channel_id=1, source_target_pairs={{0,24},{8,0},{16,8},{24,16},{1,25},{9,1},{17,9},{25,17},{2,26},{10... | collective-permute-start | bytes 589832 | tf_op jit(solution)/shard_map/ppermute | solution.py:294
  62.4 5.9 %collective-permute-start.26 = (s16[520,256]{1,0:T(8,128)(2,1)S(1)}, s16[520,256]{1,0:T(8,128)(2,1)S(1)}, u32[]{:S(2)}, u32[]{:S(2)}) collective-permute-start(s16[520,256]{1,0:T(8,128)(2,1)S(1)} %get-tuple-element.34), channel_id=1, source_target_pairs={{0,224},{32,0},{64,32},{96,64},{128,96},{160,128},{192,160},{224,1... | collective-permute-start | bytes 798728 | tf_op jit(solution)/shard_map/ppermute | solution.py:294
  69.5 2.9 %shard_map.62.parts_ref = f32[512,1024]{1,0:T(8,128)S(1)} custom-call(bf16[1024,1024]{1,0:T(8,128)(2,1)S(1)} %get-tuple-element.24.hi_ref, bf16[1024,1024]{1,0:T(8,128)(2,1)S(1)} %get-tuple-element.25.lo_ref, bf16[256,1024]{1,0:T(8,128)(2,1)S(1)} %slice.22.refs_0_, bf16[256,1024]{1,0:T(8,128)(2,1)S(1)} %collective-permute-done.7.refs_1_, ...), custom_call_target="tpu_custom_call" | custom-call | flops 1000000000 | bytes 1000000 | tf_op jit(solution)/shard_map/pallas_call | solution.py:282
  74.0 3.3 %collective-permute-start.16 = (s16[392,256]{1,0:T(8,128)(2,1)S(1)}, s16[392,256]{1,0:T(8,128)(2,1)S(1)}, u32[]{:S(2)}, u32[]{:S(2)}) collective-permute-start(s16[392,256]{1,0:T(8,128)(2,1)S(1)} %get-tuple-element.31), channel_id=1, source_target_pairs={{0,224},{32,0},{64,32},{96,64},{128,96},{160,128},{192,160},{224,1... | collective-permute-start | bytes 602120 | tf_op jit(solution)/shard_map/ppermute | solution.py:294
  77.3 2.2 %shard_map.54.parts_ref = f32[512,768]{1,0:T(8,128)S(1)} custom-call(bf16[1024,1024]{1,0:T(8,128)(2,1)S(1)} %get-tuple-element.24.hi_ref, bf16[1024,1024]{1,0:T(8,128)(2,1)S(1)} %get-tuple-element.25.lo_ref, bf16[256,768]{1,0:T(8,128)(2,1)S(1)} %slice.21.refs_0_, bf16[256,768]{1,0:T(8,128)(2,1)S(1)} %collective-permute-done.9.refs_1_, ...), custom_call_target="tpu_custom_call" | custom-call | flops 1000000000 | bytes 1000000 | tf_op jit(solution)/shard_map/pallas_call | solution.py:282
  80.7 3.8 %collective-permute-start.17 = (s16[392,256]{1,0:T(8,128)(2,1)S(1)}, s16[392,256]{1,0:T(8,128)(2,1)S(1)}, u32[]{:S(2)}, u32[]{:S(2)}) collective-permute-start(s16[392,256]{1,0:T(8,128)(2,1)S(1)} %shard_map.57), channel_id=1, source_target_pairs={{0,224},{32,0},{64,32},{96,64},{128,96},{160,128},{192,160},{224,1... | collective-permute-start | bytes 602120 | tf_op jit(solution)/shard_map/ppermute | solution.py:294
  84.9 2.1 %collective-permute-start.24 = (s16[520,256]{1,0:T(8,128)(2,1)S(1)}, s16[520,256]{1,0:T(8,128)(2,1)S(1)}, u32[]{:S(2)}, u32[]{:S(2)}) collective-permute-start(s16[520,256]{1,0:T(8,128)(2,1)S(1)} %shard_map.64), channel_id=1, source_target_pairs={{0,32},{32,64},{64,96},{96,128},{128,160},{160,192},{192,224},{224... | collective-permute-start | bytes 798728 | tf_op jit(solution)/shard_map/ppermute | solution.py:294
  87.3 2.1 %collective-permute-done.17.recv_ref = s16[392,256]{1,0:T(8,128)(2,1)S(1)} collective-permute-done((s16[392,256]{1,0:T(8,128)(2,1)S(1)}, s16[392,256]{1,0:T(8,128)(2,1)S(1)}, u32[]{:S(2)}, u32[]{:S(2)}) %collective-permute-start.17) | collective-permute-done | bytes 200736 | tf_op jit(solution)/shard_map/ppermute | solution.py:294
  89.5 3.8 %collective-permute-start.18 = (s16[392,256]{1,0:T(8,128)(2,1)S(1)}, s16[392,256]{1,0:T(8,128)(2,1)S(1)}, u32[]{:S(2)}, u32[]{:S(2)}) collective-permute-start(s16[392,256]{1,0:T(8,128)(2,1)S(1)} %shard_map.58), channel_id=1, source_target_pairs={{0,224},{32,0},{64,32},{96,64},{128,96},{160,128},{192,160},{224,1... | collective-permute-start | bytes 602120 | tf_op jit(solution)/shard_map/ppermute | solution.py:294
  95.3 3.8 %collective-permute-start.28 = (s16[520,256]{1,0:T(8,128)(2,1)S(1)}, s16[520,256]{1,0:T(8,128)(2,1)S(1)}, u32[]{:S(2)}, u32[]{:S(2)}) collective-permute-start(s16[520,256]{1,0:T(8,128)(2,1)S(1)} %shard_map.68), channel_id=1, source_target_pairs={{0,224},{32,0},{64,32},{96,64},{128,96},{160,128},{192,160},{224,1... | collective-permute-start | bytes 798728 | tf_op jit(solution)/shard_map/ppermute | solution.py:294
  100.9 3.3 %collective-permute-start.19 = (s16[392,256]{1,0:T(8,128)(2,1)S(1)}, s16[392,256]{1,0:T(8,128)(2,1)S(1)}, u32[]{:S(2)}, u32[]{:S(2)}) collective-permute-start(s16[392,256]{1,0:T(8,128)(2,1)S(1)} %shard_map.60), channel_id=1, source_target_pairs={{0,224},{32,0},{64,32},{96,64},{128,96},{160,128},{192,160},{224,1... | collective-permute-start | bytes 602120 | tf_op jit(solution)/shard_map/ppermute | solution.py:294
  104.9 2.1 %collective-permute-done.25.up_ref = s16[520,256]{1,0:T(8,128)(2,1)S(1)} collective-permute-done((s16[520,256]{1,0:T(8,128)(2,1)S(1)}, s16[520,256]{1,0:T(8,128)(2,1)S(1)}, u32[]{:S(2)}, u32[]{:S(2)}) %collective-permute-start.25) | collective-permute-done | bytes 266272 | tf_op jit(solution)/shard_map/ppermute | solution.py:294
  (71 shorter events, 28.0 us)
Async XLA Ops:
  12.9 7.9 %collective-permute-start.3 = (bf16[832,128]{1,0:T(8,128)(2,1)S(1)}, bf16[832,128]{1,0:T(8,128)(2,1)S(1)}, u32[]{:S(2)}, u32[]{:S(2)}) collective-permute-start(bf16[832,128]{1,0:T(8,128)(2,1)S(1)} %get-tuple-element.42), channel_id=1, source_target_pairs={{0,2},{2,4},{4,6},{6,0},{1,3},{3,5},{5,7},{7,1},{8,10},{10,12},{12... | collective-permute-start | bytes 638984 | tf_op jit(solution)/shard_map/ppermute | solution.py:294
  14.6 9.4 %collective-permute-start.4 = (bf16[832,128]{1,0:T(8,128)(2,1)S(1)}, bf16[832,128]{1,0:T(8,128)(2,1)S(1)}, u32[]{:S(2)}, u32[]{:S(2)}) collective-permute-start(bf16[832,128]{1,0:T(8,128)(2,1)S(1)} %get-tuple-element.42), channel_id=1, source_target_pairs={{0,4},{2,6},{4,0},{6,2},{1,5},{3,7},{5,1},{7,3},{8,12},{10,14},{12... | collective-permute-start | bytes 638984 | tf_op jit(solution)/shard_map/ppermute | solution.py:294
  15.8 9.7 %collective-permute-start.5 = (bf16[832,128]{1,0:T(8,128)(2,1)S(1)}, bf16[832,128]{1,0:T(8,128)(2,1)S(1)}, u32[]{:S(2)}, u32[]{:S(2)}) collective-permute-start(bf16[832,128]{1,0:T(8,128)(2,1)S(1)} %get-tuple-element.42), channel_id=1, source_target_pairs={{0,6},{2,0},{4,2},{6,4},{1,7},{3,1},{5,3},{7,5},{8,14},{10,8},{12,... | collective-permute-start | bytes 638984 | tf_op jit(solution)/shard_map/ppermute | solution.py:294
  25.6 26.3 %collective-permute-start.6 = (bf16[3328,128]{1,0:T(8,128)(2,1)S(1)}, bf16[3328,128]{1,0:T(8,128)(2,1)S(1)}, u32[]{:S(2)}, u32[]{:S(2)}) collective-permute-start(bf16[3328,128]{1,0:T(8,128)(2,1)S(1)} %constant_dynamic-update-slice_fusion.4.mine), channel_id=1, source_target_pairs={{0,1},{1,0},{2,3},{3,2},{4,5},{5,4},{6,7},{7,6},{8,9},{9,8},{10,11... | collective-permute-start | bytes 2555912 | tf_op jit(solution)/shard_map/ppermute | solution.py:294
  25.7 15.6 %collective-permute-start.7 = (bf16[256,1024]{1,0:T(8,128)(2,1)S(1)}, bf16[256,1024]{1,0:T(8,128)(2,1)S(1)}, u32[]{:S(2)}, u32[]{:S(2)}) collective-permute-start(bf16[256,1024]{1,0:T(8,128)(2,1)S(1)} %slice.22.refs_0_), channel_id=1, source_target_pairs={{0,8},{8,16},{16,24},{24,0},{1,9},{9,17},{17,25},{25,1},{2,10},{10... | collective-permute-start | bytes 1572872 | tf_op jit(solution)/shard_map/ppermute | solution.py:294
  25.9 15.5 %collective-permute-start.8 = (bf16[256,1024]{1,0:T(8,128)(2,1)S(1)}, bf16[256,1024]{1,0:T(8,128)(2,1)S(1)}, u32[]{:S(2)}, u32[]{:S(2)}) collective-permute-start(bf16[256,1024]{1,0:T(8,128)(2,1)S(1)} %slice.22.refs_0_), channel_id=1, source_target_pairs={{0,24},{8,0},{16,8},{24,16},{1,25},{9,1},{17,9},{25,17},{2,26},{10... | collective-permute-start | bytes 1572872 | tf_op jit(solution)/shard_map/ppermute | solution.py:294
  41.4 10.5 %collective-permute-start.20 = (bf16[128,1024]{1,0:T(8,128)(2,1)S(1)}, bf16[128,1024]{1,0:T(8,128)(2,1)S(1)}, u32[]{:S(2)}, u32[]{:S(2)}) collective-permute-start(bf16[128,1024]{1,0:T(8,128)(2,1)S(1)} %slice.25), channel_id=1, source_target_pairs={{0,8},{8,16},{16,24},{24,0},{1,9},{9,17},{17,25},{25,1},{2,10},{10... | collective-permute-start | bytes 786440 | tf_op jit(solution)/shard_map/ppermute | solution.py:294
  42.0 9.8 %collective-permute-start.21 = (bf16[128,1024]{1,0:T(8,128)(2,1)S(1)}, bf16[128,1024]{1,0:T(8,128)(2,1)S(1)}, u32[]{:S(2)}, u32[]{:S(2)}) collective-permute-start(bf16[128,1024]{1,0:T(8,128)(2,1)S(1)} %slice.26), channel_id=1, source_target_pairs={{0,24},{8,0},{16,8},{24,16},{1,25},{9,1},{17,9},{25,17},{2,26},{10... | collective-permute-start | bytes 786440 | tf_op jit(solution)/shard_map/ppermute | solution.py:294
  44.8 13.5 %collective-permute-start.10 = (bf16[256,768]{1,0:T(8,128)(2,1)S(1)}, bf16[256,768]{1,0:T(8,128)(2,1)S(1)}, u32[]{:S(2)}, u32[]{:S(2)}) collective-permute-start(bf16[256,768]{1,0:T(8,128)(2,1)S(1)} %slice.21.refs_0_), channel_id=1, source_target_pairs={{0,24},{8,0},{16,8},{24,16},{1,25},{9,1},{17,9},{25,17},{2,26},{10... | collective-permute-start | bytes 1179656 | tf_op jit(solution)/shard_map/ppermute | solution.py:294
  46.6 12.3 %collective-permute-start.9 = (bf16[256,768]{1,0:T(8,128)(2,1)S(1)}, bf16[256,768]{1,0:T(8,128)(2,1)S(1)}, u32[]{:S(2)}, u32[]{:S(2)}) collective-permute-start(bf16[256,768]{1,0:T(8,128)(2,1)S(1)} %slice.21.refs_0_), channel_id=1, source_target_pairs={{0,8},{8,16},{16,24},{24,0},{1,9},{9,17},{17,25},{25,1},{2,10},{10... | collective-permute-start | bytes 1179656 | tf_op jit(solution)/shard_map/ppermute | solution.py:294
  53.7 18.6 %collective-permute-start.22 = (s16[520,256]{1,0:T(8,128)(2,1)S(1)}, s16[520,256]{1,0:T(8,128)(2,1)S(1)}, u32[]{:S(2)}, u32[]{:S(2)}) collective-permute-start(s16[520,256]{1,0:T(8,128)(2,1)S(1)} %get-tuple-element.33), channel_id=1, source_target_pairs={{0,32},{32,64},{64,96},{96,128},{128,160},{160,192},{192,224},{224... | collective-permute-start | bytes 798728 | tf_op jit(solution)/shard_map/ppermute | solution.py:294
  58.9 13.7 %collective-permute-start.11 = (bf16[128,768]{1,0:T(8,128)(2,1)S(1)}, bf16[128,768]{1,0:T(8,128)(2,1)S(1)}, u32[]{:S(2)}, u32[]{:S(2)}) collective-permute-start(bf16[128,768]{1,0:T(8,128)(2,1)S(1)} %slice.23), channel_id=1, source_target_pairs={{0,8},{8,16},{16,24},{24,0},{1,9},{9,17},{17,25},{25,1},{2,10},{10... | collective-permute-start | bytes 589832 | tf_op jit(solution)/shard_map/ppermute | solution.py:294
  60.0 12.7 %collective-permute-start.12 = (bf16[128,768]{1,0:T(8,128)(2,1)S(1)}, bf16[128,768]{1,0:T(8,128)(2,1)S(1)}, u32[]{:S(2)}, u32[]{:S(2)}) collective-permute-start(bf16[128,768]{1,0:T(8,128)(2,1)S(1)} %slice.24), channel_id=1, source_target_pairs={{0,24},{8,0},{16,8},{24,16},{1,25},{9,1},{17,9},{25,17},{2,26},{10... | collective-permute-start | bytes 589832 | tf_op jit(solution)/shard_map/ppermute | solution.py:294
  62.4 22.1 %collective-permute-start.26 = (s16[520,256]{1,0:T(8,128)(2,1)S(1)}, s16[520,256]{1,0:T(8,128)(2,1)S(1)}, u32[]{:S(2)}, u32[]{:S(2)}) collective-permute-start(s16[520,256]{1,0:T(8,128)(2,1)S(1)} %get-tuple-element.34), channel_id=1, source_target_pairs={{0,224},{32,0},{64,32},{96,64},{128,96},{160,128},{192,160},{224,1... | collective-permute-start | bytes 798728 | tf_op jit(solution)/shard_map/ppermute | solution.py:294
  72.6 12.2 %collective-permute-start.23 = (s16[520,256]{1,0:T(8,128)(2,1)S(1)}, s16[520,256]{1,0:T(8,128)(2,1)S(1)}, u32[]{:S(2)}, u32[]{:S(2)}) collective-permute-start(s16[520,256]{1,0:T(8,128)(2,1)S(1)} %shard_map.63), channel_id=1, source_target_pairs={{0,32},{32,64},{64,96},{96,128},{128,160},{160,192},{192,224},{224... | collective-permute-start | bytes 798728 | tf_op jit(solution)/shard_map/ppermute | solution.py:294
  77.3 9.7 %collective-permute-start.13 = (s16[392,256]{1,0:T(8,128)(2,1)S(1)}, s16[392,256]{1,0:T(8,128)(2,1)S(1)}, u32[]{:S(2)}, u32[]{:S(2)}) collective-permute-start(s16[392,256]{1,0:T(8,128)(2,1)S(1)} %get-tuple-element.30), channel_id=1, source_target_pairs={{0,32},{32,64},{64,96},{96,128},{128,160},{160,192},{192,224},{224... | collective-permute-start | bytes 602120 | tf_op jit(solution)/shard_map/ppermute | solution.py:294
  80.7 8.7 %collective-permute-start.17 = (s16[392,256]{1,0:T(8,128)(2,1)S(1)}, s16[392,256]{1,0:T(8,128)(2,1)S(1)}, u32[]{:S(2)}, u32[]{:S(2)}) collective-permute-start(s16[392,256]{1,0:T(8,128)(2,1)S(1)} %shard_map.57), channel_id=1, source_target_pairs={{0,224},{32,0},{64,32},{96,64},{128,96},{160,128},{192,160},{224,1... | collective-permute-start | bytes 602120 | tf_op jit(solution)/shard_map/ppermute | solution.py:294
  84.6 10.4 %collective-permute-start.27 = (s16[520,256]{1,0:T(8,128)(2,1)S(1)}, s16[520,256]{1,0:T(8,128)(2,1)S(1)}, u32[]{:S(2)}, u32[]{:S(2)}) collective-permute-start(s16[520,256]{1,0:T(8,128)(2,1)S(1)} %shard_map.67), channel_id=1, source_target_pairs={{0,224},{32,0},{64,32},{96,64},{128,96},{160,128},{192,160},{224,1... | collective-permute-start | bytes 798728 | tf_op jit(solution)/shard_map/ppermute | solution.py:294
  84.9 14.1 %collective-permute-start.24 = (s16[520,256]{1,0:T(8,128)(2,1)S(1)}, s16[520,256]{1,0:T(8,128)(2,1)S(1)}, u32[]{:S(2)}, u32[]{:S(2)}) collective-permute-start(s16[520,256]{1,0:T(8,128)(2,1)S(1)} %shard_map.64), channel_id=1, source_target_pairs={{0,32},{32,64},{64,96},{96,128},{128,160},{160,192},{192,224},{224... | collective-permute-start | bytes 798728 | tf_op jit(solution)/shard_map/ppermute | solution.py:294
  87.2 13.3 %collective-permute-start.14 = (s16[392,256]{1,0:T(8,128)(2,1)S(1)}, s16[392,256]{1,0:T(8,128)(2,1)S(1)}, u32[]{:S(2)}, u32[]{:S(2)}) collective-permute-start(s16[392,256]{1,0:T(8,128)(2,1)S(1)} %shard_map.55), channel_id=1, source_target_pairs={{0,32},{32,64},{64,96},{96,128},{128,160},{160,192},{192,224},{224... | collective-permute-start | bytes 602120 | tf_op jit(solution)/shard_map/ppermute | solution.py:294
  89.5 11.3 %collective-permute-start.18 = (s16[392,256]{1,0:T(8,128)(2,1)S(1)}, s16[392,256]{1,0:T(8,128)(2,1)S(1)}, u32[]{:S(2)}, u32[]{:S(2)}) collective-permute-start(s16[392,256]{1,0:T(8,128)(2,1)S(1)} %shard_map.58), channel_id=1, source_target_pairs={{0,224},{32,0},{64,32},{96,64},{128,96},{160,128},{192,160},{224,1... | collective-permute-start | bytes 602120 | tf_op jit(solution)/shard_map/ppermute | solution.py:294
  95.3 9.6 %collective-permute-start.28 = (s16[520,256]{1,0:T(8,128)(2,1)S(1)}, s16[520,256]{1,0:T(8,128)(2,1)S(1)}, u32[]{:S(2)}, u32[]{:S(2)}) collective-permute-start(s16[520,256]{1,0:T(8,128)(2,1)S(1)} %shard_map.68), channel_id=1, source_target_pairs={{0,224},{32,0},{64,32},{96,64},{128,96},{160,128},{192,160},{224,1... | collective-permute-start | bytes 798728 | tf_op jit(solution)/shard_map/ppermute | solution.py:294
  100.7 8.4 %collective-permute-start.15 = (s16[392,256]{1,0:T(8,128)(2,1)S(1)}, s16[392,256]{1,0:T(8,128)(2,1)S(1)}, u32[]{:S(2)}, u32[]{:S(2)}) collective-permute-start(s16[392,256]{1,0:T(8,128)(2,1)S(1)} %shard_map.56), channel_id=1, source_target_pairs={{0,32},{32,64},{64,96},{96,128},{128,160},{160,192},{192,224},{224... | collective-permute-start | bytes 602120 | tf_op jit(solution)/shard_map/ppermute | solution.py:294
  100.9 8.2 %collective-permute-start.19 = (s16[392,256]{1,0:T(8,128)(2,1)S(1)}, s16[392,256]{1,0:T(8,128)(2,1)S(1)}, u32[]{:S(2)}, u32[]{:S(2)}) collective-permute-start(s16[392,256]{1,0:T(8,128)(2,1)S(1)} %shard_map.60), channel_id=1, source_target_pairs={{0,224},{32,0},{64,32},{96,64},{128,96},{160,128},{192,160},{224,1... | collective-permute-start | bytes 602120 | tf_op jit(solution)/shard_map/ppermute | solution.py:294
  (6 other events, 55.8 us)

commit v6 on v5

--- a/solution.py
+++ b/solution.py
@@ -17,7 +17,7 @@
 NOTE = 16
 PIECE = QUARTER + NOTE
 BUNDLE = (NX - 1) * PIECE + NOTE
-HALVES = ((4, 3, 8), (3, 4, 6))
+HALVES = ((4, 3, (4, 4)), (3, 4, (6,)))
 LATER = ((((0, 2), (4, 6)), ((6, 8),)), (((1, 3), (5, 7)), ((0, 1), (7, 8))))
 LIMIT = 32767.0
 MANT = 8192.0
@@ -207,66 +207,74 @@
     out_ref[pl.ds(groups * LANES, EXTRA), :] = tail.astype(jnp.int32).astype(jnp.int16)
 
 
-def product(rows, hi_ref, lo_ref, h_refs):
+def product(rows, hi_ref, lo_ref, h_refs, cols=slice(None)):
     total, token = None, 0
     for h in h_refs:
         size = h.shape[0]
         for g in (hi_ref, lo_ref):
-            term = jnp.dot(g[rows, pl.ds(token, size)], h[...], preferred_element_type=jnp.float32)
+            term = jnp.dot(g[rows, pl.ds(token, size)], h[:, cols], preferred_element_type=jnp.float32)
             total = term if total is None else total + term
         token += size
     return total
 
 
-def encode_pair(low, up_j, down_j, hi_ref, lo_ref, rows, h_refs, up_ref, down_ref):
+def encode_pair(low, up_j, down_j, hi_ref, lo_ref, rows, h_refs, code_refs):
     both = product(rows, hi_ref, lo_ref, h_refs)
-    for j, out_ref in ((up_j, up_ref), (down_j, down_ref)):
-        encode(both[(j - low) * LANES : (j - low + 1) * LANES], out_ref)
+    at = 0
+    for n, out_ref in enumerate(code_refs):
+        j = (up_j, down_j)[n % 2]
+        width = out_ref.shape[0] // LANES * GROUP
+        encode(both[(j - low) * LANES : (j - low + 1) * LANES, at : at + width], out_ref)
+        at += width * (n % 2)
 
 
 def opening_kernel(clip_norm, factor, own, mine, other, *refs):
-    *h_refs, up_ref, down_ref, hi_ref, lo_ref = refs
+    *refs, hi_ref, lo_ref = refs
     weighted(clip_norm, factor, own, mine, other, (1,), hi_ref, lo_ref)
-    encode_pair(2, 3, 2, hi_ref, lo_ref, slice(None), h_refs, up_ref, down_ref)
+    encode_pair(2, 3, 2, hi_ref, lo_ref, slice(None), refs[:5], refs[5:])
 
 
 def first_kernel(up_j, down_j, hi_ref, lo_ref, *refs):
-    *h_refs, up_ref, down_ref = refs
     low = min(up_j, down_j)
-    encode_pair(low, up_j, down_j, hi_ref, lo_ref, pl.ds(low * LANES, 2 * LANES), h_refs, up_ref, down_ref)
+    encode_pair(low, up_j, down_j, hi_ref, lo_ref, pl.ds(low * LANES, 2 * LANES), refs[:5], refs[5:])
 
 
 def later_kernel(ranges, hi_ref, lo_ref, *refs):
     *h_refs, out_ref = refs
-    at = 0
-    for first, stop in ranges:
-        size = (stop - first) * LANES
-        out_ref[pl.ds(at, size), :] = product(pl.ds(first * LANES, size), hi_ref, lo_ref, h_refs)
-        at += size
-
-
-def hop_kernel(i, recv_ref, parts_ref, out_ref):
-    total = parts_ref[pl.ds(i * LANES, LANES), :] + decode(recv_ref)
-    encode(total, out_ref)
-
-
-def last_kernel(i, first, up_ref, down_ref, parts_ref, *refs):
+
+    @pl.loop(0, out_ref.shape[1] // GROUP)
+    def _(n):
+        cols = pl.ds(pl.multiple_of(n * GROUP, GROUP), GROUP)
+        at = 0
+        for first, stop in ranges:
+            size = (stop - first) * LANES
+            rows = pl.ds(first * LANES, size)
+            out_ref[pl.ds(at, size), cols] = product(rows, hi_ref, lo_ref, h_refs, cols)
+            at += size
+
+
+def hop_kernel(i, at, recv_ref, parts_ref, out_ref):
+    got = decode(recv_ref)
+    encode(parts_ref[pl.ds(i * LANES, LANES), pl.ds(at, got.shape[1])] + got, out_ref)
+
+
+def last_kernel(i, at, first, up_ref, down_ref, parts_ref, *refs):
     out_hbm, total_ref, sem = refs[-3:]
-    total_ref[...] = parts_ref[pl.ds(i * LANES, LANES), :] + decode(up_ref) + decode(down_ref)
+    part = parts_ref[pl.ds(i * LANES, LANES), pl.ds(at, total_ref.shape[1])]
+    total_ref[...] = part + decode(up_ref) + decode(down_ref)
     store = pltpu.make_async_copy(total_ref, out_hbm.at[:, pl.ds(first, total_ref.shape[1])], sem)
     store.start()
     store.wait()
 
 
-def last(i, first, full, up, down, parts, before):
-    width = parts.shape[1]
+def last(i, at, first, width, full, up, down, parts, before):
     args = tuple(map(near, (up, down, parts)))
     aliases = {}
     if before is not None:
         args += (before,)
         aliases = {3: 0}
     return pl.pallas_call(
-        functools.partial(last_kernel, i, first),
+        functools.partial(last_kernel, i, at, first),
         out_shape=jax.ShapeDtypeStruct((LANES, full), jnp.float32),
         in_specs=[VMEM] * 3 + [HBM] * (len(args) - 3),
         out_specs=HBM,
@@ -301,8 +309,8 @@
     model_dim = grads.shape[1]
     gathered, ready, at = [], None, 0
     for _, _, units in HALVES:
-        own = lax.slice_in_dim(hidden, at, at + units * LANES, axis=1)
-        at += units * LANES
+        own = lax.slice_in_dim(hidden, at, at + sum(units) * LANES, axis=1)
+        at += sum(units) * LANES
         if ready is not None:
             own, ready = lax.optimization_barrier((own, ready))
         below = shift(own, "x", NX, 1)
@@ -327,15 +335,16 @@
     narrow = pltpu.VMEM((QUARTER, NX * tokens), own.dtype)
     grad_weight, first, hi, lo = None, 0, None, None
     for half, ((up_hops, down_hops, units), h) in enumerate(zip(HALVES, gathered)):
-        up, down = list(range(7 - up_hops, 7)), list(range(down_hops - 1, -1, -1))
-        width = units * LANES
-        code = pltpu.VMEM((width // GROUP * LANES + EXTRA, GROUP), jnp.int16)
+        ways = ((1, list(range(7 - up_hops, 7))), (-1, list(range(down_hops - 1, -1, -1))))
+        up_j, down_j = ways[0][1][0], ways[1][1][0]
+        widths = [u * LANES for u in units]
+        shapes = [pltpu.VMEM((w // GROUP * LANES + EXTRA, GROUP), jnp.int16) for w in widths]
+        pairs = tuple(c for c in shapes for _ in range(2))
         if half == 0:
             kernel = functools.partial(opening_kernel, clip_norm, factor)
-            codes = call(kernel, (code, code), 10**9, *packs, *h, scratch=[narrow, narrow])
+            codes = call(kernel, pairs, 10**9, *packs, *h, scratch=[narrow, narrow])
         else:
-            kernel = functools.partial(first_kernel, up[0], down[0])
-            codes = call(kernel, (code, code), 10**9, hi, lo, *h)
+            codes = call(functools.partial(first_kernel, up_j, down_j), pairs, 10**9, hi, lo, *h)
         codes = list(codes)
         if half == 0:
             kernel = functools.partial(scale_kernel, clip_norm, factor)
@@ -345,19 +354,24 @@
         for n, ranges in enumerate(LATER[half]):
             order = [j for start, stop in ranges for j in range(start, stop)]
             home.update({j: (n, i) for i, j in enumerate(order)})
-            shape = pltpu.VMEM((len(order) * LANES, width), jnp.float32)
+            shape = pltpu.VMEM((len(order) * LANES, sum(widths)), jnp.float32)
             parts.append(call(functools.partial(later_kernel, ranges), shape, 10**9, hi, lo, *h))
         for n in range(max(up_hops, down_hops)):
-            for at, (way, order) in enumerate(((1, up), (-1, down))):
-                if n < len(order):
-                    if n:
-                        p, i = home[order[n]]
-                        kernel = functools.partial(hop_kernel, i)
-                        codes[at] = call(kernel, code, 10**6, codes[at], parts[p])
-                    codes[at] = shift(codes[at], "z", NZ, way)
+            for stream, code in enumerate(shapes):
+                for side, (way, order) in enumerate(ways):
+                    if n < len(order):
+                        at = 2 * stream + side
+                        if n:
+                            p, i = home[order[n]]
+                            kernel = functools.partial(hop_kernel, i, sum(widths[:stream]))
+                            codes[at] = call(kernel, code, 10**6, codes[at], parts[p])
+                        codes[at] = shift(codes[at], "z", NZ, way)
         p, i = home[NZ - 1]
-        grad_weight = last(i, first, hidden.shape[1], *codes, parts[p], grad_weight)
-        first += width
+        for stream, width in enumerate(widths):
+            at = sum(widths[:stream])
+            pair = codes[2 * stream : 2 * stream + 2]
+            grad_weight = last(i, at, first + at, width, hidden.shape[1], *pair, parts[p], grad_weight)
+        first += sum(widths)
     return grad_weight, ratio[:2, 0]
 
 

time: 110 us -> 109 us (level)
  the two profiles are of different devices: /device:TPU:8 before, /device:TPU:6 now
where the time goes in v6:
time: 109 us
  starting transfers between devices  50.9 us (47%)
  waiting for transfers between devices  33.6 us (31%)
  Pallas kernels  22.2 us (20%)
  between operations  1.26 us (1%)
    ppermute x36, starting transfers between devices, shift(): lax.ppermute(value, axis, [(i, (i + by) % size) for i in range(size)])  50.9 us
    ppermute x36, waiting for transfers between devices, shift(): lax.ppermute(value, axis, [(i, (i + by) % size) for i in range(size)])  33.6 us
    pallas_call x23, Pallas kernels, call(): pl.pallas_call(kernel, out_shape=out_shape, in_specs=[VMEM] * len(args),...  16.1 us
    pallas_call x1, Pallas kernels, prepare(): pl.pallas_call(prepare_kernel, out_shape=(pltpu.VMEM(grads.shape, grads.d...  3.61 us
    pallas_call x3, Pallas kernels, last(): pl.pallas_call(functools.partial(last_kernel, i, at, first), out_shape=ja...  2.44 us
  transfers between devices with their start and end apart: 36, of which 14 were waited for; matrix products, arithmetic and copies ran while one was open for 1% of the time, Pallas kernels for 16%

profile of v6, /device:TPU:6, one launch (start us, length us, event | category | flops | bytes accessed | tf_op | source)
XLA Modules:
  0.0 108.9 jit_solution(12364414503147295796)
XLA Ops:
  0.6 3.6 %shard_map.50 = (bf16[256,4096]{1,0:T(8,128)(2,1)S(1)}, bf16[272,128]{1,0:T(8,128)(2,1)S(1)}, bf16[272,128]{1,0:T(8,128)(2,1)S(1)}, bf16[272,128]{1,0:T(8,128)(2,1)S(1)}, bf16[16,128]{1,0:T(8,128)(2,1)S(1)}) custom-call(s32[2]{0:T(128)} %len_hbm.1, bf16[256,1792]{1,0:T(8,128)(2,1)} %hidden_hbm.1, bf16[256,4096]{1,0:T(8,128)(2,1)} %grads_hbm.1), custom_call_target="tpu_custom_call" | custom-call | flops 400000000 | bytes 5000000 | tf_op jit(solution)/shard_map/pallas_call | solution.py:107
  4.3 2.3 %collective-permute-start = (bf16[272,128]{1,0:T(8,128)(2,1)S(1)}, bf16[272,128]{1,0:T(8,128)(2,1)S(1)}, u32[]{:S(2)}, u32[]{:S(2)}) collective-permute-start(bf16[272,128]{1,0:T(8,128)(2,1)S(1)} %get-tuple-element.22), channel_id=1, source_target_pairs={{0,8},{8,16},{16,24},{24,0},{1,9},{9,17},{17,25},{25,1},{2,10},{10... | collective-permute-start | bytes 208904 | tf_op jit(solution)/shard_map/ppermute | solution.py:302
  9.1 3.2 %collective-permute-done.1 = bf16[272,128]{1,0:T(8,128)(2,1)S(1)} collective-permute-done((bf16[272,128]{1,0:T(8,128)(2,1)S(1)}, bf16[272,128]{1,0:T(8,128)(2,1)S(1)}, u32[]{:S(2)}, u32[]{:S(2)}) %collective-permute-start.1) | collective-permute-done | bytes 69664 | tf_op jit(solution)/shard_map/ppermute | solution.py:302
  14.5 2.9 %collective-permute-start.4 = (bf16[832,128]{1,0:T(8,128)(2,1)S(1)}, bf16[832,128]{1,0:T(8,128)(2,1)S(1)}, u32[]{:S(2)}, u32[]{:S(2)}) collective-permute-start(bf16[832,128]{1,0:T(8,128)(2,1)S(1)} %get-tuple-element.46), channel_id=1, source_target_pairs={{0,4},{2,6},{4,0},{6,2},{1,5},{3,7},{5,1},{7,3},{8,12},{10,14},{12... | collective-permute-start | bytes 638984 | tf_op jit(solution)/shard_map/ppermute | solution.py:302
  22.1 3.3 %collective-permute-done.4 = bf16[832,128]{1,0:T(8,128)(2,1)S(1)} collective-permute-done((bf16[832,128]{1,0:T(8,128)(2,1)S(1)}, bf16[832,128]{1,0:T(8,128)(2,1)S(1)}, u32[]{:S(2)}, u32[]{:S(2)}) %collective-permute-start.4) | collective-permute-done | bytes 213024 | tf_op jit(solution)/shard_map/ppermute | solution.py:302
  25.8 3.4 %collective-permute-done.7.refs_1_ = bf16[256,1024]{1,0:T(8,128)(2,1)S(1)} collective-permute-done((bf16[256,1024]{1,0:T(8,128)(2,1)S(1)}, bf16[256,1024]{1,0:T(8,128)(2,1)S(1)}, u32[]{:S(2)}, u32[]{:S(2)}) %collective-permute-start.7) | collective-permute-done | bytes 524320 | tf_op jit(solution)/shard_map/ppermute | solution.py:302
  31.0 3.2 %collective-permute-start.9 = (bf16[256,768]{1,0:T(8,128)(2,1)S(1)}, bf16[256,768]{1,0:T(8,128)(2,1)S(1)}, u32[]{:S(2)}, u32[]{:S(2)}) collective-permute-start(bf16[256,768]{1,0:T(8,128)(2,1)S(1)} %slice.21.refs_0_), channel_id=1, source_target_pairs={{0,8},{8,16},{16,24},{24,0},{1,9},{9,17},{17,25},{25,1},{2,10},{10... | collective-permute-start | bytes 1179656 | tf_op jit(solution)/shard_map/ppermute | solution.py:302
  34.2 6.0 %collective-permute-done.10.refs_4_ = bf16[256,768]{1,0:T(8,128)(2,1)S(1)} collective-permute-done((bf16[256,768]{1,0:T(8,128)(2,1)S(1)}, bf16[256,768]{1,0:T(8,128)(2,1)S(1)}, u32[]{:S(2)}, u32[]{:S(2)}) %collective-permute-start.10) | collective-permute-done | bytes 393248 | tf_op jit(solution)/shard_map/ppermute | solution.py:302
  40.3 3.6 %collective-permute-start.11 = (bf16[128,768]{1,0:T(8,128)(2,1)S(1)}, bf16[128,768]{1,0:T(8,128)(2,1)S(1)}, u32[]{:S(2)}, u32[]{:S(2)}) collective-permute-start(bf16[128,768]{1,0:T(8,128)(2,1)S(1)} %slice.23), channel_id=1, source_target_pairs={{0,8},{8,16},{16,24},{24,0},{1,9},{9,17},{17,25},{25,1},{2,10},{10... | collective-permute-start | bytes 589832 | tf_op jit(solution)/shard_map/ppermute | solution.py:302
  44.0 3.3 %collective-permute-start.20 = (bf16[128,1024]{1,0:T(8,128)(2,1)S(1)}, bf16[128,1024]{1,0:T(8,128)(2,1)S(1)}, u32[]{:S(2)}, u32[]{:S(2)}) collective-permute-start(bf16[128,1024]{1,0:T(8,128)(2,1)S(1)} %slice.25), channel_id=1, source_target_pairs={{0,8},{8,16},{16,24},{24,0},{1,9},{9,17},{17,25},{25,1},{2,10},{10... | collective-permute-start | bytes 786440 | tf_op jit(solution)/shard_map/ppermute | solution.py:302
  52.1 5.9 %collective-permute-start.16 = (s16[392,256]{1,0:T(8,128)(2,1)S(1)}, s16[392,256]{1,0:T(8,128)(2,1)S(1)}, u32[]{:S(2)}, u32[]{:S(2)}) collective-permute-start(s16[392,256]{1,0:T(8,128)(2,1)S(1)} %get-tuple-element.33), channel_id=1, source_target_pairs={{0,224},{32,0},{64,32},{96,64},{128,96},{160,128},{192,160},{224,1... | collective-permute-start | bytes 602120 | tf_op jit(solution)/shard_map/ppermute | solution.py:302
  58.1 1.9 %shard_map.61 = (s16[264,256]{1,0:T(8,128)(2,1)S(1)}, s16[264,256]{1,0:T(8,128)(2,1)S(1)}, s16[264,256]{1,0:T(8,128)(2,1)S(1)}, s16[264,256]{1,0:T(8,128)(2,1)S(1)}) custom-call(bf16[1024,256]{1,0:T(8,128)(2,1)S(1)} %shard_map.51.own, bf16[3328,128]{1,0:T(8,128)(2,1)S(1)} %constant_dynamic-update-slice_fusion.4.mine, ...), custom_call_target="tpu_custom_call" | custom-call | flops 1000000000 | bytes 1000000 | tf_op jit(solution)/shard_map/pallas_call | solution.py:290
  60.0 3.3 %collective-permute-start.33 = (s16[264,256]{1,0:T(8,128)(2,1)S(1)}, s16[264,256]{1,0:T(8,128)(2,1)S(1)}, u32[]{:S(2)}, u32[]{:S(2)}) collective-permute-start(s16[264,256]{1,0:T(8,128)(2,1)S(1)} %get-tuple-element.38), channel_id=1, source_target_pairs={{0,224},{32,0},{64,32},{96,64},{128,96},{160,128},{192,160},{224,1... | collective-permute-start | bytes 405512 | tf_op jit(solution)/shard_map/ppermute | solution.py:302
  63.3 2.5 %shard_map.54.parts_ref = f32[512,768]{1,0:T(8,128)S(1)} custom-call(bf16[1024,1024]{1,0:T(8,128)(2,1)S(1)} %get-tuple-element.26.hi_ref, bf16[1024,1024]{1,0:T(8,128)(2,1)S(1)} %get-tuple-element.27.lo_ref, bf16[256,768]{1,0:T(8,128)(2,1)S(1)} %slice.21.refs_0_, bf16[256,768]{1,0:T(8,128)(2,1)S(1)} %collective-permute-done.9.refs_1_, ...), custom_call_target="tpu_custom_call" | custom-call | flops 1000000000 | bytes 1000000 | tf_op jit(solution)/shard_map/pallas_call | solution.py:290
  68.1 3.2 %collective-permute-start.26 = (s16[264,256]{1,0:T(8,128)(2,1)S(1)}, s16[264,256]{1,0:T(8,128)(2,1)S(1)}, u32[]{:S(2)}, u32[]{:S(2)}) collective-permute-start(s16[264,256]{1,0:T(8,128)(2,1)S(1)} %get-tuple-element.36), channel_id=1, source_target_pairs={{0,224},{32,0},{64,32},{96,64},{128,96},{160,128},{192,160},{224,1... | collective-permute-start | bytes 405512 | tf_op jit(solution)/shard_map/ppermute | solution.py:302
  71.6 3.4 %shard_map.62.parts_ref = f32[512,1024]{1,0:T(8,128)S(1)} custom-call(bf16[1024,1024]{1,0:T(8,128)(2,1)S(1)} %get-tuple-element.26.hi_ref, bf16[1024,1024]{1,0:T(8,128)(2,1)S(1)} %get-tuple-element.27.lo_ref, bf16[256,1024]{1,0:T(8,128)(2,1)S(1)} %slice.22.refs_0_, bf16[256,1024]{1,0:T(8,128)(2,1)S(1)} %collective-permute-done.7.refs_1_, ...), custom_call_target="tpu_custom_call" | custom-call | flops 1000000000 | bytes 1000000 | tf_op jit(solution)/shard_map/pallas_call | solution.py:290
  75.1 3.3 %collective-permute-start.34 = (s16[264,256]{1,0:T(8,128)(2,1)S(1)}, s16[264,256]{1,0:T(8,128)(2,1)S(1)}, u32[]{:S(2)}, u32[]{:S(2)}) collective-permute-start(s16[264,256]{1,0:T(8,128)(2,1)S(1)} %shard_map.72), channel_id=1, source_target_pairs={{0,224},{32,0},{64,32},{96,64},{128,96},{160,128},{192,160},{224,1... | collective-permute-start | bytes 405512 | tf_op jit(solution)/shard_map/ppermute | solution.py:302
  79.3 3.3 %collective-permute-start.18 = (s16[392,256]{1,0:T(8,128)(2,1)S(1)}, s16[392,256]{1,0:T(8,128)(2,1)S(1)}, u32[]{:S(2)}, u32[]{:S(2)}) collective-permute-start(s16[392,256]{1,0:T(8,128)(2,1)S(1)} %shard_map.58), channel_id=1, source_target_pairs={{0,224},{32,0},{64,32},{96,64},{128,96},{160,128},{192,160},{224,1... | collective-permute-start | bytes 602120 | tf_op jit(solution)/shard_map/ppermute | solution.py:302
  82.7 2.1 %collective-permute-start.27 = (s16[264,256]{1,0:T(8,128)(2,1)S(1)}, s16[264,256]{1,0:T(8,128)(2,1)S(1)}, u32[]{:S(2)}, u32[]{:S(2)}) collective-permute-start(s16[264,256]{1,0:T(8,128)(2,1)S(1)} %shard_map.67), channel_id=1, source_target_pairs={{0,224},{32,0},{64,32},{96,64},{128,96},{160,128},{192,160},{224,1... | collective-permute-start | bytes 405512 | tf_op jit(solution)/shard_map/ppermute | solution.py:302
  86.6 2.8 %collective-permute-done.23.recv_ref = s16[264,256]{1,0:T(8,128)(2,1)S(1)} collective-permute-done((s16[264,256]{1,0:T(8,128)(2,1)S(1)}, s16[264,256]{1,0:T(8,128)(2,1)S(1)}, u32[]{:S(2)}, u32[]{:S(2)}) %collective-permute-start.23) | collective-permute-done | bytes 135200 | tf_op jit(solution)/shard_map/ppermute | solution.py:302
  91.6 3.3 %collective-permute-start.19 = (s16[392,256]{1,0:T(8,128)(2,1)S(1)}, s16[392,256]{1,0:T(8,128)(2,1)S(1)}, u32[]{:S(2)}, u32[]{:S(2)}) collective-permute-start(s16[392,256]{1,0:T(8,128)(2,1)S(1)} %shard_map.60), channel_id=1, source_target_pairs={{0,224},{32,0},{64,32},{96,64},{128,96},{160,128},{192,160},{224,1... | collective-permute-start | bytes 602120 | tf_op jit(solution)/shard_map/ppermute | solution.py:302
  94.9 2.0 %shard_map.65.parts_ref = f32[256,1024]{1,0:T(8,128)S(1)} custom-call(bf16[1024,1024]{1,0:T(8,128)(2,1)S(1)} %get-tuple-element.26.hi_ref, bf16[1024,1024]{1,0:T(8,128)(2,1)S(1)} %get-tuple-element.27.lo_ref, bf16[256,1024]{1,0:T(8,128)(2,1)S(1)} %slice.22.refs_0_, bf16[256,1024]{1,0:T(8,128)(2,1)S(1)} %collective-permute-done.7.refs_1_, ...), custom_call_target="tpu_custom_call" | custom-call | flops 1000000000 | bytes 1000000 | tf_op jit(solution)/shard_map/pallas_call | solution.py:290
  97.1 2.1 %collective-permute-start.28 = (s16[264,256]{1,0:T(8,128)(2,1)S(1)}, s16[264,256]{1,0:T(8,128)(2,1)S(1)}, u32[]{:S(2)}, u32[]{:S(2)}) collective-permute-start(s16[264,256]{1,0:T(8,128)(2,1)S(1)} %shard_map.68), channel_id=1, source_target_pairs={{0,224},{32,0},{64,32},{96,64},{128,96},{160,128},{192,160},{224,1... | collective-permute-start | bytes 405512 | tf_op jit(solution)/shard_map/ppermute | solution.py:302
  100.2 5.4 %collective-permute-done.32.up_ref = s16[264,256]{1,0:T(8,128)(2,1)S(1)} collective-permute-done((s16[264,256]{1,0:T(8,128)(2,1)S(1)}, s16[264,256]{1,0:T(8,128)(2,1)S(1)}, u32[]{:S(2)}, u32[]{:S(2)}) %collective-permute-start.32) | collective-permute-done | bytes 135200 | tf_op jit(solution)/shard_map/ppermute | solution.py:302
  (91 shorter events, 28.4 us)
Async XLA Ops:
  13.1 9.0 %collective-permute-start.3 = (bf16[832,128]{1,0:T(8,128)(2,1)S(1)}, bf16[832,128]{1,0:T(8,128)(2,1)S(1)}, u32[]{:S(2)}, u32[]{:S(2)}) collective-permute-start(bf16[832,128]{1,0:T(8,128)(2,1)S(1)} %get-tuple-element.46), channel_id=1, source_target_pairs={{0,2},{2,4},{4,6},{6,0},{1,3},{3,5},{5,7},{7,1},{8,10},{10,12},{12... | collective-permute-start | bytes 638984 | tf_op jit(solution)/shard_map/ppermute | solution.py:302
  14.5 11.0 %collective-permute-start.4 = (bf16[832,128]{1,0:T(8,128)(2,1)S(1)}, bf16[832,128]{1,0:T(8,128)(2,1)S(1)}, u32[]{:S(2)}, u32[]{:S(2)}) collective-permute-start(bf16[832,128]{1,0:T(8,128)(2,1)S(1)} %get-tuple-element.46), channel_id=1, source_target_pairs={{0,4},{2,6},{4,0},{6,2},{1,5},{3,7},{5,1},{7,3},{8,12},{10,14},{12... | collective-permute-start | bytes 638984 | tf_op jit(solution)/shard_map/ppermute | solution.py:302
  17.4 11.8 %collective-permute-start.7 = (bf16[256,1024]{1,0:T(8,128)(2,1)S(1)}, bf16[256,1024]{1,0:T(8,128)(2,1)S(1)}, u32[]{:S(2)}, u32[]{:S(2)}) collective-permute-start(bf16[256,1024]{1,0:T(8,128)(2,1)S(1)} %slice.22.refs_0_), channel_id=1, source_target_pairs={{0,8},{8,16},{16,24},{24,0},{1,9},{9,17},{17,25},{25,1},{2,10},{10... | collective-permute-start | bytes 1572872 | tf_op jit(solution)/shard_map/ppermute | solution.py:302
  18.1 12.9 %collective-permute-start.8 = (bf16[256,1024]{1,0:T(8,128)(2,1)S(1)}, bf16[256,1024]{1,0:T(8,128)(2,1)S(1)}, u32[]{:S(2)}, u32[]{:S(2)}) collective-permute-start(bf16[256,1024]{1,0:T(8,128)(2,1)S(1)} %slice.22.refs_0_), channel_id=1, source_target_pairs={{0,24},{8,0},{16,8},{24,16},{1,25},{9,1},{17,9},{25,17},{2,26},{10... | collective-permute-start | bytes 1572872 | tf_op jit(solution)/shard_map/ppermute | solution.py:302
  25.7 22.2 %collective-permute-start.6 = (bf16[3328,128]{1,0:T(8,128)(2,1)S(1)}, bf16[3328,128]{1,0:T(8,128)(2,1)S(1)}, u32[]{:S(2)}, u32[]{:S(2)}) collective-permute-start(bf16[3328,128]{1,0:T(8,128)(2,1)S(1)} %constant_dynamic-update-slice_fusion.4.mine), channel_id=1, source_target_pairs={{0,1},{1,0},{2,3},{3,2},{4,5},{5,4},{6,7},{7,6},{8,9},{9,8},{10,11... | collective-permute-start | bytes 2555912 | tf_op jit(solution)/shard_map/ppermute | solution.py:302
  31.0 9.2 %collective-permute-start.10 = (bf16[256,768]{1,0:T(8,128)(2,1)S(1)}, bf16[256,768]{1,0:T(8,128)(2,1)S(1)}, u32[]{:S(2)}, u32[]{:S(2)}) collective-permute-start(bf16[256,768]{1,0:T(8,128)(2,1)S(1)} %slice.21.refs_0_), channel_id=1, source_target_pairs={{0,24},{8,0},{16,8},{24,16},{1,25},{9,1},{17,9},{25,17},{2,26},{10... | collective-permute-start | bytes 1179656 | tf_op jit(solution)/shard_map/ppermute | solution.py:302
  31.0 9.2 %collective-permute-start.9 = (bf16[256,768]{1,0:T(8,128)(2,1)S(1)}, bf16[256,768]{1,0:T(8,128)(2,1)S(1)}, u32[]{:S(2)}, u32[]{:S(2)}) collective-permute-start(bf16[256,768]{1,0:T(8,128)(2,1)S(1)} %slice.21.refs_0_), channel_id=1, source_target_pairs={{0,8},{8,16},{16,24},{24,0},{1,9},{9,17},{17,25},{25,1},{2,10},{10... | collective-permute-start | bytes 1179656 | tf_op jit(solution)/shard_map/ppermute | solution.py:302
  44.0 14.1 %collective-permute-start.20 = (bf16[128,1024]{1,0:T(8,128)(2,1)S(1)}, bf16[128,1024]{1,0:T(8,128)(2,1)S(1)}, u32[]{:S(2)}, u32[]{:S(2)}) collective-permute-start(bf16[128,1024]{1,0:T(8,128)(2,1)S(1)} %slice.25), channel_id=1, source_target_pairs={{0,8},{8,16},{16,24},{24,0},{1,9},{9,17},{17,25},{25,1},{2,10},{10... | collective-permute-start | bytes 786440 | tf_op jit(solution)/shard_map/ppermute | solution.py:302
  47.3 10.8 %collective-permute-start.21 = (bf16[128,1024]{1,0:T(8,128)(2,1)S(1)}, bf16[128,1024]{1,0:T(8,128)(2,1)S(1)}, u32[]{:S(2)}, u32[]{:S(2)}) collective-permute-start(bf16[128,1024]{1,0:T(8,128)(2,1)S(1)} %slice.26), channel_id=1, source_target_pairs={{0,24},{8,0},{16,8},{24,16},{1,25},{9,1},{17,9},{25,17},{2,26},{10... | collective-permute-start | bytes 786440 | tf_op jit(solution)/shard_map/ppermute | solution.py:302
  52.1 13.7 %collective-permute-start.16 = (s16[392,256]{1,0:T(8,128)(2,1)S(1)}, s16[392,256]{1,0:T(8,128)(2,1)S(1)}, u32[]{:S(2)}, u32[]{:S(2)}) collective-permute-start(s16[392,256]{1,0:T(8,128)(2,1)S(1)} %get-tuple-element.33), channel_id=1, source_target_pairs={{0,224},{32,0},{64,32},{96,64},{128,96},{160,128},{192,160},{224,1... | collective-permute-start | bytes 602120 | tf_op jit(solution)/shard_map/ppermute | solution.py:302
  58.1 10.0 %collective-permute-start.13 = (s16[392,256]{1,0:T(8,128)(2,1)S(1)}, s16[392,256]{1,0:T(8,128)(2,1)S(1)}, u32[]{:S(2)}, u32[]{:S(2)}) collective-permute-start(s16[392,256]{1,0:T(8,128)(2,1)S(1)} %get-tuple-element.32), channel_id=1, source_target_pairs={{0,32},{32,64},{64,96},{96,128},{128,160},{160,192},{192,224},{224... | collective-permute-start | bytes 602120 | tf_op jit(solution)/shard_map/ppermute | solution.py:302
  60.0 11.5 %collective-permute-start.33 = (s16[264,256]{1,0:T(8,128)(2,1)S(1)}, s16[264,256]{1,0:T(8,128)(2,1)S(1)}, u32[]{:S(2)}, u32[]{:S(2)}) collective-permute-start(s16[264,256]{1,0:T(8,128)(2,1)S(1)} %get-tuple-element.38), channel_id=1, source_target_pairs={{0,224},{32,0},{64,32},{96,64},{128,96},{160,128},{192,160},{224,1... | collective-permute-start | bytes 405512 | tf_op jit(solution)/shard_map/ppermute | solution.py:302
  66.0 13.0 %collective-permute-start.17 = (s16[392,256]{1,0:T(8,128)(2,1)S(1)}, s16[392,256]{1,0:T(8,128)(2,1)S(1)}, u32[]{:S(2)}, u32[]{:S(2)}) collective-permute-start(s16[392,256]{1,0:T(8,128)(2,1)S(1)} %shard_map.57), channel_id=1, source_target_pairs={{0,224},{32,0},{64,32},{96,64},{128,96},{160,128},{192,160},{224,1... | collective-permute-start | bytes 602120 | tf_op jit(solution)/shard_map/ppermute | solution.py:302
  68.1 10.5 %collective-permute-start.22 = (s16[264,256]{1,0:T(8,128)(2,1)S(1)}, s16[264,256]{1,0:T(8,128)(2,1)S(1)}, u32[]{:S(2)}, u32[]{:S(2)}) collective-permute-start(s16[264,256]{1,0:T(8,128)(2,1)S(1)} %get-tuple-element.35), channel_id=1, source_target_pairs={{0,32},{32,64},{64,96},{96,128},{128,160},{160,192},{192,224},{224... | collective-permute-start | bytes 405512 | tf_op jit(solution)/shard_map/ppermute | solution.py:302
  68.1 11.1 %collective-permute-start.26 = (s16[264,256]{1,0:T(8,128)(2,1)S(1)}, s16[264,256]{1,0:T(8,128)(2,1)S(1)}, u32[]{:S(2)}, u32[]{:S(2)}) collective-permute-start(s16[264,256]{1,0:T(8,128)(2,1)S(1)} %get-tuple-element.36), channel_id=1, source_target_pairs={{0,224},{32,0},{64,32},{96,64},{128,96},{160,128},{192,160},{224,1... | collective-permute-start | bytes 405512 | tf_op jit(solution)/shard_map/ppermute | solution.py:302
  71.5 18.1 %collective-permute-start.14 = (s16[392,256]{1,0:T(8,128)(2,1)S(1)}, s16[392,256]{1,0:T(8,128)(2,1)S(1)}, u32[]{:S(2)}, u32[]{:S(2)}) collective-permute-start(s16[392,256]{1,0:T(8,128)(2,1)S(1)} %shard_map.55), channel_id=1, source_target_pairs={{0,32},{32,64},{64,96},{96,128},{128,160},{160,192},{192,224},{224... | collective-permute-start | bytes 602120 | tf_op jit(solution)/shard_map/ppermute | solution.py:302
  79.0 10.4 %collective-permute-start.23 = (s16[264,256]{1,0:T(8,128)(2,1)S(1)}, s16[264,256]{1,0:T(8,128)(2,1)S(1)}, u32[]{:S(2)}, u32[]{:S(2)}) collective-permute-start(s16[264,256]{1,0:T(8,128)(2,1)S(1)} %shard_map.63), channel_id=1, source_target_pairs={{0,32},{32,64},{64,96},{96,128},{128,160},{160,192},{192,224},{224... | collective-permute-start | bytes 405512 | tf_op jit(solution)/shard_map/ppermute | solution.py:302
  79.3 12.1 %collective-permute-start.18 = (s16[392,256]{1,0:T(8,128)(2,1)S(1)}, s16[392,256]{1,0:T(8,128)(2,1)S(1)}, u32[]{:S(2)}, u32[]{:S(2)}) collective-permute-start(s16[392,256]{1,0:T(8,128)(2,1)S(1)} %shard_map.58), channel_id=1, source_target_pairs={{0,224},{32,0},{64,32},{96,64},{128,96},{160,128},{192,160},{224,1... | collective-permute-start | bytes 602120 | tf_op jit(solution)/shard_map/ppermute | solution.py:302
  82.7 8.9 %collective-permute-start.27 = (s16[264,256]{1,0:T(8,128)(2,1)S(1)}, s16[264,256]{1,0:T(8,128)(2,1)S(1)}, u32[]{:S(2)}, u32[]{:S(2)}) collective-permute-start(s16[264,256]{1,0:T(8,128)(2,1)S(1)} %shard_map.67), channel_id=1, source_target_pairs={{0,224},{32,0},{64,32},{96,64},{128,96},{160,128},{192,160},{224,1... | collective-permute-start | bytes 405512 | tf_op jit(solution)/shard_map/ppermute | solution.py:302
  86.5 13.0 %collective-permute-start.35 = (s16[264,256]{1,0:T(8,128)(2,1)S(1)}, s16[264,256]{1,0:T(8,128)(2,1)S(1)}, u32[]{:S(2)}, u32[]{:S(2)}) collective-permute-start(s16[264,256]{1,0:T(8,128)(2,1)S(1)} %shard_map.73), channel_id=1, source_target_pairs={{0,224},{32,0},{64,32},{96,64},{128,96},{160,128},{192,160},{224,1... | collective-permute-start | bytes 405512 | tf_op jit(solution)/shard_map/ppermute | solution.py:302
  89.5 9.7 %collective-permute-start.24 = (s16[264,256]{1,0:T(8,128)(2,1)S(1)}, s16[264,256]{1,0:T(8,128)(2,1)S(1)}, u32[]{:S(2)}, u32[]{:S(2)}) collective-permute-start(s16[264,256]{1,0:T(8,128)(2,1)S(1)} %shard_map.64), channel_id=1, source_target_pairs={{0,32},{32,64},{64,96},{96,128},{128,160},{160,192},{192,224},{224... | collective-permute-start | bytes 405512 | tf_op jit(solution)/shard_map/ppermute | solution.py:302
  91.4 16.4 %collective-permute-start.15 = (s16[392,256]{1,0:T(8,128)(2,1)S(1)}, s16[392,256]{1,0:T(8,128)(2,1)S(1)}, u32[]{:S(2)}, u32[]{:S(2)}) collective-permute-start(s16[392,256]{1,0:T(8,128)(2,1)S(1)} %shard_map.56), channel_id=1, source_target_pairs={{0,32},{32,64},{64,96},{96,128},{128,160},{160,192},{192,224},{224... | collective-permute-start | bytes 602120 | tf_op jit(solution)/shard_map/ppermute | solution.py:302
  91.6 16.2 %collective-permute-start.19 = (s16[392,256]{1,0:T(8,128)(2,1)S(1)}, s16[392,256]{1,0:T(8,128)(2,1)S(1)}, u32[]{:S(2)}, u32[]{:S(2)}) collective-permute-start(s16[392,256]{1,0:T(8,128)(2,1)S(1)} %shard_map.60), channel_id=1, source_target_pairs={{0,224},{32,0},{64,32},{96,64},{128,96},{160,128},{192,160},{224,1... | collective-permute-start | bytes 602120 | tf_op jit(solution)/shard_map/ppermute | solution.py:302
  97.1 9.3 %collective-permute-start.28 = (s16[264,256]{1,0:T(8,128)(2,1)S(1)}, s16[264,256]{1,0:T(8,128)(2,1)S(1)}, u32[]{:S(2)}, u32[]{:S(2)}) collective-permute-start(s16[264,256]{1,0:T(8,128)(2,1)S(1)} %shard_map.68), channel_id=1, source_target_pairs={{0,224},{32,0},{64,32},{96,64},{128,96},{160,128},{192,160},{224,1... | collective-permute-start | bytes 405512 | tf_op jit(solution)/shard_map/ppermute | solution.py:302
  (13 other events, 100.4 us)

commit v7 on v5

--- a/solution.py
+++ b/solution.py
@@ -17,7 +17,7 @@
 NOTE = 16
 PIECE = QUARTER + NOTE
 BUNDLE = (NX - 1) * PIECE + NOTE
-HALVES = ((4, 3, 8), (3, 4, 6))
+HALVES = ((4, 3, 6), (3, 4, 8))
 LATER = ((((0, 2), (4, 6)), ((6, 8),)), (((1, 3), (5, 7)), ((0, 1), (7, 8))))
 LIMIT = 32767.0
 MANT = 8192.0
@@ -299,19 +299,19 @@
     doc_total = lengths.shape[0] * NX * NZ
     ff = hidden.shape[1] * NY * 2
     model_dim = grads.shape[1]
-    gathered, ready, at = [], None, 0
-    for _, _, units in HALVES:
+    gathered, at = [], 0
+    for n, (_, _, units) in enumerate(HALVES):
         own = lax.slice_in_dim(hidden, at, at + units * LANES, axis=1)
         at += units * LANES
-        if ready is not None:
-            own, ready = lax.optimization_barrier((own, ready))
         below = shift(own, "x", NX, 1)
         above = shift(own, "x", NX, -1)
-        below, above = lax.optimization_barrier((below, above))
-        ready = below
-        far0 = shift(below[: tokens // 2], "x", NX, 1)
-        far1 = shift(above[tokens // 2 :], "x", NX, -1)
-        gathered.append((own, below, far0, far1, above))
+        if n == 0:
+            far = (shift(own, "x", NX, 2),)
+        if n:
+            below, above = lax.optimization_barrier((below, above))
+            half = tokens // 2
+            far = (shift(below[:half], "x", NX, 1), shift(above[half:], "x", NX, -1))
+        gathered.append((own, below, *far, above))
 
     masked, *sends, note = prepare(lengths, hidden, grads)
     got = [shift(s, "x", NX, k) for k, s in enumerate(sends, 1)]

time: 110 us -> 116 us (1.055)
  the two profiles are of different devices: /device:TPU:8 before, /device:TPU:6 now
where the time goes in v7:
time: 116 us
  waiting for transfers between devices  53.7 us (46%)
  starting transfers between devices  40.9 us (35%)
  Pallas kernels  18.9 us (16%)
    ppermute x28, waiting for transfers between devices, shift(): lax.ppermute(value, axis, [(i, (i + by) % size) for i in range(size)])  53.7 us
    ppermute x28, starting transfers between devices, shift(): lax.ppermute(value, axis, [(i, (i + by) % size) for i in range(size)])  40.9 us
    pallas_call x18, Pallas kernels, call(): pl.pallas_call(kernel, out_shape=out_shape, in_specs=[VMEM] * len(args),...  13.5 us
    pallas_call x1, Pallas kernels, prepare(): pl.pallas_call(prepare_kernel, out_shape=(pltpu.VMEM(grads.shape, grads.d...  3.61 us
  transfers between devices with their start and end apart: 28, of which 14 were waited for; matrix products, arithmetic and copies ran while one was open for 1% of the time, Pallas kernels for 12%

profile of v7, /device:TPU:6, one launch (start us, length us, event | category | flops | bytes accessed | tf_op | source)
XLA Modules:
  0.0 115.6 jit_solution(164541166176740508)
XLA Ops:
  0.6 3.6 %shard_map.50 = (bf16[256,4096]{1,0:T(8,128)(2,1)S(1)}, bf16[272,128]{1,0:T(8,128)(2,1)S(1)}, bf16[272,128]{1,0:T(8,128)(2,1)S(1)}, bf16[272,128]{1,0:T(8,128)(2,1)S(1)}, bf16[16,128]{1,0:T(8,128)(2,1)S(1)}) custom-call(s32[2]{0:T(128)} %len_hbm.1, bf16[256,1792]{1,0:T(8,128)(2,1)} %hidden_hbm.1, bf16[256,4096]{1,0:T(8,128)(2,1)} %grads_hbm.1), custom_call_target="tpu_custom_call" | custom-call | flops 400000000 | bytes 5000000 | tf_op jit(solution)/shard_map/pallas_call | solution.py:107
  4.3 2.3 %collective-permute-start = (bf16[272,128]{1,0:T(8,128)(2,1)S(1)}, bf16[272,128]{1,0:T(8,128)(2,1)S(1)}, u32[]{:S(2)}, u32[]{:S(2)}) collective-permute-start(bf16[272,128]{1,0:T(8,128)(2,1)S(1)} %get-tuple-element.17), channel_id=1, source_target_pairs={{0,8},{8,16},{16,24},{24,0},{1,9},{9,17},{17,25},{25,1},{2,10},{10... | collective-permute-start | bytes 208904 | tf_op jit(solution)/shard_map/ppermute | solution.py:294
  9.1 3.2 %collective-permute-done.1 = bf16[272,128]{1,0:T(8,128)(2,1)S(1)} collective-permute-done((bf16[272,128]{1,0:T(8,128)(2,1)S(1)}, bf16[272,128]{1,0:T(8,128)(2,1)S(1)}, u32[]{:S(2)}, u32[]{:S(2)}) %collective-permute-start.1) | collective-permute-done | bytes 69664 | tf_op jit(solution)/shard_map/ppermute | solution.py:294
  14.5 2.9 %collective-permute-start.4 = (bf16[832,128]{1,0:T(8,128)(2,1)S(1)}, bf16[832,128]{1,0:T(8,128)(2,1)S(1)}, u32[]{:S(2)}, u32[]{:S(2)}) collective-permute-start(bf16[832,128]{1,0:T(8,128)(2,1)S(1)} %get-tuple-element.36), channel_id=1, source_target_pairs={{0,4},{2,6},{4,0},{6,2},{1,5},{3,7},{5,1},{7,3},{8,12},{10,14},{12... | collective-permute-start | bytes 638984 | tf_op jit(solution)/shard_map/ppermute | solution.py:294
  18.7 3.4 %collective-permute-done.3 = bf16[832,128]{1,0:T(8,128)(2,1)S(1)} collective-permute-done((bf16[832,128]{1,0:T(8,128)(2,1)S(1)}, bf16[832,128]{1,0:T(8,128)(2,1)S(1)}, u32[]{:S(2)}, u32[]{:S(2)}) %collective-permute-start.3) | collective-permute-done | bytes 213024 | tf_op jit(solution)/shard_map/ppermute | solution.py:294
  22.1 3.3 %collective-permute-done.4 = bf16[832,128]{1,0:T(8,128)(2,1)S(1)} collective-permute-done((bf16[832,128]{1,0:T(8,128)(2,1)S(1)}, bf16[832,128]{1,0:T(8,128)(2,1)S(1)}, u32[]{:S(2)}, u32[]{:S(2)}) %collective-permute-start.4) | collective-permute-done | bytes 213024 | tf_op jit(solution)/shard_map/ppermute | solution.py:294
  27.8 12.3 %collective-permute-done.7.refs_1_ = bf16[256,1024]{1,0:T(8,128)(2,1)S(1)} collective-permute-done((bf16[256,1024]{1,0:T(8,128)(2,1)S(1)}, bf16[256,1024]{1,0:T(8,128)(2,1)S(1)}, u32[]{:S(2)}, u32[]{:S(2)}) %collective-permute-start.7) | collective-permute-done | bytes 524320 | tf_op jit(solution)/shard_map/ppermute | solution.py:294
  40.1 1.8 %collective-permute-done.8.refs_4_ = bf16[256,1024]{1,0:T(8,128)(2,1)S(1)} collective-permute-done((bf16[256,1024]{1,0:T(8,128)(2,1)S(1)}, bf16[256,1024]{1,0:T(8,128)(2,1)S(1)}, u32[]{:S(2)}, u32[]{:S(2)}) %collective-permute-start.8) | collective-permute-done | bytes 524320 | tf_op jit(solution)/shard_map/ppermute | solution.py:294
  42.1 3.3 %collective-permute-start.9 = (bf16[128,1024]{1,0:T(8,128)(2,1)S(1)}, bf16[128,1024]{1,0:T(8,128)(2,1)S(1)}, u32[]{:S(2)}, u32[]{:S(2)}) collective-permute-start(bf16[128,1024]{1,0:T(8,128)(2,1)S(1)} %slice.16), channel_id=1, source_target_pairs={{0,8},{8,16},{16,24},{24,0},{1,9},{9,17},{17,25},{25,1},{2,10},{10... | collective-permute-start | bytes 786440 | tf_op jit(solution)/shard_map/ppermute | solution.py:294
  49.1 11.8 %collective-permute-done.10.refs_3_ = bf16[128,1024]{1,0:T(8,128)(2,1)S(1)} collective-permute-done((bf16[128,1024]{1,0:T(8,128)(2,1)S(1)}, bf16[128,1024]{1,0:T(8,128)(2,1)S(1)}, u32[]{:S(2)}, u32[]{:S(2)}) %collective-permute-start.10) | collective-permute-done | bytes 262176 | tf_op jit(solution)/shard_map/ppermute | solution.py:294
  60.8 1.7 %shard_map.53 = (s16[520,256]{1,0:T(8,128)(2,1)S(1)}, s16[520,256]{1,0:T(8,128)(2,1)S(1)}) custom-call(bf16[1024,1024]{1,0:T(8,128)(2,1)S(1)} %get-tuple-element.21.hi_ref, bf16[1024,1024]{1,0:T(8,128)(2,1)S(1)} %get-tuple-element.22.lo_ref, bf16[256,1024]{1,0:T(8,128)(2,1)S(1)} %slice.15.refs_0_, bf16[256,1024]{1,0:T(8,128)(2,1)S(1)} %collective-permute-done.7.refs_1_, ...), custom_call_target="tpu_custom_call" | custom-call | flops 1000000000 | bytes 1000000 | tf_op jit(solution)/shard_map/pallas_call | solution.py:282
  62.5 5.9 %collective-permute-start.14 = (s16[520,256]{1,0:T(8,128)(2,1)S(1)}, s16[520,256]{1,0:T(8,128)(2,1)S(1)}, u32[]{:S(2)}, u32[]{:S(2)}) collective-permute-start(s16[520,256]{1,0:T(8,128)(2,1)S(1)} %get-tuple-element.26), channel_id=1, source_target_pairs={{0,224},{32,0},{64,32},{96,64},{128,96},{160,128},{192,160},{224,1... | collective-permute-start | bytes 798728 | tf_op jit(solution)/shard_map/ppermute | solution.py:294
  68.5 2.9 %shard_map.54.parts_ref = f32[512,1024]{1,0:T(8,128)S(1)} custom-call(bf16[1024,1024]{1,0:T(8,128)(2,1)S(1)} %get-tuple-element.21.hi_ref, bf16[1024,1024]{1,0:T(8,128)(2,1)S(1)} %get-tuple-element.22.lo_ref, bf16[256,1024]{1,0:T(8,128)(2,1)S(1)} %slice.15.refs_0_, bf16[256,1024]{1,0:T(8,128)(2,1)S(1)} %collective-permute-done.7.refs_1_, ...), custom_call_target="tpu_custom_call" | custom-call | flops 1000000000 | bytes 1000000 | tf_op jit(solution)/shard_map/pallas_call | solution.py:282
  72.6 3.8 %collective-permute-start.15 = (s16[520,256]{1,0:T(8,128)(2,1)S(1)}, s16[520,256]{1,0:T(8,128)(2,1)S(1)}, u32[]{:S(2)}, u32[]{:S(2)}) collective-permute-start(s16[520,256]{1,0:T(8,128)(2,1)S(1)} %shard_map.57), channel_id=1, source_target_pairs={{0,224},{32,0},{64,32},{96,64},{128,96},{160,128},{192,160},{224,1... | collective-permute-start | bytes 798728 | tf_op jit(solution)/shard_map/ppermute | solution.py:294
  77.8 3.2 %collective-permute-start.25 = (s16[392,256]{1,0:T(8,128)(2,1)S(1)}, s16[392,256]{1,0:T(8,128)(2,1)S(1)}, u32[]{:S(2)}, u32[]{:S(2)}) collective-permute-start(s16[392,256]{1,0:T(8,128)(2,1)S(1)} %get-tuple-element.28), channel_id=1, source_target_pairs={{0,224},{32,0},{64,32},{96,64},{128,96},{160,128},{192,160},{224,1... | collective-permute-start | bytes 602120 | tf_op jit(solution)/shard_map/ppermute | solution.py:294
  81.0 1.8 %shard_map.62.parts_ref = f32[512,768]{1,0:T(8,128)S(1)} custom-call(bf16[1024,1024]{1,0:T(8,128)(2,1)S(1)} %get-tuple-element.21.hi_ref, bf16[1024,1024]{1,0:T(8,128)(2,1)S(1)} %get-tuple-element.22.lo_ref, bf16[256,768]{1,0:T(8,128)(2,1)S(1)} %slice.18.refs_0_, bf16[256,768]{1,0:T(8,128)(2,1)S(1)} %collective-permute-done.18.refs_1_, ...), custom_call_target="tpu_custom_call" | custom-call | flops 1000000000 | bytes 1000000 | tf_op jit(solution)/shard_map/pallas_call | solution.py:282
  82.8 4.0 %collective-permute-done.21.recv_ref = s16[392,256]{1,0:T(8,128)(2,1)S(1)} collective-permute-done((s16[392,256]{1,0:T(8,128)(2,1)S(1)}, s16[392,256]{1,0:T(8,128)(2,1)S(1)}, u32[]{:S(2)}, u32[]{:S(2)}) %collective-permute-start.21) | collective-permute-done | bytes 200736 | tf_op jit(solution)/shard_map/ppermute | solution.py:294
  87.8 3.3 %collective-permute-start.16 = (s16[520,256]{1,0:T(8,128)(2,1)S(1)}, s16[520,256]{1,0:T(8,128)(2,1)S(1)}, u32[]{:S(2)}, u32[]{:S(2)}) collective-permute-start(s16[520,256]{1,0:T(8,128)(2,1)S(1)} %shard_map.58), channel_id=1, source_target_pairs={{0,224},{32,0},{64,32},{96,64},{128,96},{160,128},{192,160},{224,1... | collective-permute-start | bytes 798728 | tf_op jit(solution)/shard_map/ppermute | solution.py:294
  91.3 2.1 %collective-permute-start.26 = (s16[392,256]{1,0:T(8,128)(2,1)S(1)}, s16[392,256]{1,0:T(8,128)(2,1)S(1)}, u32[]{:S(2)}, u32[]{:S(2)}) collective-permute-start(s16[392,256]{1,0:T(8,128)(2,1)S(1)} %shard_map.67), channel_id=1, source_target_pairs={{0,224},{32,0},{64,32},{96,64},{128,96},{160,128},{192,160},{224,1... | collective-permute-start | bytes 602120 | tf_op jit(solution)/shard_map/ppermute | solution.py:294
  93.4 2.2 %collective-permute-done.22.recv_ref = s16[392,256]{1,0:T(8,128)(2,1)S(1)} collective-permute-done((s16[392,256]{1,0:T(8,128)(2,1)S(1)}, s16[392,256]{1,0:T(8,128)(2,1)S(1)}, u32[]{:S(2)}, u32[]{:S(2)}) %collective-permute-start.22) | collective-permute-done | bytes 200736 | tf_op jit(solution)/shard_map/ppermute | solution.py:294
  97.4 3.9 %collective-permute-done.12.recv_ref = s16[520,256]{1,0:T(8,128)(2,1)S(1)} collective-permute-done((s16[520,256]{1,0:T(8,128)(2,1)S(1)}, s16[520,256]{1,0:T(8,128)(2,1)S(1)}, u32[]{:S(2)}, u32[]{:S(2)}) %collective-permute-start.12) | collective-permute-done | bytes 266272 | tf_op jit(solution)/shard_map/ppermute | solution.py:294
  101.8 3.3 %collective-permute-start.17 = (s16[520,256]{1,0:T(8,128)(2,1)S(1)}, s16[520,256]{1,0:T(8,128)(2,1)S(1)}, u32[]{:S(2)}, u32[]{:S(2)}) collective-permute-start(s16[520,256]{1,0:T(8,128)(2,1)S(1)} %shard_map.60), channel_id=1, source_target_pairs={{0,224},{32,0},{64,32},{96,64},{128,96},{160,128},{192,160},{224,1... | collective-permute-start | bytes 798728 | tf_op jit(solution)/shard_map/ppermute | solution.py:294
  106.6 2.1 %collective-permute-start.24 = (s16[392,256]{1,0:T(8,128)(2,1)S(1)}, s16[392,256]{1,0:T(8,128)(2,1)S(1)}, u32[]{:S(2)}, u32[]{:S(2)}) collective-permute-start(s16[392,256]{1,0:T(8,128)(2,1)S(1)} %shard_map.66), channel_id=1, source_target_pairs={{0,32},{32,64},{64,96},{96,128},{128,160},{160,192},{192,224},{224... | collective-permute-start | bytes 602120 | tf_op jit(solution)/shard_map/ppermute | solution.py:294
  109.3 2.8 %collective-permute-done.27.down_ref = s16[392,256]{1,0:T(8,128)(2,1)S(1)} collective-permute-done((s16[392,256]{1,0:T(8,128)(2,1)S(1)}, s16[392,256]{1,0:T(8,128)(2,1)S(1)}, u32[]{:S(2)}, u32[]{:S(2)}) %collective-permute-start.27) | collective-permute-done | bytes 200736 | tf_op jit(solution)/shard_map/ppermute | solution.py:294
  (67 shorter events, 23.5 us)
Async XLA Ops:
  13.1 9.0 %collective-permute-start.3 = (bf16[832,128]{1,0:T(8,128)(2,1)S(1)}, bf16[832,128]{1,0:T(8,128)(2,1)S(1)}, u32[]{:S(2)}, u32[]{:S(2)}) collective-permute-start(bf16[832,128]{1,0:T(8,128)(2,1)S(1)} %get-tuple-element.36), channel_id=1, source_target_pairs={{0,2},{2,4},{4,6},{6,0},{1,3},{3,5},{5,7},{7,1},{8,10},{10,12},{12... | collective-permute-start | bytes 638984 | tf_op jit(solution)/shard_map/ppermute | solution.py:294
  14.5 11.0 %collective-permute-start.4 = (bf16[832,128]{1,0:T(8,128)(2,1)S(1)}, bf16[832,128]{1,0:T(8,128)(2,1)S(1)}, u32[]{:S(2)}, u32[]{:S(2)}) collective-permute-start(bf16[832,128]{1,0:T(8,128)(2,1)S(1)} %get-tuple-element.36), channel_id=1, source_target_pairs={{0,4},{2,6},{4,0},{6,2},{1,5},{3,7},{5,1},{7,3},{8,12},{10,14},{12... | collective-permute-start | bytes 638984 | tf_op jit(solution)/shard_map/ppermute | solution.py:294
  17.4 8.2 %collective-permute-start.5 = (bf16[832,128]{1,0:T(8,128)(2,1)S(1)}, bf16[832,128]{1,0:T(8,128)(2,1)S(1)}, u32[]{:S(2)}, u32[]{:S(2)}) collective-permute-start(bf16[832,128]{1,0:T(8,128)(2,1)S(1)} %get-tuple-element.36), channel_id=1, source_target_pairs={{0,6},{2,0},{4,2},{6,4},{1,7},{3,1},{5,3},{7,5},{8,14},{10,8},{12,... | collective-permute-start | bytes 638984 | tf_op jit(solution)/shard_map/ppermute | solution.py:294
  25.6 20.8 %collective-permute-start.6 = (bf16[3328,128]{1,0:T(8,128)(2,1)S(1)}, bf16[3328,128]{1,0:T(8,128)(2,1)S(1)}, u32[]{:S(2)}, u32[]{:S(2)}) collective-permute-start(bf16[3328,128]{1,0:T(8,128)(2,1)S(1)} %constant_dynamic-update-slice_fusion.4.mine), channel_id=1, source_target_pairs={{0,1},{1,0},{2,3},{3,2},{4,5},{5,4},{6,7},{7,6},{8,9},{9,8},{10,11... | collective-permute-start | bytes 2555912 | tf_op jit(solution)/shard_map/ppermute | solution.py:294
  25.7 14.4 %collective-permute-start.7 = (bf16[256,1024]{1,0:T(8,128)(2,1)S(1)}, bf16[256,1024]{1,0:T(8,128)(2,1)S(1)}, u32[]{:S(2)}, u32[]{:S(2)}) collective-permute-start(bf16[256,1024]{1,0:T(8,128)(2,1)S(1)} %slice.15.refs_0_), channel_id=1, source_target_pairs={{0,8},{8,16},{16,24},{24,0},{1,9},{9,17},{17,25},{25,1},{2,10},{10... | collective-permute-start | bytes 1572872 | tf_op jit(solution)/shard_map/ppermute | solution.py:294
  26.7 15.2 %collective-permute-start.8 = (bf16[256,1024]{1,0:T(8,128)(2,1)S(1)}, bf16[256,1024]{1,0:T(8,128)(2,1)S(1)}, u32[]{:S(2)}, u32[]{:S(2)}) collective-permute-start(bf16[256,1024]{1,0:T(8,128)(2,1)S(1)} %slice.15.refs_0_), channel_id=1, source_target_pairs={{0,24},{8,0},{16,8},{24,16},{1,25},{9,1},{17,9},{25,17},{2,26},{10... | collective-permute-start | bytes 1572872 | tf_op jit(solution)/shard_map/ppermute | solution.py:294
  41.9 18.9 %collective-permute-start.10 = (bf16[128,1024]{1,0:T(8,128)(2,1)S(1)}, bf16[128,1024]{1,0:T(8,128)(2,1)S(1)}, u32[]{:S(2)}, u32[]{:S(2)}) collective-permute-start(bf16[128,1024]{1,0:T(8,128)(2,1)S(1)} %slice.17), channel_id=1, source_target_pairs={{0,24},{8,0},{16,8},{24,16},{1,25},{9,1},{17,9},{25,17},{2,26},{10... | collective-permute-start | bytes 786440 | tf_op jit(solution)/shard_map/ppermute | solution.py:294
  42.1 18.8 %collective-permute-start.9 = (bf16[128,1024]{1,0:T(8,128)(2,1)S(1)}, bf16[128,1024]{1,0:T(8,128)(2,1)S(1)}, u32[]{:S(2)}, u32[]{:S(2)}) collective-permute-start(bf16[128,1024]{1,0:T(8,128)(2,1)S(1)} %slice.16), channel_id=1, source_target_pairs={{0,8},{8,16},{16,24},{24,0},{1,9},{9,17},{17,25},{25,1},{2,10},{10... | collective-permute-start | bytes 786440 | tf_op jit(solution)/shard_map/ppermute | solution.py:294
  45.4 31.0 %collective-permute-start.18 = (bf16[256,768]{1,0:T(8,128)(2,1)S(1)}, bf16[256,768]{1,0:T(8,128)(2,1)S(1)}, u32[]{:S(2)}, u32[]{:S(2)}) collective-permute-start(bf16[256,768]{1,0:T(8,128)(2,1)S(1)} %slice.18.refs_0_), channel_id=1, source_target_pairs={{0,8},{8,16},{16,24},{24,0},{1,9},{9,17},{17,25},{25,1},{2,10},{10... | collective-permute-start | bytes 1179656 | tf_op jit(solution)/shard_map/ppermute | solution.py:294
  45.5 30.9 %collective-permute-start.19 = (bf16[256,768]{1,0:T(8,128)(2,1)S(1)}, bf16[256,768]{1,0:T(8,128)(2,1)S(1)}, u32[]{:S(2)}, u32[]{:S(2)}) collective-permute-start(bf16[256,768]{1,0:T(8,128)(2,1)S(1)} %slice.18.refs_0_), channel_id=1, source_target_pairs={{0,16},{8,24},{16,0},{24,8},{1,17},{9,25},{17,1},{25,9},{2,18},{10... | collective-permute-start | bytes 1179656 | tf_op jit(solution)/shard_map/ppermute | solution.py:294
  46.3 30.0 %collective-permute-start.20 = (bf16[256,768]{1,0:T(8,128)(2,1)S(1)}, bf16[256,768]{1,0:T(8,128)(2,1)S(1)}, u32[]{:S(2)}, u32[]{:S(2)}) collective-permute-start(bf16[256,768]{1,0:T(8,128)(2,1)S(1)} %slice.18.refs_0_), channel_id=1, source_target_pairs={{0,24},{8,0},{16,8},{24,16},{1,25},{9,1},{17,9},{25,17},{2,26},{10... | collective-permute-start | bytes 1179656 | tf_op jit(solution)/shard_map/ppermute | solution.py:294
  62.5 9.9 %collective-permute-start.14 = (s16[520,256]{1,0:T(8,128)(2,1)S(1)}, s16[520,256]{1,0:T(8,128)(2,1)S(1)}, u32[]{:S(2)}, u32[]{:S(2)}) collective-permute-start(s16[520,256]{1,0:T(8,128)(2,1)S(1)} %get-tuple-element.26), channel_id=1, source_target_pairs={{0,224},{32,0},{64,32},{96,64},{128,96},{160,128},{192,160},{224,1... | collective-permute-start | bytes 798728 | tf_op jit(solution)/shard_map/ppermute | solution.py:294
  68.5 18.6 %collective-permute-start.11 = (s16[520,256]{1,0:T(8,128)(2,1)S(1)}, s16[520,256]{1,0:T(8,128)(2,1)S(1)}, u32[]{:S(2)}, u32[]{:S(2)}) collective-permute-start(s16[520,256]{1,0:T(8,128)(2,1)S(1)} %get-tuple-element.25), channel_id=1, source_target_pairs={{0,32},{32,64},{64,96},{96,128},{128,160},{160,192},{192,224},{224... | collective-permute-start | bytes 798728 | tf_op jit(solution)/shard_map/ppermute | solution.py:294
  72.6 15.0 %collective-permute-start.15 = (s16[520,256]{1,0:T(8,128)(2,1)S(1)}, s16[520,256]{1,0:T(8,128)(2,1)S(1)}, u32[]{:S(2)}, u32[]{:S(2)}) collective-permute-start(s16[520,256]{1,0:T(8,128)(2,1)S(1)} %shard_map.57), channel_id=1, source_target_pairs={{0,224},{32,0},{64,32},{96,64},{128,96},{160,128},{192,160},{224,1... | collective-permute-start | bytes 798728 | tf_op jit(solution)/shard_map/ppermute | solution.py:294
  77.7 9.2 %collective-permute-start.21 = (s16[392,256]{1,0:T(8,128)(2,1)S(1)}, s16[392,256]{1,0:T(8,128)(2,1)S(1)}, u32[]{:S(2)}, u32[]{:S(2)}) collective-permute-start(s16[392,256]{1,0:T(8,128)(2,1)S(1)} %get-tuple-element.27), channel_id=1, source_target_pairs={{0,32},{32,64},{64,96},{96,128},{128,160},{160,192},{192,224},{224... | collective-permute-start | bytes 602120 | tf_op jit(solution)/shard_map/ppermute | solution.py:294
  77.8 13.3 %collective-permute-start.25 = (s16[392,256]{1,0:T(8,128)(2,1)S(1)}, s16[392,256]{1,0:T(8,128)(2,1)S(1)}, u32[]{:S(2)}, u32[]{:S(2)}) collective-permute-start(s16[392,256]{1,0:T(8,128)(2,1)S(1)} %get-tuple-element.28), channel_id=1, source_target_pairs={{0,224},{32,0},{64,32},{96,64},{128,96},{160,128},{192,160},{224,1... | collective-permute-start | bytes 602120 | tf_op jit(solution)/shard_map/ppermute | solution.py:294
  87.0 8.6 %collective-permute-start.22 = (s16[392,256]{1,0:T(8,128)(2,1)S(1)}, s16[392,256]{1,0:T(8,128)(2,1)S(1)}, u32[]{:S(2)}, u32[]{:S(2)}) collective-permute-start(s16[392,256]{1,0:T(8,128)(2,1)S(1)} %shard_map.63), channel_id=1, source_target_pairs={{0,32},{32,64},{64,96},{96,128},{128,160},{160,192},{192,224},{224... | collective-permute-start | bytes 602120 | tf_op jit(solution)/shard_map/ppermute | solution.py:294
  87.3 14.0 %collective-permute-start.12 = (s16[520,256]{1,0:T(8,128)(2,1)S(1)}, s16[520,256]{1,0:T(8,128)(2,1)S(1)}, u32[]{:S(2)}, u32[]{:S(2)}) collective-permute-start(s16[520,256]{1,0:T(8,128)(2,1)S(1)} %shard_map.55), channel_id=1, source_target_pairs={{0,32},{32,64},{64,96},{96,128},{128,160},{160,192},{192,224},{224... | collective-permute-start | bytes 798728 | tf_op jit(solution)/shard_map/ppermute | solution.py:294
  87.8 13.8 %collective-permute-start.16 = (s16[520,256]{1,0:T(8,128)(2,1)S(1)}, s16[520,256]{1,0:T(8,128)(2,1)S(1)}, u32[]{:S(2)}, u32[]{:S(2)}) collective-permute-start(s16[520,256]{1,0:T(8,128)(2,1)S(1)} %shard_map.58), channel_id=1, source_target_pairs={{0,224},{32,0},{64,32},{96,64},{128,96},{160,128},{192,160},{224,1... | collective-permute-start | bytes 798728 | tf_op jit(solution)/shard_map/ppermute | solution.py:294
  91.3 14.8 %collective-permute-start.26 = (s16[392,256]{1,0:T(8,128)(2,1)S(1)}, s16[392,256]{1,0:T(8,128)(2,1)S(1)}, u32[]{:S(2)}, u32[]{:S(2)}) collective-permute-start(s16[392,256]{1,0:T(8,128)(2,1)S(1)} %shard_map.67), channel_id=1, source_target_pairs={{0,224},{32,0},{64,32},{96,64},{128,96},{160,128},{192,160},{224,1... | collective-permute-start | bytes 602120 | tf_op jit(solution)/shard_map/ppermute | solution.py:294
  95.8 10.6 %collective-permute-start.23 = (s16[392,256]{1,0:T(8,128)(2,1)S(1)}, s16[392,256]{1,0:T(8,128)(2,1)S(1)}, u32[]{:S(2)}, u32[]{:S(2)}) collective-permute-start(s16[392,256]{1,0:T(8,128)(2,1)S(1)} %shard_map.64), channel_id=1, source_target_pairs={{0,32},{32,64},{64,96},{96,128},{128,160},{160,192},{192,224},{224... | collective-permute-start | bytes 602120 | tf_op jit(solution)/shard_map/ppermute | solution.py:294
  101.5 12.9 %collective-permute-start.13 = (s16[520,256]{1,0:T(8,128)(2,1)S(1)}, s16[520,256]{1,0:T(8,128)(2,1)S(1)}, u32[]{:S(2)}, u32[]{:S(2)}) collective-permute-start(s16[520,256]{1,0:T(8,128)(2,1)S(1)} %shard_map.56), channel_id=1, source_target_pairs={{0,32},{32,64},{64,96},{96,128},{128,160},{160,192},{192,224},{224... | collective-permute-start | bytes 798728 | tf_op jit(solution)/shard_map/ppermute | solution.py:294
  101.8 12.6 %collective-permute-start.17 = (s16[520,256]{1,0:T(8,128)(2,1)S(1)}, s16[520,256]{1,0:T(8,128)(2,1)S(1)}, u32[]{:S(2)}, u32[]{:S(2)}) collective-permute-start(s16[520,256]{1,0:T(8,128)(2,1)S(1)} %shard_map.60), channel_id=1, source_target_pairs={{0,224},{32,0},{64,32},{96,64},{128,96},{160,128},{192,160},{224,1... | collective-permute-start | bytes 798728 | tf_op jit(solution)/shard_map/ppermute | solution.py:294
  106.6 7.0 %collective-permute-start.24 = (s16[392,256]{1,0:T(8,128)(2,1)S(1)}, s16[392,256]{1,0:T(8,128)(2,1)S(1)}, u32[]{:S(2)}, u32[]{:S(2)}) collective-permute-start(s16[392,256]{1,0:T(8,128)(2,1)S(1)} %shard_map.66), channel_id=1, source_target_pairs={{0,32},{32,64},{64,96},{96,128},{128,160},{160,192},{192,224},{224... | collective-permute-start | bytes 602120 | tf_op jit(solution)/shard_map/ppermute | solution.py:294
  (5 other events, 47.4 us)

commit v8 on v5

--- a/solution.py
+++ b/solution.py
@@ -17,7 +17,7 @@
 NOTE = 16
 PIECE = QUARTER + NOTE
 BUNDLE = (NX - 1) * PIECE + NOTE
-HALVES = ((4, 3, 8), (3, 4, 6))
+HALVES = ((4, 3, 6), (3, 4, 8))
 LATER = ((((0, 2), (4, 6)), ((6, 8),)), (((1, 3), (5, 7)), ((0, 1), (7, 8))))
 LIMIT = 32767.0
 MANT = 8192.0
@@ -64,11 +64,15 @@
 def prepare_kernel(len_hbm, hidden_hbm, grads_hbm, masked_ref, s1, s2, s3, note_ref, grads_ref, hidden_ref, len_ref, sem, len_sem):
     lengths = pltpu.make_async_copy(len_hbm, len_ref, len_sem)
     lengths.start()
-    loads = [
-        pltpu.make_async_copy(src.at[pl.ds(d * SLOT, SLOT), :], dst.at[pl.ds(d * SLOT, SLOT), :], sem.at[i, d])
-        for d in range(2)
-        for i, (src, dst) in enumerate(((grads_hbm, grads_ref), (hidden_hbm, hidden_ref)))
-    ]
+    piece = SLOT // 4
+
+    def copies(i, d):
+        src, dst = ((grads_hbm, grads_ref), (hidden_hbm, hidden_ref))[i]
+        rows = [pl.ds(d * SLOT + n * piece, piece) for n in range(4)]
+        return [pltpu.make_async_copy(src.at[r, :], dst.at[r, :], sem.at[i, d, n]) for n, r in enumerate(rows)]
+
+    groups = [copies(i, d) for d in range(2) for i in range(2)]
+    loads = [c for g in groups for c in g]
     for load in loads:
         load.start()
     x, y, core = (lax.axis_index(a) for a in ("x", "y", "core"))
@@ -78,12 +82,14 @@
         rows = pl.ds(d * SLOT, SLOT)
         if d == 0:
             lengths.wait()
-        loads[2 * d].wait()
+        for load in groups[2 * d]:
+            load.wait()
         g = grads_ref[rows, :]
         token = lax.broadcasted_iota(jnp.int32, g.shape, 0)
         m = jnp.where(token < len_ref[d], g.astype(jnp.float32), 0.0).astype(g.dtype)
         masked_ref[rows, :] = m
-        loads[2 * d + 1].wait()
+        for load in groups[2 * d + 1]:
+            load.wait()
         h = hidden_ref[rows, :]
         gram_g = lax.dot_general(m, m, NT, preferred_element_type=jnp.float32)
         gram_h = lax.dot_general(h, h, NT, preferred_element_type=jnp.float32)
@@ -119,7 +125,7 @@
             pltpu.VMEM(grads.shape, grads.dtype),
             pltpu.VMEM(hidden.shape, hidden.dtype),
             pltpu.SMEM(lengths.shape, lengths.dtype),
-            pltpu.SemaphoreType.DMA((2, 2)),
+            pltpu.SemaphoreType.DMA((2, 2, 4)),
             pltpu.SemaphoreType.DMA(()),
         ],
         compiler_params=pltpu.CompilerParams(vmem_limit_bytes=GRANT),

time: 110 us -> 108 us (0.982)
  the two profiles are of different devices: /device:TPU:8 before, /device:TPU:24 now
where the time goes in v8:
time: 108 us
  starting transfers between devices  45.1 us (42%)
  waiting for transfers between devices  41.1 us (38%)
  Pallas kernels  19.8 us (18%)
  between operations  1.17 us (1%)
    ppermute x29, starting transfers between devices, shift(): lax.ppermute(value, axis, [(i, (i + by) % size) for i in range(size)])  45.1 us
    ppermute x29, waiting for transfers between devices, shift(): lax.ppermute(value, axis, [(i, (i + by) % size) for i in range(size)])  41.1 us
    pallas_call x18, Pallas kernels, call(): pl.pallas_call(kernel, out_shape=out_shape, in_specs=[VMEM] * len(args),...  14.3 us
    pallas_call x1, Pallas kernels, prepare(): pl.pallas_call(prepare_kernel, out_shape=(pltpu.VMEM(grads.shape, grads.d...  3.62 us
  transfers between devices with their start and end apart: 29, of which 14 were waited for; matrix products, arithmetic and copies ran while one was open for 1% of the time, Pallas kernels for 12%

profile of v8, /device:TPU:24, one launch (start us, length us, event | category | flops | bytes accessed | tf_op | source)
XLA Modules:
  0.0 108.1 jit_solution(576204760508140166)
XLA Ops:
  0.6 3.6 %shard_map.50 = (bf16[256,4096]{1,0:T(8,128)(2,1)S(1)}, bf16[272,128]{1,0:T(8,128)(2,1)S(1)}, bf16[272,128]{1,0:T(8,128)(2,1)S(1)}, bf16[272,128]{1,0:T(8,128)(2,1)S(1)}, bf16[16,128]{1,0:T(8,128)(2,1)S(1)}) custom-call(s32[2]{0:T(128)} %len_hbm.1, bf16[256,1792]{1,0:T(8,128)(2,1)} %hidden_hbm.1, bf16[256,4096]{1,0:T(8,128)(2,1)} %grads_hbm.1), custom_call_target="tpu_custom_call" | custom-call | flops 400000000 | bytes 5000000 | tf_op jit(solution)/shard_map/pallas_call | solution.py:113
  5.8 2.7 %collective-permute-start.1 = (bf16[272,128]{1,0:T(8,128)(2,1)S(1)}, bf16[272,128]{1,0:T(8,128)(2,1)S(1)}, u32[]{:S(2)}, u32[]{:S(2)}) collective-permute-start(bf16[272,128]{1,0:T(8,128)(2,1)S(1)} %get-tuple-element.21), channel_id=1, source_target_pairs={{0,16},{8,24},{16,0},{24,8},{1,17},{9,25},{17,1},{25,9},{2,18},{10... | collective-permute-start | bytes 208904 | tf_op jit(solution)/shard_map/ppermute | solution.py:300
  13.5 2.3 %collective-permute-start.4 = (bf16[832,128]{1,0:T(8,128)(2,1)S(1)}, bf16[832,128]{1,0:T(8,128)(2,1)S(1)}, u32[]{:S(2)}, u32[]{:S(2)}) collective-permute-start(bf16[832,128]{1,0:T(8,128)(2,1)S(1)} %get-tuple-element.42), channel_id=1, source_target_pairs={{0,4},{2,6},{4,0},{6,2},{1,5},{3,7},{5,1},{7,3},{8,12},{10,14},{12... | collective-permute-start | bytes 638984 | tf_op jit(solution)/shard_map/ppermute | solution.py:300
  16.5 2.6 %collective-permute-start.8 = (bf16[256,768]{1,0:T(8,128)(2,1)S(1)}, bf16[256,768]{1,0:T(8,128)(2,1)S(1)}, u32[]{:S(2)}, u32[]{:S(2)}) collective-permute-start(bf16[256,768]{1,0:T(8,128)(2,1)S(1)} %slice.22.refs_0_), channel_id=1, source_target_pairs={{0,24},{8,0},{16,8},{24,16},{1,25},{9,1},{17,9},{25,17},{2,26},{10... | collective-permute-start | bytes 1179656 | tf_op jit(solution)/shard_map/ppermute | solution.py:300
  21.2 5.0 %collective-permute-done.5 = bf16[832,128]{1,0:T(8,128)(2,1)S(1)} collective-permute-done((bf16[832,128]{1,0:T(8,128)(2,1)S(1)}, bf16[832,128]{1,0:T(8,128)(2,1)S(1)}, u32[]{:S(2)}, u32[]{:S(2)}) %collective-permute-start.5) | collective-permute-done | bytes 213024 | tf_op jit(solution)/shard_map/ppermute | solution.py:300
  26.4 2.8 %collective-permute-start.10 = (bf16[256,1024]{1,0:T(8,128)(2,1)S(1)}, bf16[256,1024]{1,0:T(8,128)(2,1)S(1)}, u32[]{:S(2)}, u32[]{:S(2)}) collective-permute-start(bf16[256,1024]{1,0:T(8,128)(2,1)S(1)} %slice.21.refs_0_), channel_id=1, source_target_pairs={{0,24},{8,0},{16,8},{24,16},{1,25},{9,1},{17,9},{25,17},{2,26},{10... | collective-permute-start | bytes 1572872 | tf_op jit(solution)/shard_map/ppermute | solution.py:300
  29.3 11.6 %collective-permute-done.10.refs_4_ = bf16[256,1024]{1,0:T(8,128)(2,1)S(1)} collective-permute-done((bf16[256,1024]{1,0:T(8,128)(2,1)S(1)}, bf16[256,1024]{1,0:T(8,128)(2,1)S(1)}, u32[]{:S(2)}, u32[]{:S(2)}) %collective-permute-start.10) | collective-permute-done | bytes 524320 | tf_op jit(solution)/shard_map/ppermute | solution.py:300
  40.8 2.8 %collective-permute-done.9.refs_1_ = bf16[256,1024]{1,0:T(8,128)(2,1)S(1)} collective-permute-done((bf16[256,1024]{1,0:T(8,128)(2,1)S(1)}, bf16[256,1024]{1,0:T(8,128)(2,1)S(1)}, u32[]{:S(2)}, u32[]{:S(2)}) %collective-permute-start.9) | collective-permute-done | bytes 524320 | tf_op jit(solution)/shard_map/ppermute | solution.py:300
  43.8 3.5 %collective-permute-start.12 = (bf16[128,1024]{1,0:T(8,128)(2,1)S(1)}, bf16[128,1024]{1,0:T(8,128)(2,1)S(1)}, u32[]{:S(2)}, u32[]{:S(2)}) collective-permute-start(bf16[128,1024]{1,0:T(8,128)(2,1)S(1)} %slice.24), channel_id=1, source_target_pairs={{0,24},{8,0},{16,8},{24,16},{1,25},{9,1},{17,9},{25,17},{2,26},{10... | collective-permute-start | bytes 786440 | tf_op jit(solution)/shard_map/ppermute | solution.py:300
  48.9 2.8 %collective-permute-done.11.refs_2_ = bf16[128,1024]{1,0:T(8,128)(2,1)S(1)} collective-permute-done((bf16[128,1024]{1,0:T(8,128)(2,1)S(1)}, bf16[128,1024]{1,0:T(8,128)(2,1)S(1)}, u32[]{:S(2)}, u32[]{:S(2)}) %collective-permute-start.11) | collective-permute-done | bytes 262176 | tf_op jit(solution)/shard_map/ppermute | solution.py:300
  53.4 5.3 %collective-permute-start.16 = (s16[520,256]{1,0:T(8,128)(2,1)S(1)}, s16[520,256]{1,0:T(8,128)(2,1)S(1)}, u32[]{:S(2)}, u32[]{:S(2)}) collective-permute-start(s16[520,256]{1,0:T(8,128)(2,1)S(1)} %get-tuple-element.31), channel_id=1, source_target_pairs={{0,224},{32,0},{64,32},{96,64},{128,96},{160,128},{192,160},{224,1... | collective-permute-start | bytes 798728 | tf_op jit(solution)/shard_map/ppermute | solution.py:300
  58.8 3.6 %collective-permute-start.21 = (bf16[128,768]{1,0:T(8,128)(2,1)S(1)}, bf16[128,768]{1,0:T(8,128)(2,1)S(1)}, u32[]{:S(2)}, u32[]{:S(2)}) collective-permute-start(bf16[128,768]{1,0:T(8,128)(2,1)S(1)} %slice.26), channel_id=1, source_target_pairs={{0,24},{8,0},{16,8},{24,16},{1,25},{9,1},{17,9},{25,17},{2,26},{10... | collective-permute-start | bytes 589832 | tf_op jit(solution)/shard_map/ppermute | solution.py:300
  62.4 2.9 %shard_map.54.parts_ref = f32[512,1024]{1,0:T(8,128)S(1)} custom-call(bf16[1024,1024]{1,0:T(8,128)(2,1)S(1)} %get-tuple-element.24.hi_ref, bf16[1024,1024]{1,0:T(8,128)(2,1)S(1)} %get-tuple-element.25.lo_ref, bf16[256,1024]{1,0:T(8,128)(2,1)S(1)} %slice.21.refs_0_, bf16[256,1024]{1,0:T(8,128)(2,1)S(1)} %collective-permute-done.9.refs_1_, ...), custom_call_target="tpu_custom_call" | custom-call | flops 1000000000 | bytes 1000000 | tf_op jit(solution)/shard_map/pallas_call | solution.py:288
  65.4 3.3 %collective-permute-start.17 = (s16[520,256]{1,0:T(8,128)(2,1)S(1)}, s16[520,256]{1,0:T(8,128)(2,1)S(1)}, u32[]{:S(2)}, u32[]{:S(2)}) collective-permute-start(s16[520,256]{1,0:T(8,128)(2,1)S(1)} %shard_map.57), channel_id=1, source_target_pairs={{0,224},{32,0},{64,32},{96,64},{128,96},{160,128},{192,160},{224,1... | collective-permute-start | bytes 798728 | tf_op jit(solution)/shard_map/ppermute | solution.py:300
  70.4 3.2 %collective-permute-start.26 = (s16[392,256]{1,0:T(8,128)(2,1)S(1)}, s16[392,256]{1,0:T(8,128)(2,1)S(1)}, u32[]{:S(2)}, u32[]{:S(2)}) collective-permute-start(s16[392,256]{1,0:T(8,128)(2,1)S(1)} %get-tuple-element.34), channel_id=1, source_target_pairs={{0,224},{32,0},{64,32},{96,64},{128,96},{160,128},{192,160},{224,1... | collective-permute-start | bytes 602120 | tf_op jit(solution)/shard_map/ppermute | solution.py:300
  73.6 2.2 %shard_map.62.parts_ref = f32[512,768]{1,0:T(8,128)S(1)} custom-call(bf16[1024,1024]{1,0:T(8,128)(2,1)S(1)} %get-tuple-element.24.hi_ref, bf16[1024,1024]{1,0:T(8,128)(2,1)S(1)} %get-tuple-element.25.lo_ref, bf16[256,768]{1,0:T(8,128)(2,1)S(1)} %slice.22.refs_0_, bf16[256,768]{1,0:T(8,128)(2,1)S(1)} %collective-permute-done.7.refs_1_, ...), custom_call_target="tpu_custom_call" | custom-call | flops 1000000000 | bytes 1000000 | tf_op jit(solution)/shard_map/pallas_call | solution.py:288
  75.8 2.8 %collective-permute-done.22.recv_ref = s16[392,256]{1,0:T(8,128)(2,1)S(1)} collective-permute-done((s16[392,256]{1,0:T(8,128)(2,1)S(1)}, s16[392,256]{1,0:T(8,128)(2,1)S(1)}, u32[]{:S(2)}, u32[]{:S(2)}) %collective-permute-start.22) | collective-permute-done | bytes 200736 | tf_op jit(solution)/shard_map/ppermute | solution.py:300
  79.4 3.3 %collective-permute-start.18 = (s16[520,256]{1,0:T(8,128)(2,1)S(1)}, s16[520,256]{1,0:T(8,128)(2,1)S(1)}, u32[]{:S(2)}, u32[]{:S(2)}) collective-permute-start(s16[520,256]{1,0:T(8,128)(2,1)S(1)} %shard_map.58), channel_id=1, source_target_pairs={{0,224},{32,0},{64,32},{96,64},{128,96},{160,128},{192,160},{224,1... | collective-permute-start | bytes 798728 | tf_op jit(solution)/shard_map/ppermute | solution.py:300
  82.8 2.1 %collective-permute-start.27 = (s16[392,256]{1,0:T(8,128)(2,1)S(1)}, s16[392,256]{1,0:T(8,128)(2,1)S(1)}, u32[]{:S(2)}, u32[]{:S(2)}) collective-permute-start(s16[392,256]{1,0:T(8,128)(2,1)S(1)} %shard_map.67), channel_id=1, source_target_pairs={{0,224},{32,0},{64,32},{96,64},{128,96},{160,128},{192,160},{224,1... | collective-permute-start | bytes 602120 | tf_op jit(solution)/shard_map/ppermute | solution.py:300
  84.9 3.0 %collective-permute-done.23.recv_ref = s16[392,256]{1,0:T(8,128)(2,1)S(1)} collective-permute-done((s16[392,256]{1,0:T(8,128)(2,1)S(1)}, s16[392,256]{1,0:T(8,128)(2,1)S(1)}, u32[]{:S(2)}, u32[]{:S(2)}) %collective-permute-start.23) | collective-permute-done | bytes 200736 | tf_op jit(solution)/shard_map/ppermute | solution.py:300
  89.7 3.9 %collective-permute-done.14.recv_ref = s16[520,256]{1,0:T(8,128)(2,1)S(1)} collective-permute-done((s16[520,256]{1,0:T(8,128)(2,1)S(1)}, s16[520,256]{1,0:T(8,128)(2,1)S(1)}, u32[]{:S(2)}, u32[]{:S(2)}) %collective-permute-start.14) | collective-permute-done | bytes 266272 | tf_op jit(solution)/shard_map/ppermute | solution.py:300
  94.1 3.3 %collective-permute-start.19 = (s16[520,256]{1,0:T(8,128)(2,1)S(1)}, s16[520,256]{1,0:T(8,128)(2,1)S(1)}, u32[]{:S(2)}, u32[]{:S(2)}) collective-permute-start(s16[520,256]{1,0:T(8,128)(2,1)S(1)} %shard_map.60), channel_id=1, source_target_pairs={{0,224},{32,0},{64,32},{96,64},{128,96},{160,128},{192,160},{224,1... | collective-permute-start | bytes 798728 | tf_op jit(solution)/shard_map/ppermute | solution.py:300
  99.1 2.1 %collective-permute-start.25 = (s16[392,256]{1,0:T(8,128)(2,1)S(1)}, s16[392,256]{1,0:T(8,128)(2,1)S(1)}, u32[]{:S(2)}, u32[]{:S(2)}) collective-permute-start(s16[392,256]{1,0:T(8,128)(2,1)S(1)} %shard_map.66), channel_id=1, source_target_pairs={{0,32},{32,64},{64,96},{96,128},{128,160},{160,192},{192,224},{224... | collective-permute-start | bytes 602120 | tf_op jit(solution)/shard_map/ppermute | solution.py:300
  101.8 2.8 %collective-permute-done.28.down_ref = s16[392,256]{1,0:T(8,128)(2,1)S(1)} collective-permute-done((s16[392,256]{1,0:T(8,128)(2,1)S(1)}, s16[392,256]{1,0:T(8,128)(2,1)S(1)}, u32[]{:S(2)}, u32[]{:S(2)}) %collective-permute-start.28) | collective-permute-done | bytes 200736 | tf_op jit(solution)/shard_map/ppermute | solution.py:300
  (71 shorter events, 23.4 us)
Async XLA Ops:
  12.9 8.2 %collective-permute-start.3 = (bf16[832,128]{1,0:T(8,128)(2,1)S(1)}, bf16[832,128]{1,0:T(8,128)(2,1)S(1)}, u32[]{:S(2)}, u32[]{:S(2)}) collective-permute-start(bf16[832,128]{1,0:T(8,128)(2,1)S(1)} %get-tuple-element.42), channel_id=1, source_target_pairs={{0,2},{2,4},{4,6},{6,0},{1,3},{3,5},{5,7},{7,1},{8,10},{10,12},{12... | collective-permute-start | bytes 638984 | tf_op jit(solution)/shard_map/ppermute | solution.py:300
  13.5 7.7 %collective-permute-start.4 = (bf16[832,128]{1,0:T(8,128)(2,1)S(1)}, bf16[832,128]{1,0:T(8,128)(2,1)S(1)}, u32[]{:S(2)}, u32[]{:S(2)}) collective-permute-start(bf16[832,128]{1,0:T(8,128)(2,1)S(1)} %get-tuple-element.42), channel_id=1, source_target_pairs={{0,4},{2,6},{4,0},{6,2},{1,5},{3,7},{5,1},{7,3},{8,12},{10,14},{12... | collective-permute-start | bytes 638984 | tf_op jit(solution)/shard_map/ppermute | solution.py:300
  15.8 10.6 %collective-permute-start.7 = (bf16[256,768]{1,0:T(8,128)(2,1)S(1)}, bf16[256,768]{1,0:T(8,128)(2,1)S(1)}, u32[]{:S(2)}, u32[]{:S(2)}) collective-permute-start(bf16[256,768]{1,0:T(8,128)(2,1)S(1)} %slice.22.refs_0_), channel_id=1, source_target_pairs={{0,8},{8,16},{16,24},{24,0},{1,9},{9,17},{17,25},{25,1},{2,10},{10... | collective-permute-start | bytes 1179656 | tf_op jit(solution)/shard_map/ppermute | solution.py:300
  16.5 9.9 %collective-permute-start.8 = (bf16[256,768]{1,0:T(8,128)(2,1)S(1)}, bf16[256,768]{1,0:T(8,128)(2,1)S(1)}, u32[]{:S(2)}, u32[]{:S(2)}) collective-permute-start(bf16[256,768]{1,0:T(8,128)(2,1)S(1)} %slice.22.refs_0_), channel_id=1, source_target_pairs={{0,24},{8,0},{16,8},{24,16},{1,25},{9,1},{17,9},{25,17},{2,26},{10... | collective-permute-start | bytes 1179656 | tf_op jit(solution)/shard_map/ppermute | solution.py:300
  19.2 7.1 %collective-permute-start.5 = (bf16[832,128]{1,0:T(8,128)(2,1)S(1)}, bf16[832,128]{1,0:T(8,128)(2,1)S(1)}, u32[]{:S(2)}, u32[]{:S(2)}) collective-permute-start(bf16[832,128]{1,0:T(8,128)(2,1)S(1)} %get-tuple-element.42), channel_id=1, source_target_pairs={{0,6},{2,0},{4,2},{6,4},{1,7},{3,1},{5,3},{7,5},{8,14},{10,8},{12,... | collective-permute-start | bytes 638984 | tf_op jit(solution)/shard_map/ppermute | solution.py:300
  26.2 21.3 %collective-permute-start.6 = (bf16[3328,128]{1,0:T(8,128)(2,1)S(1)}, bf16[3328,128]{1,0:T(8,128)(2,1)S(1)}, u32[]{:S(2)}, u32[]{:S(2)}) collective-permute-start(bf16[3328,128]{1,0:T(8,128)(2,1)S(1)} %constant_dynamic-update-slice_fusion.4.mine), channel_id=1, source_target_pairs={{0,1},{1,0},{2,3},{3,2},{4,5},{5,4},{6,7},{7,6},{8,9},{9,8},{10,11... | collective-permute-start | bytes 2555912 | tf_op jit(solution)/shard_map/ppermute | solution.py:300
  26.4 14.4 %collective-permute-start.10 = (bf16[256,1024]{1,0:T(8,128)(2,1)S(1)}, bf16[256,1024]{1,0:T(8,128)(2,1)S(1)}, u32[]{:S(2)}, u32[]{:S(2)}) collective-permute-start(bf16[256,1024]{1,0:T(8,128)(2,1)S(1)} %slice.21.refs_0_), channel_id=1, source_target_pairs={{0,24},{8,0},{16,8},{24,16},{1,25},{9,1},{17,9},{25,17},{2,26},{10... | collective-permute-start | bytes 1572872 | tf_op jit(solution)/shard_map/ppermute | solution.py:300
  29.3 14.4 %collective-permute-start.9 = (bf16[256,1024]{1,0:T(8,128)(2,1)S(1)}, bf16[256,1024]{1,0:T(8,128)(2,1)S(1)}, u32[]{:S(2)}, u32[]{:S(2)}) collective-permute-start(bf16[256,1024]{1,0:T(8,128)(2,1)S(1)} %slice.21.refs_0_), channel_id=1, source_target_pairs={{0,8},{8,16},{16,24},{24,0},{1,9},{9,17},{17,25},{25,1},{2,10},{10... | collective-permute-start | bytes 1572872 | tf_op jit(solution)/shard_map/ppermute | solution.py:300
  43.7 8.0 %collective-permute-start.11 = (bf16[128,1024]{1,0:T(8,128)(2,1)S(1)}, bf16[128,1024]{1,0:T(8,128)(2,1)S(1)}, u32[]{:S(2)}, u32[]{:S(2)}) collective-permute-start(bf16[128,1024]{1,0:T(8,128)(2,1)S(1)} %slice.23), channel_id=1, source_target_pairs={{0,8},{8,16},{16,24},{24,0},{1,9},{9,17},{17,25},{25,1},{2,10},{10... | collective-permute-start | bytes 786440 | tf_op jit(solution)/shard_map/ppermute | solution.py:300
  43.8 7.9 %collective-permute-start.12 = (bf16[128,1024]{1,0:T(8,128)(2,1)S(1)}, bf16[128,1024]{1,0:T(8,128)(2,1)S(1)}, u32[]{:S(2)}, u32[]{:S(2)}) collective-permute-start(bf16[128,1024]{1,0:T(8,128)(2,1)S(1)} %slice.24), channel_id=1, source_target_pairs={{0,24},{8,0},{16,8},{24,16},{1,25},{9,1},{17,9},{25,17},{2,26},{10... | collective-permute-start | bytes 786440 | tf_op jit(solution)/shard_map/ppermute | solution.py:300
  53.4 11.9 %collective-permute-start.16 = (s16[520,256]{1,0:T(8,128)(2,1)S(1)}, s16[520,256]{1,0:T(8,128)(2,1)S(1)}, u32[]{:S(2)}, u32[]{:S(2)}) collective-permute-start(s16[520,256]{1,0:T(8,128)(2,1)S(1)} %get-tuple-element.31), channel_id=1, source_target_pairs={{0,224},{32,0},{64,32},{96,64},{128,96},{160,128},{192,160},{224,1... | collective-permute-start | bytes 798728 | tf_op jit(solution)/shard_map/ppermute | solution.py:300
  58.7 10.1 %collective-permute-start.20 = (bf16[128,768]{1,0:T(8,128)(2,1)S(1)}, bf16[128,768]{1,0:T(8,128)(2,1)S(1)}, u32[]{:S(2)}, u32[]{:S(2)}) collective-permute-start(bf16[128,768]{1,0:T(8,128)(2,1)S(1)} %slice.25), channel_id=1, source_target_pairs={{0,8},{8,16},{16,24},{24,0},{1,9},{9,17},{17,25},{25,1},{2,10},{10... | collective-permute-start | bytes 589832 | tf_op jit(solution)/shard_map/ppermute | solution.py:300
  58.8 10.0 %collective-permute-start.21 = (bf16[128,768]{1,0:T(8,128)(2,1)S(1)}, bf16[128,768]{1,0:T(8,128)(2,1)S(1)}, u32[]{:S(2)}, u32[]{:S(2)}) collective-permute-start(bf16[128,768]{1,0:T(8,128)(2,1)S(1)} %slice.26), channel_id=1, source_target_pairs={{0,24},{8,0},{16,8},{24,16},{1,25},{9,1},{17,9},{25,17},{2,26},{10... | collective-permute-start | bytes 589832 | tf_op jit(solution)/shard_map/ppermute | solution.py:300
  62.3 16.5 %collective-permute-start.13 = (s16[520,256]{1,0:T(8,128)(2,1)S(1)}, s16[520,256]{1,0:T(8,128)(2,1)S(1)}, u32[]{:S(2)}, u32[]{:S(2)}) collective-permute-start(s16[520,256]{1,0:T(8,128)(2,1)S(1)} %get-tuple-element.30), channel_id=1, source_target_pairs={{0,32},{32,64},{64,96},{96,128},{128,160},{160,192},{192,224},{224... | collective-permute-start | bytes 798728 | tf_op jit(solution)/shard_map/ppermute | solution.py:300
  65.4 13.7 %collective-permute-start.17 = (s16[520,256]{1,0:T(8,128)(2,1)S(1)}, s16[520,256]{1,0:T(8,128)(2,1)S(1)}, u32[]{:S(2)}, u32[]{:S(2)}) collective-permute-start(s16[520,256]{1,0:T(8,128)(2,1)S(1)} %shard_map.57), channel_id=1, source_target_pairs={{0,224},{32,0},{64,32},{96,64},{128,96},{160,128},{192,160},{224,1... | collective-permute-start | bytes 798728 | tf_op jit(solution)/shard_map/ppermute | solution.py:300
  70.3 8.3 %collective-permute-start.22 = (s16[392,256]{1,0:T(8,128)(2,1)S(1)}, s16[392,256]{1,0:T(8,128)(2,1)S(1)}, u32[]{:S(2)}, u32[]{:S(2)}) collective-permute-start(s16[392,256]{1,0:T(8,128)(2,1)S(1)} %get-tuple-element.33), channel_id=1, source_target_pairs={{0,32},{32,64},{64,96},{96,128},{128,160},{160,192},{192,224},{224... | collective-permute-start | bytes 602120 | tf_op jit(solution)/shard_map/ppermute | solution.py:300
  70.4 12.3 %collective-permute-start.26 = (s16[392,256]{1,0:T(8,128)(2,1)S(1)}, s16[392,256]{1,0:T(8,128)(2,1)S(1)}, u32[]{:S(2)}, u32[]{:S(2)}) collective-permute-start(s16[392,256]{1,0:T(8,128)(2,1)S(1)} %get-tuple-element.34), channel_id=1, source_target_pairs={{0,224},{32,0},{64,32},{96,64},{128,96},{160,128},{192,160},{224,1... | collective-permute-start | bytes 602120 | tf_op jit(solution)/shard_map/ppermute | solution.py:300
  78.8 9.1 %collective-permute-start.23 = (s16[392,256]{1,0:T(8,128)(2,1)S(1)}, s16[392,256]{1,0:T(8,128)(2,1)S(1)}, u32[]{:S(2)}, u32[]{:S(2)}) collective-permute-start(s16[392,256]{1,0:T(8,128)(2,1)S(1)} %shard_map.63), channel_id=1, source_target_pairs={{0,32},{32,64},{64,96},{96,128},{128,160},{160,192},{192,224},{224... | collective-permute-start | bytes 602120 | tf_op jit(solution)/shard_map/ppermute | solution.py:300
  79.1 14.6 %collective-permute-start.14 = (s16[520,256]{1,0:T(8,128)(2,1)S(1)}, s16[520,256]{1,0:T(8,128)(2,1)S(1)}, u32[]{:S(2)}, u32[]{:S(2)}) collective-permute-start(s16[520,256]{1,0:T(8,128)(2,1)S(1)} %shard_map.55), channel_id=1, source_target_pairs={{0,32},{32,64},{64,96},{96,128},{128,160},{160,192},{192,224},{224... | collective-permute-start | bytes 798728 | tf_op jit(solution)/shard_map/ppermute | solution.py:300
  79.4 14.5 %collective-permute-start.18 = (s16[520,256]{1,0:T(8,128)(2,1)S(1)}, s16[520,256]{1,0:T(8,128)(2,1)S(1)}, u32[]{:S(2)}, u32[]{:S(2)}) collective-permute-start(s16[520,256]{1,0:T(8,128)(2,1)S(1)} %shard_map.58), channel_id=1, source_target_pairs={{0,224},{32,0},{64,32},{96,64},{128,96},{160,128},{192,160},{224,1... | collective-permute-start | bytes 798728 | tf_op jit(solution)/shard_map/ppermute | solution.py:300
  82.8 15.8 %collective-permute-start.27 = (s16[392,256]{1,0:T(8,128)(2,1)S(1)}, s16[392,256]{1,0:T(8,128)(2,1)S(1)}, u32[]{:S(2)}, u32[]{:S(2)}) collective-permute-start(s16[392,256]{1,0:T(8,128)(2,1)S(1)} %shard_map.67), channel_id=1, source_target_pairs={{0,224},{32,0},{64,32},{96,64},{128,96},{160,128},{192,160},{224,1... | collective-permute-start | bytes 602120 | tf_op jit(solution)/shard_map/ppermute | solution.py:300
  88.1 10.8 %collective-permute-start.24 = (s16[392,256]{1,0:T(8,128)(2,1)S(1)}, s16[392,256]{1,0:T(8,128)(2,1)S(1)}, u32[]{:S(2)}, u32[]{:S(2)}) collective-permute-start(s16[392,256]{1,0:T(8,128)(2,1)S(1)} %shard_map.64), channel_id=1, source_target_pairs={{0,32},{32,64},{64,96},{96,128},{128,160},{160,192},{192,224},{224... | collective-permute-start | bytes 602120 | tf_op jit(solution)/shard_map/ppermute | solution.py:300
  93.8 13.1 %collective-permute-start.15 = (s16[520,256]{1,0:T(8,128)(2,1)S(1)}, s16[520,256]{1,0:T(8,128)(2,1)S(1)}, u32[]{:S(2)}, u32[]{:S(2)}) collective-permute-start(s16[520,256]{1,0:T(8,128)(2,1)S(1)} %shard_map.56), channel_id=1, source_target_pairs={{0,32},{32,64},{64,96},{96,128},{128,160},{160,192},{192,224},{224... | collective-permute-start | bytes 798728 | tf_op jit(solution)/shard_map/ppermute | solution.py:300
  94.1 12.8 %collective-permute-start.19 = (s16[520,256]{1,0:T(8,128)(2,1)S(1)}, s16[520,256]{1,0:T(8,128)(2,1)S(1)}, u32[]{:S(2)}, u32[]{:S(2)}) collective-permute-start(s16[520,256]{1,0:T(8,128)(2,1)S(1)} %shard_map.60), channel_id=1, source_target_pairs={{0,224},{32,0},{64,32},{96,64},{128,96},{160,128},{192,160},{224,1... | collective-permute-start | bytes 798728 | tf_op jit(solution)/shard_map/ppermute | solution.py:300
  (6 other events, 44.5 us)
